TPU v7x, 32 devices: a whole 2x2x4 slice. The times are simulated.
32 devices in a mesh: ctx: 8 (over z, x), fsdp: 4 (over y, core).
Axes of the slice: x: 2, y: 2, z: 4, core: 2. Of those that a mesh axis runs over, the one named last changes fastest.
Arguments:
- tokens: bfloat16 [4, 2048, 768], P('fsdp', 'ctx'), may hold values from -6 to 6
- seq_lengths: int32 [4, 2], P('fsdp'), may hold values from 1024 to 1024, as said below
- deal: int32 [4, 16], P('fsdp'), may hold values from 0 to 15, each once within a row
- w_query: float32 [768, 768], P('fsdp'), may hold values from -0.375 to 0.375
- w_key: float32 [768, 768], P('fsdp'), may hold values from -0.21875 to 0.21875
- w_value: float32 [768, 768], P('fsdp'), may hold values from -0.21875 to 0.21875
- w_attn_out: float32 [768, 768], P('fsdp'), may hold values from -1.75 to 1.75
- b_query: float32 [768], P('fsdp'), may hold values from -1.8 to 1.8
- b_value: float32 [768], P('fsdp'), may hold values from -1.8 to 1.8
- b_attn_out: float32 [768], P('fsdp'), may hold values from -1.8 to 1.8
- norm1_gain: float32 [768], P('fsdp'), may hold values from 0.5 to 1.5
- norm1_bias: float32 [768], P('fsdp'), may hold values from -1.8 to 1.8
- w_in: float32 [768, 3072], P('fsdp'), may hold values from -0.21875 to 0.21875
- b_in: float32 [3072], P('fsdp'), may hold values from -1.8 to 1.8
- w_out: float32 [3072, 768], P('fsdp'), may hold values from -0.109375 to 0.109375
- b_out: float32 [768], P('fsdp'), may hold values from -1.8 to 1.8
- norm2_gain: float32 [768], P('fsdp'), may hold values from 0.5 to 1.5
- norm2_bias: float32 [768], P('fsdp'), may hold values from -1.8 to 1.8
- cotangent: bfloat16 [4, 2048, 768], P('fsdp', 'ctx'), may hold values from -6 to 6
Outputs:
- layer_out: bfloat16 [4, 2048, 768], P('fsdp', 'ctx')
- grad_tokens: float32 [4, 2048, 768], P('fsdp', 'ctx')
- grad_w_query: float32 [768, 768], P('fsdp')
- grad_w_key: float32 [768, 768], P('fsdp')
- grad_w_value: float32 [768, 768], P('fsdp')
- grad_w_attn_out: float32 [768, 768], P('fsdp')
- grad_b_query: float32 [768], P('fsdp')
- grad_b_value: float32 [768], P('fsdp')
- grad_b_attn_out: float32 [768], P('fsdp')
- grad_norm1_gain: float32 [768], P('fsdp')
- grad_norm1_bias: float32 [768], P('fsdp')
- grad_w_in: float32 [768, 3072], P('fsdp')
- grad_b_in: float32 [3072], P('fsdp')
- grad_w_out: float32 [3072, 768], P('fsdp')
- grad_b_out: float32 [768], P('fsdp')
- grad_norm2_gain: float32 [768], P('fsdp')
- grad_norm2_bias: float32 [768], P('fsdp')
Inputs may be any that keep to these rules, and one draw needn't show every extreme that they name: `seq_lengths`: row g gives the tokens of the 2 sequences of group g; each sequence starts on a block boundary and is padded to whole blocks, and the padded sequences of a row fill exactly its 16 blocks. `deal`: each row is a permutation of the natural blocks of its group; dealt slot b lies on the device with ctx index b // 2.
All inputs are finite; a program needn't handle non-finite values.
Results may differ from a plain program's by a relative error of at most 0.024.
Values may be sent and summed in bfloat16 or wider, within the bound.
A program may use at most 192 MiB of HBM per device.

v0:
```python
import jax
import jax.numpy as jnp
from jax import lax
from jax.sharding import PartitionSpec as P

HEADS = 12
HEAD_DIM = 64
BLOCK = 128


EPSILON = 1e-12
NEG_FILL = -1e30


def block_codes(lengths, deal_row):
    padded = (lengths + BLOCK - 1) // BLOCK * BLOCK
    seq_ends = jnp.cumsum(padded)
    offsets = jnp.tile(jnp.arange(BLOCK, dtype=jnp.int32), deal_row.shape[0])
    natural = jnp.repeat(deal_row * BLOCK, BLOCK) + offsets
    passed = (natural[:, None] >= seq_ends[None, :]).astype(jnp.int32)
    seq_ids = jnp.sum(passed, axis=1)
    begins = jnp.sum(passed * padded[None, :], axis=1)
    owners = (seq_ids[:, None] == jnp.arange(lengths.shape[0], dtype=jnp.int32)[None, :]).astype(
        jnp.int32
    )
    own_length = jnp.sum(owners * lengths[None, :], axis=1)
    key_codes = jnp.where(natural - begins < own_length, seq_ids, -1)
    return (seq_ids, key_codes)


def to_half(value):
    return value.astype(jnp.bfloat16)


def exact_gelu(value):
    return jax.nn.gelu(value, approximate=False)


def split_heads(matrix):
    return matrix.reshape(matrix.shape[0], HEADS, HEAD_DIM)


def sub_width(rows):
    width = rows
    while width > 1024 and width % 2 == 0:
        width = width // 2
    return width


def add_rows(total, term, at_row):
    current = lax.dynamic_slice_in_dim(total, at_row, term.shape[0])
    return lax.dynamic_update_slice_in_dim(total, current + term, at_row, 0)


def norm_forward(residual, gain, shift):
    centre = residual - jnp.mean(residual, axis=-1, keepdims=True)
    spread = jnp.mean(centre * centre, axis=-1, keepdims=True)
    inverse = lax.rsqrt(spread + EPSILON)
    normed = centre * inverse
    return (normed * gain + shift, normed, inverse)


def norm_backward(upstream, gain, normed, inverse):
    scaled = upstream * gain
    across = jnp.mean(scaled, axis=-1, keepdims=True)
    along = jnp.mean(scaled * normed, axis=-1, keepdims=True)
    grad_residual = inverse * (scaled - across - normed * along)
    return (grad_residual, jnp.sum(upstream * normed, axis=0), jnp.sum(upstream, axis=0))


def score_grads(
    query_heads, grad_heads, key_part, value_part, query_ids, code_part, log_totals, delta, scale
):
    scores = (
        jnp.einsum("qhd,khd->hqk", query_heads, key_part, preferred_element_type=jnp.float32)
        * scale
    )
    scores = jnp.where((query_ids[:, None] == code_part[None, :])[None], scores, NEG_FILL)
    probs = jnp.exp(scores - log_totals[:, :, None])
    grad_probs = jnp.einsum(
        "qhd,khd->hqk", grad_heads, value_part, preferred_element_type=jnp.float32
    )
    grad_scores = (probs * (grad_probs - delta[:, :, None])).astype(jnp.bfloat16)
    return (probs, grad_scores)


def attend_forward(query_heads, query_ids, key_codes_all, scale, carry, piece):
    keys, values = piece
    rows = keys.shape[0]
    width = sub_width(rows)

    def one_block(state, offset):
        running, totals, accum = state
        key_part = split_heads(lax.dynamic_slice_in_dim(keys, offset, width))
        value_part = split_heads(lax.dynamic_slice_in_dim(values, offset, width))
        code_part = lax.dynamic_slice_in_dim(key_codes_all, offset, width)
        scores = (
            jnp.einsum("qhd,khd->hqk", query_heads, key_part, preferred_element_type=jnp.float32)
            * scale
        )
        scores = jnp.where((query_ids[:, None] == code_part[None, :])[None], scores, NEG_FILL)
        newest = jnp.maximum(running, jnp.max(scores, axis=-1))
        factor = jnp.exp(running - newest)
        weights = jnp.exp(scores - newest[:, :, None])
        totals = totals * factor + jnp.sum(weights, axis=-1)
        mixed = jnp.einsum(
            "hqk,khd->qhd",
            weights.astype(jnp.bfloat16),
            value_part,
            preferred_element_type=jnp.float32,
        )
        accum = accum * jnp.transpose(factor)[:, :, None] + mixed
        return ((newest, totals, accum), None)

    carry, unused = lax.scan(one_block, carry, jnp.arange(rows // width, dtype=jnp.int32) * width)
    return carry


def attend_back(
    query_heads, grad_heads, query_ids, key_codes_all, log_totals, delta, scale, carry, piece
):
    keys, values = piece
    rows = keys.shape[0]
    width = sub_width(rows)

    def one_block(state, offset):
        grad_query, grad_keys_all, grad_values_all = state
        key_part = split_heads(lax.dynamic_slice_in_dim(keys, offset, width))
        value_part = split_heads(lax.dynamic_slice_in_dim(values, offset, width))
        code_part = lax.dynamic_slice_in_dim(key_codes_all, offset, width)
        probs, grad_scores = score_grads(
            query_heads,
            grad_heads,
            key_part,
            value_part,
            query_ids,
            code_part,
            log_totals,
            delta,
            scale,
        )
        grad_query = (
            grad_query
            + jnp.einsum("hqk,khd->qhd", grad_scores, key_part, preferred_element_type=jnp.float32)
            * scale
        )
        key_term = (
            jnp.einsum("hqk,qhd->khd", grad_scores, query_heads, preferred_element_type=jnp.float32)
            * scale
        )
        value_term = jnp.einsum(
            "hqk,qhd->khd",
            probs.astype(jnp.bfloat16),
            grad_heads,
            preferred_element_type=jnp.float32,
        )
        grad_keys_all = add_rows(grad_keys_all, key_term.reshape(width, HEADS * HEAD_DIM), offset)
        grad_values_all = add_rows(
            grad_values_all, value_term.reshape(width, HEADS * HEAD_DIM), offset
        )
        return ((grad_query, grad_keys_all, grad_values_all), None)

    carry, unused = lax.scan(one_block, carry, jnp.arange(rows // width, dtype=jnp.int32) * width)
    return carry


def body(
    tokens,
    seq_lengths,
    deal,
    w_query,
    w_key,
    w_value,
    w_attn_out,
    b_query,
    b_value,
    b_attn_out,
    norm1_gain,
    norm1_bias,
    w_in,
    b_in,
    w_out,
    b_out,
    norm2_gain,
    norm2_bias,
    cotangent,
):
    gathered = (
        lax.all_gather(to_half(w_query), "fsdp", axis=0, tiled=True),
        lax.all_gather(to_half(w_key), "fsdp", axis=0, tiled=True),
        lax.all_gather(to_half(w_value), "fsdp", axis=0, tiled=True),
        lax.all_gather(to_half(w_attn_out), "fsdp", axis=0, tiled=True),
        lax.all_gather(to_half(b_query), "fsdp", axis=0, tiled=True),
        lax.all_gather(to_half(b_value), "fsdp", axis=0, tiled=True),
        lax.all_gather(to_half(b_attn_out), "fsdp", axis=0, tiled=True),
        lax.all_gather(to_half(norm1_gain), "fsdp", axis=0, tiled=True),
        lax.all_gather(to_half(norm1_bias), "fsdp", axis=0, tiled=True),
        lax.all_gather(to_half(w_in), "fsdp", axis=0, tiled=True),
        lax.all_gather(to_half(b_in), "fsdp", axis=0, tiled=True),
        lax.all_gather(to_half(w_out), "fsdp", axis=0, tiled=True),
        lax.all_gather(to_half(b_out), "fsdp", axis=0, tiled=True),
        lax.all_gather(to_half(norm2_gain), "fsdp", axis=0, tiled=True),
        lax.all_gather(to_half(norm2_bias), "fsdp", axis=0, tiled=True),
    )
    (
        query_weight,
        key_weight,
        value_weight,
        mix_weight,
        query_bias,
        value_bias,
        mix_bias,
        gain_one,
        shift_one,
        inner_weight,
        inner_bias,
        outer_weight,
        outer_bias,
        gain_two,
        shift_two,
    ) = gathered
    scale = HEAD_DIM ** (-0.5)
    inputs = tokens[0]
    rows = inputs.shape[0]
    query_ids_all, key_codes_all = block_codes(seq_lengths[0], deal[0])
    first_row = lax.axis_index("ctx") * rows
    query_ids = lax.dynamic_slice_in_dim(query_ids_all, first_row, rows)
    query = (
        jnp.dot(inputs, query_weight, preferred_element_type=jnp.float32)
        + query_bias.astype(jnp.float32)
    ).astype(jnp.bfloat16)
    keys = jnp.dot(inputs, key_weight, preferred_element_type=jnp.float32).astype(jnp.bfloat16)
    values = (
        jnp.dot(inputs, value_weight, preferred_element_type=jnp.float32)
        + value_bias.astype(jnp.float32)
    ).astype(jnp.bfloat16)
    query_heads = split_heads(query)
    start_state = (
        jnp.full((HEADS, rows), NEG_FILL, jnp.float32),
        jnp.zeros((HEADS, rows), jnp.float32),
        jnp.zeros((rows, HEADS, HEAD_DIM), jnp.float32),
    )
    running, totals, accum = attend_forward(
        query_heads,
        query_ids,
        key_codes_all,
        scale,
        start_state,
        (
            lax.all_gather(keys, "ctx", axis=0, tiled=True),
            lax.all_gather(values, "ctx", axis=0, tiled=True),
        ),
    )
    out_heads = accum / jnp.transpose(totals)[:, :, None]
    log_totals = running + jnp.log(totals)
    attn_in = out_heads.reshape(rows, HEADS * HEAD_DIM).astype(jnp.bfloat16)
    residual_one = (
        inputs.astype(jnp.float32)
        + jnp.dot(attn_in, mix_weight, preferred_element_type=jnp.float32)
        + mix_bias.astype(jnp.float32)
    )
    normal_one, normed_one, inverse_one = norm_forward(
        residual_one, gain_one.astype(jnp.float32), shift_one.astype(jnp.float32)
    )
    normal_half = normal_one.astype(jnp.bfloat16)
    pre_act = jnp.dot(
        normal_half, inner_weight, preferred_element_type=jnp.float32
    ) + inner_bias.astype(jnp.float32)
    activated, gelu_pull = jax.vjp(exact_gelu, pre_act)
    hidden = activated.astype(jnp.bfloat16)
    residual_two = (
        normal_one
        + jnp.dot(hidden, outer_weight, preferred_element_type=jnp.float32)
        + outer_bias.astype(jnp.float32)
    )
    layer_out, normed_two, inverse_two = norm_forward(
        residual_two, gain_two.astype(jnp.float32), shift_two.astype(jnp.float32)
    )
    upstream = cotangent[0].astype(jnp.float32)
    grad_two, grad_gain_two, grad_shift_two = norm_backward(
        upstream, gain_two.astype(jnp.float32), normed_two, inverse_two
    )
    grad_branch = grad_two.astype(jnp.bfloat16)
    grad_outer_bias = jnp.sum(grad_branch.astype(jnp.float32), axis=0)
    grad_outer = jnp.einsum("tf,td->fd", hidden, grad_branch, preferred_element_type=jnp.float32)
    grad_hidden = jnp.einsum(
        "td,fd->tf", grad_branch, outer_weight, preferred_element_type=jnp.float32
    )
    grad_pre = gelu_pull(grad_hidden)[0].astype(jnp.bfloat16)
    grad_inner_bias = jnp.sum(grad_pre.astype(jnp.float32), axis=0)
    grad_inner = jnp.einsum("td,tf->df", normal_half, grad_pre, preferred_element_type=jnp.float32)
    grad_normal = grad_two + jnp.einsum(
        "tf,df->td", grad_pre, inner_weight, preferred_element_type=jnp.float32
    )
    grad_one, grad_gain_one, grad_shift_one = norm_backward(
        grad_normal, gain_one.astype(jnp.float32), normed_one, inverse_one
    )
    grad_attn = grad_one.astype(jnp.bfloat16)
    grad_mix_bias = jnp.sum(grad_attn.astype(jnp.float32), axis=0)
    grad_mix = jnp.einsum("td,te->de", attn_in, grad_attn, preferred_element_type=jnp.float32)
    grad_mixed = jnp.einsum(
        "te,de->td", grad_attn, mix_weight, preferred_element_type=jnp.float32
    ).astype(jnp.bfloat16)
    grad_heads = split_heads(grad_mixed)
    delta = jnp.einsum("qhd,qhd->hq", grad_heads.astype(jnp.float32), out_heads)
    group_rows = key_codes_all.shape[0]
    start_back = (
        jnp.zeros((rows, HEADS, HEAD_DIM), jnp.float32),
        jnp.zeros((group_rows, HEADS * HEAD_DIM), jnp.float32),
        jnp.zeros((group_rows, HEADS * HEAD_DIM), jnp.float32),
    )
    grad_query_heads, grad_keys_all, grad_values_all = attend_back(
        query_heads,
        grad_heads,
        query_ids,
        key_codes_all,
        log_totals,
        delta,
        scale,
        start_back,
        (
            lax.all_gather(keys, "ctx", axis=0, tiled=True),
            lax.all_gather(values, "ctx", axis=0, tiled=True),
        ),
    )
    grad_keys_flat, grad_values_flat = (
        lax.psum_scatter(
            grad_keys_all.astype(jnp.bfloat16), "ctx", scatter_dimension=0, tiled=True
        ).astype(jnp.float32),
        lax.psum_scatter(
            grad_values_all.astype(jnp.bfloat16), "ctx", scatter_dimension=0, tiled=True
        ).astype(jnp.float32),
    )
    grad_query_half = grad_query_heads.reshape(rows, HEADS * HEAD_DIM).astype(jnp.bfloat16)
    grad_keys_half = grad_keys_flat.astype(jnp.bfloat16)
    grad_values_half = grad_values_flat.astype(jnp.bfloat16)
    grad_query_weight = jnp.einsum(
        "td,te->de", inputs, grad_query_half, preferred_element_type=jnp.float32
    )
    grad_key_weight = jnp.einsum(
        "td,te->de", inputs, grad_keys_half, preferred_element_type=jnp.float32
    )
    grad_value_weight = jnp.einsum(
        "td,te->de", inputs, grad_values_half, preferred_element_type=jnp.float32
    )
    grad_query_bias = jnp.sum(grad_query_half.astype(jnp.float32), axis=0)
    grad_value_bias = jnp.sum(grad_values_half.astype(jnp.float32), axis=0)
    grad_inputs = (
        grad_one
        + jnp.einsum("te,de->td", grad_query_half, query_weight, preferred_element_type=jnp.float32)
        + jnp.einsum("te,de->td", grad_keys_half, key_weight, preferred_element_type=jnp.float32)
        + jnp.einsum(
            "te,de->td", grad_values_half, value_weight, preferred_element_type=jnp.float32
        )
    )
    shares = (
        lax.psum_scatter(
            grad_query_weight.astype(jnp.bfloat16), "fsdp", scatter_dimension=0, tiled=True
        ).astype(jnp.float32),
        lax.psum_scatter(
            grad_key_weight.astype(jnp.bfloat16), "fsdp", scatter_dimension=0, tiled=True
        ).astype(jnp.float32),
        lax.psum_scatter(
            grad_value_weight.astype(jnp.bfloat16), "fsdp", scatter_dimension=0, tiled=True
        ).astype(jnp.float32),
        lax.psum_scatter(
            grad_mix.astype(jnp.bfloat16), "fsdp", scatter_dimension=0, tiled=True
        ).astype(jnp.float32),
        lax.psum_scatter(
            grad_query_bias.astype(jnp.bfloat16), "fsdp", scatter_dimension=0, tiled=True
        ).astype(jnp.float32),
        lax.psum_scatter(
            grad_value_bias.astype(jnp.bfloat16), "fsdp", scatter_dimension=0, tiled=True
        ).astype(jnp.float32),
        lax.psum_scatter(
            grad_mix_bias.astype(jnp.bfloat16), "fsdp", scatter_dimension=0, tiled=True
        ).astype(jnp.float32),
        lax.psum_scatter(
            grad_gain_one.astype(jnp.bfloat16), "fsdp", scatter_dimension=0, tiled=True
        ).astype(jnp.float32),
        lax.psum_scatter(
            grad_shift_one.astype(jnp.bfloat16), "fsdp", scatter_dimension=0, tiled=True
        ).astype(jnp.float32),
        lax.psum_scatter(
            grad_inner.astype(jnp.bfloat16), "fsdp", scatter_dimension=0, tiled=True
        ).astype(jnp.float32),
        lax.psum_scatter(
            grad_inner_bias.astype(jnp.bfloat16), "fsdp", scatter_dimension=0, tiled=True
        ).astype(jnp.float32),
        lax.psum_scatter(
            grad_outer.astype(jnp.bfloat16), "fsdp", scatter_dimension=0, tiled=True
        ).astype(jnp.float32),
        lax.psum_scatter(
            grad_outer_bias.astype(jnp.bfloat16), "fsdp", scatter_dimension=0, tiled=True
        ).astype(jnp.float32),
        lax.psum_scatter(
            grad_gain_two.astype(jnp.bfloat16), "fsdp", scatter_dimension=0, tiled=True
        ).astype(jnp.float32),
        lax.psum_scatter(
            grad_shift_two.astype(jnp.bfloat16), "fsdp", scatter_dimension=0, tiled=True
        ).astype(jnp.float32),
    )
    summed = (
        lax.psum(shares[0].astype(jnp.bfloat16), "ctx").astype(jnp.float32),
        lax.psum(shares[1].astype(jnp.bfloat16), "ctx").astype(jnp.float32),
        lax.psum(shares[2].astype(jnp.bfloat16), "ctx").astype(jnp.float32),
        lax.psum(shares[3].astype(jnp.bfloat16), "ctx").astype(jnp.float32),
        lax.psum(shares[4].astype(jnp.bfloat16), "ctx").astype(jnp.float32),
        lax.psum(shares[5].astype(jnp.bfloat16), "ctx").astype(jnp.float32),
        lax.psum(shares[6].astype(jnp.bfloat16), "ctx").astype(jnp.float32),
        lax.psum(shares[7].astype(jnp.bfloat16), "ctx").astype(jnp.float32),
        lax.psum(shares[8].astype(jnp.bfloat16), "ctx").astype(jnp.float32),
        lax.psum(shares[9].astype(jnp.bfloat16), "ctx").astype(jnp.float32),
        lax.psum(shares[10].astype(jnp.bfloat16), "ctx").astype(jnp.float32),
        lax.psum(shares[11].astype(jnp.bfloat16), "ctx").astype(jnp.float32),
        lax.psum(shares[12].astype(jnp.bfloat16), "ctx").astype(jnp.float32),
        lax.psum(shares[13].astype(jnp.bfloat16), "ctx").astype(jnp.float32),
        lax.psum(shares[14].astype(jnp.bfloat16), "ctx").astype(jnp.float32),
    )
    return (
        layer_out.astype(jnp.bfloat16)[None],
        grad_inputs[None],
        summed[0],
        summed[1],
        summed[2],
        summed[3],
        summed[4],
        summed[5],
        summed[6],
        summed[7],
        summed[8],
        summed[9],
        summed[10],
        summed[11],
        summed[12],
        summed[13],
        summed[14],
    )


def solution(mesh):
    placed = (
        P("fsdp", "ctx", None),
        P("fsdp", None),
        P("fsdp", None),
        P("fsdp", None),
        P("fsdp", None),
        P("fsdp", None),
        P("fsdp", None),
        P("fsdp"),
        P("fsdp"),
        P("fsdp"),
        P("fsdp"),
        P("fsdp"),
        P("fsdp", None),
        P("fsdp"),
        P("fsdp", None),
        P("fsdp"),
        P("fsdp"),
        P("fsdp"),
        P("fsdp", "ctx", None),
    )
    return jax.shard_map(
        body,
        mesh=mesh,
        in_specs=placed,
        out_specs=(
            P("fsdp", "ctx", None),
            P("fsdp", "ctx", None),
            P("fsdp", None),
            P("fsdp", None),
            P("fsdp", None),
            P("fsdp", None),
            P("fsdp"),
            P("fsdp"),
            P("fsdp"),
            P("fsdp"),
            P("fsdp"),
            P("fsdp", None),
            P("fsdp"),
            P("fsdp", None),
            P("fsdp"),
            P("fsdp"),
            P("fsdp"),
        ),
        check_vma=False,
    )
```

profile of v0, /device:TPU:0, one launch (start us, length us, event | category | flops | bytes accessed | tf_op | source)
XLA Modules:
  0.0 999.6 jit_solution(6662218395162565756)
XLA Ops:
  13.2 17.3 %all-gather.10.cloned.1.call-done = bf16[768,768]{1,0:T(8,128)(2,1)} async-done(((bf16[192,768]{1,0:T(8,128)(2,1)}), bf16[768,768]{1,0:T(8,128)(2,1)}) %all-gather.10.cloned.1.call-update) | async-done | bytes 1179664 | tf_op jit(solution)/shard_map/all_gather | solution.py:190
  35.9 10.8 %all-reduce.20 = (bf16[768]{0:T(1024)(128)(2,1)S(1)}, bf16[768]{0:T(1024)(128)(2,1)S(1)}, bf16[768]{0:T(1024)(128)(2,1)S(1)}, bf16[768]{0:T(1024)(128)(2,1)S(1)}...) all-reduce(bf16[768]{0:T(1024)(128)(2,1)S(1)} %dynamic-update-slice, ...), channel_id=1, replica_groups=mesh['ctx'=8,'fsdp'=4] {'fsdp'}, use_global_device_ids=true, to_apply=%add | all-reduce | flops 5376 | bytes 21504
  46.7 3.5 all-gather.16.cloned.1.call-done
  60.1 5.4 all-gather
  71.9 61.2 %all-gather.12.cloned.1.call-done = bf16[2048,768]{1,0:T(8,128)(2,1)} async-done(((bf16[256,768]{1,0:T(8,128)(2,1)}), bf16[2048,768]{1,0:T(8,128)(2,1)}) %all-gather.12.cloned.1.call-update) | async-done | bytes 3145744 | tf_op jit(solution)/shard_map/all_gather | solution.py:250
  133.0 4.7 copy.81
  137.7 57.0 %all-gather.18.cloned.1.call-done = bf16[2048,768]{1,0:T(8,128)(2,1)} async-done(((bf16[256,768]{1,0:T(8,128)(2,1)}), bf16[2048,768]{1,0:T(8,128)(2,1)}) %all-gather.18.cloned.1.call-update) | async-done | bytes 3145744 | tf_op jit(solution)/shard_map/all_gather | solution.py:251
  194.7 4.7 copy.82
  199.5 48.9 %while.30 = (s32[]{:T(128)}, f32[12,256]{1,0:T(8,128)S(1)}, f32[12,256]{1,0:T(8,128)S(1)}, f32[256,12,64]{0,2,1:T(8,128)S(1)}, s32[256]{0:T(256)S(1)}, /*index=5...) while((s32[]{:T(128)}, f32[12,256]{1,0:T(8,128)S(1)}, ...), condition=%wide.region_7.8_spmd.clone, body=%wide.region_4.7_spmd.clone.sunk | while | flops 840779776 | bytes 100742368 | solution.py:115
  202.3 3.7 constant_dynamic-slice_fusion.7
  206.0 6.7 fusion.145
  212.8 7.2 fusion.147
  226.9 3.4 constant_dynamic-slice_fusion.7
  230.3 6.7 fusion.145
  237.0 7.3 fusion.147
  253.5 11.8 %multiply_convert_fusion = (bf16[256,3072]{1,0:T(8,128)(2,1)S(1)}, f32[256,3072]{1,0:T(8,128)}, f32[256,3072]{1,0:T(8,128)}) fusion(f32[3072]{0:T(1024)S(1)} %bitcast.218, bf16[768,3072]{1,0:T(8,128)(2,1)} %all-gather.22.cloned.1.call-done, f32[256,768]{1,0:T(8,128)S(1)} %get-tuple-element.487, f32[768]{0:T(1024)S(1)} %copy-done.38, ...), kind=kOutput, calls=%fused_computation.45 | convolution fusion | flops 1260847104 | bytes 13389824 | tf_op jit(solution)/shard_map/dot_general | solution.py:266
  265.3 26.3 %all-gather.24.cloned.1.call-done = bf16[3072,768]{1,0:T(8,128)(2,1)} async-done(((bf16[768,768]{1,0:T(8,128)(2,1)}), bf16[3072,768]{1,0:T(8,128)(2,1)}) %all-gather.24.cloned.1.call-update) | async-done | bytes 4718608 | tf_op jit(solution)/shard_map/all_gather | solution.py:200
  291.6 4.0 fusion.77
  310.7 3.4 broadcast.241.clone
  314.2 142.7 %while.31 = (s32[]{:T(128)}, f32[256,12,64]{0,2,1:T(8,128)}, f32[2048,768]{0,1:T(8,128)}, f32[2048,768]{0,1:T(8,128)}, s32[2]{0:T(128)S(1)}, /*index=5*/bf16[204...) while((s32[]{:T(128)}, f32[256,12,64]{0,2,1:T(8,128)}, ...), condition=%wide.region_17.18_spmd.clone, body=%wide.region_16.17_spmd.clone.sunk | while | flops 2047934464 | bytes 192349648 | solution.py:163
  322.3 3.5 constant_dynamic-slice_fusion.9
  325.8 7.0 fusion.161
  332.8 5.0 fusion.162
  337.9 9.4 fusion.163
  349.3 6.7 bitcast_add_fusion.3
  356.0 15.6 %dynamic_update_slice.10 = f32[2048,768]{0,1:T(8,128)} dynamic-update-slice(f32[2048,768]{0,1:T(8,128)} %get-tuple-element.709, f32[1024,768]{0,1:T(8,128)} %get-tuple-element.650, s32[]{:T(128)S(6)} %select_n.88, s32[]{:T(128)} %constant.74.clone.1..sunk.1) | dynamic-update-slice | bytes 6291460 | tf_op jit(solution)/shard_map/while/body/eval_jaxpr/dynamic_update_slice | solution.py:52
  371.6 15.0 %dynamic_update_slice.11 = f32[2048,768]{0,1:T(8,128)} dynamic-update-slice(f32[2048,768]{0,1:T(8,128)} %get-tuple-element.710, f32[1024,768]{0,1:T(8,128)S(1)} %get-tuple-element.651, s32[]{:T(128)S(6)} %select_n.88, s32[]{:T(128)} %constant.74.clone.1..sunk.1) | dynamic-update-slice | bytes 6291460 | tf_op jit(solution)/shard_map/while/body/eval_jaxpr/dynamic_update_slice | solution.py:52
  397.8 7.2 fusion.161
  405.0 5.2 fusion.162
  410.2 9.4 fusion.163
  421.6 6.5 bitcast_add_fusion.3
  428.1 14.8 %dynamic_update_slice.10 = f32[2048,768]{0,1:T(8,128)} dynamic-update-slice(f32[2048,768]{0,1:T(8,128)} %get-tuple-element.709, f32[1024,768]{0,1:T(8,128)} %get-tuple-element.650, s32[]{:T(128)S(6)} %select_n.88, s32[]{:T(128)} %constant.74.clone.1..sunk.1) | dynamic-update-slice | bytes 6291460 | tf_op jit(solution)/shard_map/while/body/eval_jaxpr/dynamic_update_slice | solution.py:52
  442.9 13.8 %dynamic_update_slice.11 = f32[2048,768]{0,1:T(8,128)} dynamic-update-slice(f32[2048,768]{0,1:T(8,128)} %get-tuple-element.710, f32[1024,768]{0,1:T(8,128)S(1)} %get-tuple-element.651, s32[]{:T(128)S(6)} %select_n.88, s32[]{:T(128)} %constant.74.clone.1..sunk.1) | dynamic-update-slice | bytes 6291460 | tf_op jit(solution)/shard_map/while/body/eval_jaxpr/dynamic_update_slice | solution.py:52
  456.9 4.9 convert_element_type.315
  462.0 4.9 convert_element_type.316
  470.3 67.0 %reduce-scatter.15.cloned.1.call-done = bf16[256,768]{0,1:T(8,128)(2,1)} async-done(((bf16[2048,768]{0,1:T(8,128)(2,1)}), bf16[256,768]{0,1:T(8,128)(2,1)}) %reduce-scatter.15.cloned.1.call-update) | async-done | bytes 393232 | tf_op jit(solution)/shard_map/reduce_scatter | solution.py:327
  540.3 74.6 %reduce-scatter.17.cloned.1.call-done = bf16[256,768]{0,1:T(8,128)(2,1)} async-done(((bf16[2048,768]{0,1:T(8,128)(2,1)}), bf16[256,768]{0,1:T(8,128)(2,1)}) %reduce-scatter.17.cloned.1.call-update) | async-done | bytes 393232 | tf_op jit(solution)/shard_map/reduce_scatter | solution.py:330
  619.6 5.2 convolution_convert_fusion.1
  626.4 3.6 convolution_convert_fusion
  630.1 12.2 %reduce-scatter.25.cloned.1.call-done = bf16[192,768]{1,0:T(8,128)(2,1)} async-done(((bf16[768,768]{1,0:T(8,128)(2,1)}), bf16[192,768]{1,0:T(8,128)(2,1)}) %reduce-scatter.25.cloned.1.call-update) | async-done | bytes 294928
  644.2 26.5 %reduce-scatter.27.cloned.1.call-done = bf16[192,768]{1,0:T(8,128)(2,1)} async-done(((bf16[768,768]{1,0:T(8,128)(2,1)}), bf16[192,768]{1,0:T(8,128)(2,1)}) %reduce-scatter.27.cloned.1.call-update) | async-done | bytes 294928
  672.6 26.4 %reduce-scatter.29.cloned.1.call-done = bf16[192,768]{1,0:T(8,128)(2,1)} async-done(((bf16[768,768]{1,0:T(8,128)(2,1)}), bf16[192,768]{1,0:T(8,128)(2,1)}) %reduce-scatter.29.cloned.1.call-update) | async-done | bytes 294928
  700.9 26.5 %reduce-scatter.19.cloned.1.call-done = bf16[192,768]{1,0:T(8,128)(2,1)} async-done(((bf16[768,768]{1,0:T(8,128)(2,1)}), bf16[192,768]{1,0:T(8,128)(2,1)}) %reduce-scatter.19.cloned.1.call-update) | async-done | bytes 294928 | tf_op jit(solution)/shard_map/reduce_scatter | solution.py:366
  727.3 50.3 %reduce-scatter.21.cloned.1.call-done = bf16[192,3072]{1,0:T(8,128)(2,1)} async-done(((bf16[768,3072]{1,0:T(8,128)(2,1)}), bf16[192,3072]{1,0:T(8,128)(2,1)}) %reduce-scatter.21.cloned.1.call-update) | async-done | bytes 1179664 | tf_op jit(solution)/shard_map/reduce_scatter | solution.py:384
  777.6 50.5 %reduce-scatter.23.cloned.1.call-done = bf16[768,768]{1,0:T(8,128)(2,1)} async-done(((bf16[3072,768]{1,0:T(8,128)(2,1)}), bf16[768,768]{1,0:T(8,128)(2,1)}) %reduce-scatter.23.cloned.1.call-update) | async-done | bytes 1179664 | tf_op jit(solution)/shard_map/reduce_scatter | solution.py:390
  833.8 11.3 %all-reduce.19 = (bf16[768]{0:T(1024)(128)(2,1)S(1)}, bf16[768]{0:T(1024)(128)(2,1)S(1)}, bf16[768]{0:T(1024)(128)(2,1)S(1)}, bf16[768]{0:T(1024)(128)(2,1)S(1)}...) all-reduce(bf16[768]{0:T(1024)(128)(2,1)S(1)} %dynamic-update-slice, ...), channel_id=1, replica_groups=mesh['ctx'=8,'fsdp'=4] {'fsdp'}, use_global_device_ids=true, to_apply=%add.7 | all-reduce | flops 9984 | bytes 39936
  845.8 23.2 %all-reduce.17 = (bf16[192]{0:T(256)(128)(2,1)S(1)}, bf16[192]{0:T(256)(128)(2,1)S(1)}, bf16[192]{0:T(256)(128)(2,1)S(1)}, bf16[192]{0:T(256)(128)(2,1)S(1)}, bf...) all-reduce(bf16[192]{0:T(256)(128)(2,1)S(1)} %dynamic-slice.9, ...), channel_id=1, replica_groups=mesh['ctx'=8,'fsdp'=4] {'ctx'}, use_global_device_ids=true, to_apply=%region_30.31 | all-reduce | flops 2304 | bytes 9216 | tf_op jit(solution)/shard_map/psum | solution.py:408
  878.3 104.3 %all-reduce.23.cloned.1.call-done = (bf16[192,768]{0,1:T(8,128)(2,1)}, bf16[192,768]{0,1:T(8,128)(2,1)}, bf16[192,768]{0,1:T(8,128)(2,1)}, bf16[192,768]{1,0:T(8...) async-done(((bf16[192,768]{0,1:T(8,128)(2,1)}, bf16[192,768]{0,1:T(8,128)(2,1)}, bf16[192,768]{0,1:T(8,128)(2,1)}, bf16[192,768]{1,0:T(8,128)(2,1)}, ...) | async-done | bytes 3538960 | tf_op jit(solution)/shard_map/psum | solution.py:404
  (369 shorter events, 118.4 us)
Async XLA Ops:
  7.2 26.0 %copy-start.59 = (u32[32]{0:T(128)S(1)}, u32[32]{0:T(128)}, u32[]{:S(2)}) copy-start(u32[32]{0:T(128)} %constant.165) | copy-start | bytes 388
  7.2 23.2 %copy-start.9 = (bf16[1,256,768]{2,1,0:T(8,128)(2,1)S(1)}, bf16[1,256,768]{2,1,0:T(8,128)(2,1)}, u32[]{:S(2)}) copy-start(bf16[1,256,768]{2,1,0:T(8,128)(2,1)} %param.23) | copy-start | bytes 1179652
  7.2 25.8 %copy-start.61 = (f32[192]{0:T(256)S(1)}, f32[192]{0:T(256)}, u32[]{:S(2)}) copy-start(f32[192]{0:T(256)} %param.30) | copy-start | bytes 2308
  7.2 25.8 %copy-start.62 = (f32[192]{0:T(256)S(1)}, f32[192]{0:T(256)}, u32[]{:S(2)}) copy-start(f32[192]{0:T(256)} %param.31) | copy-start | bytes 2308
  7.2 25.8 %copy-start.63 = (f32[192]{0:T(256)S(1)}, f32[192]{0:T(256)}, u32[]{:S(2)}) copy-start(f32[192]{0:T(256)} %param.32) | copy-start | bytes 2308
  7.2 25.9 %copy-start.64 = (f32[192]{0:T(256)S(1)}, f32[192]{0:T(256)}, u32[]{:S(2)}) copy-start(f32[192]{0:T(256)} %param.34) | copy-start | bytes 2308
  7.3 25.9 %copy-start.65 = (f32[192]{0:T(256)S(1)}, f32[192]{0:T(256)}, u32[]{:S(2)}) copy-start(f32[192]{0:T(256)} %param.33) | copy-start | bytes 2308
  7.3 25.9 %copy-start.66 = (f32[192]{0:T(256)S(1)}, f32[192]{0:T(256)}, u32[]{:S(2)}) copy-start(f32[192]{0:T(256)} %param.38) | copy-start | bytes 2308
  7.3 25.9 %copy-start.67 = (f32[192]{0:T(256)S(1)}, f32[192]{0:T(256)}, u32[]{:S(2)}) copy-start(f32[192]{0:T(256)} %param.39) | copy-start | bytes 2308
  7.3 23.2 %all-gather.10.cloned.1.call-start = ((), (), s32[]{:S(2)}) async-start(), calls=%async_computation.8 | async-start | bytes 1474560 | tf_op jit(solution)/shard_map/all_gather | solution.py:190
  9.3 40.9 %all-gather.16.cloned.1.call-start = ((), (), s32[]{:S(2)}) async-start(), calls=%async_computation.11 | async-start | bytes 1474560 | tf_op jit(solution)/shard_map/all_gather | solution.py:191
  11.2 41.6 %copy-start.29 = (f32[192,768]{1,0:T(8,128)S(1)}, f32[192,768]{1,0:T(8,128)}, u32[]{:S(2)}) copy-start(f32[192,768]{1,0:T(8,128)} %param.29) | copy-start | bytes 1769476
  11.2 58.8 %all-gather.14.cloned.1.call-start = ((), (), s32[]{:S(2)}) async-start(), calls=%async_computation.10 | async-start | bytes 1474560 | tf_op jit(solution)/shard_map/all_gather | solution.py:189
  13.1 119.9 %all-gather.12.cloned.1.call-start = ((), (), s32[]{:S(2)}) async-start(), calls=%async_computation.9 | async-start | bytes 3538944 | tf_op jit(solution)/shard_map/all_gather | solution.py:250
  33.0 161.8 %all-gather.18.cloned.1.call-start = ((), (), s32[]{:S(2)}) async-start(), calls=%async_computation.12 | async-start | bytes 3538944 | tf_op jit(solution)/shard_map/all_gather | solution.py:251
  52.7 197.8 %all-gather.20.cloned.1.call-start = ((), (), s32[]{:S(2)}) async-start(), calls=%async_computation.13 | async-start | bytes 1474560 | tf_op jit(solution)/shard_map/all_gather | solution.py:192
  53.6 199.9 %all-gather.22.cloned.1.call-start = ((), (), s32[]{:S(2)}) async-start(), calls=%async_computation.14 | async-start | bytes 5898240 | tf_op jit(solution)/shard_map/all_gather | solution.py:198
  56.5 9.7 copy-start.69
  56.5 235.1 %all-gather.24.cloned.1.call-start = ((), (), s32[]{:S(2)}) async-start(), calls=%async_computation.15 | async-start | bytes 5898240 | tf_op jit(solution)/shard_map/all_gather | solution.py:200
  59.4 477.9 %reduce-scatter.15.cloned.1.call-start = ((), (), s32[]{:S(2)}) async-start(), calls=%async_computation.16 | async-start | bytes 3538944 | tf_op jit(solution)/shard_map/reduce_scatter | solution.py:327
  212.7 8.2 copy-start
  237.0 8.3 copy-start
  252.5 50.5 %copy-start.3 = (f32[256,768]{1,0:T(8,128)}, f32[256,768]{1,0:T(8,128)S(1)}, u32[]{:S(2)}) copy-start(f32[256,768]{1,0:T(8,128)S(1)} %get-tuple-element.487) | copy-start | bytes 2359300
  252.6 12.7 %copy-start.44 = (f32[256]{0:T(256)}, f32[256]{0:T(256)S(1)}, u32[]{:S(2)}) copy-start(f32[256]{0:T(256)S(1)} %broadcast_multiply_fusion.5) | copy-start | bytes 3076
  252.8 12.4 %copy-start.52 = (f32[256]{0:T(256)}, f32[256]{0:T(256)S(1)}, u32[]{:S(2)}) copy-start(f32[256]{0:T(256)S(1)} %add_rsqrt_fusion.1) | copy-start | bytes 3076
  265.3 30.3 %copy-start.14 = (bf16[256,3072]{1,0:T(8,128)(2,1)}, bf16[256,3072]{1,0:T(8,128)(2,1)S(1)}, u32[]{:S(2)}) copy-start(bf16[256,3072]{1,0:T(8,128)(2,1)S(1)} %get-tuple-element.476) | copy-start | bytes 4718596
  320.9 11.9 %copy-start.1 = (f32[12,1024,256]{2,1,0:T(8,128)}, f32[12,1024,256]{2,1,0:T(8,128)S(1)}, u32[]{:S(2)}) copy-start(f32[12,1024,256]{2,1,0:T(8,128)S(1)} %fusion.160) | copy-start | bytes 37748740 | tf_op jit(solution)/shard_map/while
  332.8 14.5 %slice-start = ((s8[6291456]{0:T(1024)(128)(4,1)}), s8[4194304]{0:T(1024)(128)(4,1)S(1)}, s32[]{:S(2)}) async-start(s8[6291456]{0:T(1024)(128)(4,1)} %bitcast.204), calls=%async_computation.25 | async-start | bytes 8388608 | tf_op jit(solution)/shard_map/while
  337.9 9.4 slice-start.1
  393.1 11.9 %copy-start.1 = (f32[12,1024,256]{2,1,0:T(8,128)}, f32[12,1024,256]{2,1,0:T(8,128)S(1)}, u32[]{:S(2)}) copy-start(f32[12,1024,256]{2,1,0:T(8,128)S(1)} %fusion.160) | copy-start | bytes 37748740 | tf_op jit(solution)/shard_map/while
  405.0 14.6 %slice-start = ((s8[6291456]{0:T(1024)(128)(4,1)}), s8[4194304]{0:T(1024)(128)(4,1)S(1)}, s32[]{:S(2)}) async-start(s8[6291456]{0:T(1024)(128)(4,1)} %bitcast.204), calls=%async_computation.25 | async-start | bytes 8388608 | tf_op jit(solution)/shard_map/while
  410.2 9.4 slice-start.1
  461.9 153.0 %reduce-scatter.17.cloned.1.call-start = ((), (), s32[]{:S(2)}) async-start(), calls=%async_computation.17 | async-start | bytes 3538944 | tf_op jit(solution)/shard_map/reduce_scatter | solution.py:330
  466.9 175.5 %reduce-scatter.25.cloned.1.call-start = ((), (), s32[]{:S(2)}) async-start(), calls=%async_computation.21 | async-start | bytes 1474560
  470.3 200.4 %reduce-scatter.27.cloned.1.call-start = ((), (), s32[]{:S(2)}) async-start(), calls=%async_computation.22 | async-start | bytes 1474560
  540.2 77.7 %copy-start.8 = (f32[256,768]{1,0:T(8,128)S(1)}, f32[256,768]{1,0:T(8,128)}, u32[]{:S(2)}) copy-start(f32[256,768]{1,0:T(8,128)} %copy-done.7) | copy-start | bytes 2359300
  540.2 77.7 %copy-start.17 = (bf16[256,12,64]{0,2,1:T(8,128)(2,1)S(1)}, bf16[256,12,64]{0,2,1:T(8,128)(2,1)}, u32[]{:S(2)}) copy-start(bf16[256,12,64]{0,2,1:T(8,128)(2,1)} %copy-done.16) | copy-start | bytes 1179652
  540.3 158.7 %reduce-scatter.29.cloned.1.call-start = ((), (), s32[]{:S(2)}) async-start(), calls=%async_computation.23 | async-start | bytes 1474560
  617.9 109.5 %reduce-scatter.19.cloned.1.call-start = ((), (), s32[]{:S(2)}) async-start(), calls=%async_computation.18 | async-start | bytes 1474560 | tf_op jit(solution)/shard_map/reduce_scatter | solution.py:366
  619.5 158.2 %reduce-scatter.21.cloned.1.call-start = ((), (), s32[]{:S(2)}) async-start(), calls=%async_computation.19 | async-start | bytes 5898240 | tf_op jit(solution)/shard_map/reduce_scatter | solution.py:384
  624.7 203.3 %reduce-scatter.23.cloned.1.call-start = ((), (), s32[]{:S(2)}) async-start(), calls=%async_computation.20 | async-start | bytes 5898240 | tf_op jit(solution)/shard_map/reduce_scatter | solution.py:390
  630.0 198.1 %copy-start.68 = (f32[192]{0:T(256)S(1)}, f32[192]{0:T(256)}, u32[]{:S(2)}) copy-start(f32[192]{0:T(256)} %param.40) | copy-start | bytes 2308
  630.0 198.6 %copy-start.19 = (bf16[1,256,768]{2,1,0:T(8,128)(2,1)S(1)}, bf16[1,256,768]{2,1,0:T(8,128)(2,1)}, u32[]{:S(2)}) copy-start(bf16[1,256,768]{2,1,0:T(8,128)(2,1)} %param.41) | copy-start | bytes 1179652
  630.1 352.5 %all-reduce.23.cloned.1.call-start = ((), (), s32[]{:S(2)}) async-start(), calls=%async_computation.24 | async-start | bytes 7667712 | tf_op jit(solution)/shard_map/psum | solution.py:404
  828.1 46.0 %copy-start.12 = (bf16[768,768]{1,0:T(8,128)(2,1)S(1)}, bf16[768,768]{1,0:T(8,128)(2,1)}, u32[]{:S(2)}) copy-start(bf16[768,768]{1,0:T(8,128)(2,1)} %all-gather.10.cloned.1.call-done) | copy-start | bytes 3538948
  828.1 46.0 %copy-start.24 = (bf16[256,768]{0,1:T(8,128)(2,1)S(1)}, bf16[256,768]{0,1:T(8,128)(2,1)}, u32[]{:S(2)}) copy-start(bf16[256,768]{0,1:T(8,128)(2,1)} %reduce-scatter.15.cloned.1.call-done) | copy-start | bytes 1179652
  869.0 6.9 copy-start.26
  982.6 7.0 copy-start.28
  (58 other events, 230.6 us)
Sparse Core Ops, SparseCore 0:
  10.3 20.1 all-gather.9
  32.6 17.5 all-gather.15
  52.4 17.5 all-gather.13
  72.6 60.4 all-gather.11
  135.6 59.0 all-gather.17
  196.7 16.0 all-gather.19
  215.0 37.4 all-gather.21
  254.0 37.4 all-gather.23
  462.0 75.2 reduce-scatter.14
  540.7 74.0 reduce-scatter.16
  617.4 24.8 reduce-scatter.24
  644.9 25.7 reduce-scatter.26
  673.3 25.7 reduce-scatter.28
  701.6 25.7 reduce-scatter.18
  729.7 47.8 reduce-scatter.20
  780.2 47.8 reduce-scatter.22
  832.9 149.6 all-reduce.22
where the time goes:
time: 1010 us; the launch traced here: 1000 us
  waiting for transfers between devices  605 us (60%)
  local copies, waits for them, and re-layouts  122 us (12%)
  matrix products  120 us (12%)
  other arithmetic  75.4 us (7%)
  blocking collectives  50.6 us (5%)
  between operations  17.1 us (2%)
    psum x1, waiting for transfers between devices, body(): lax.psum(shares[0].astype(jnp.bfloat16), 'ctx').astype(jnp.float32)  104 us
    reduce_scatter x1, waiting for transfers between devices, body(): lax.psum_scatter(grad_values_all.astype(jnp.bfloat16), 'ctx', scatter_dim...  74.6 us
    reduce_scatter x1, waiting for transfers between devices, body(): lax.psum_scatter(grad_keys_all.astype(jnp.bfloat16), 'ctx', scatter_dimen...  67 us
    unnamed x20, waiting for transfers between devices  65.4 us
    all_gather x1, waiting for transfers between devices, body(): lax.all_gather(keys, 'ctx', axis=0, tiled=True)  61.2 us
    dynamic_update_slice x4, local copies, waits for them, and re-layouts, add_rows(): return lax.dynamic_update_slice_in_dim(total, current + term, at_row, 0)  59.3 us
    all_gather x1, waiting for transfers between devices, body(): lax.all_gather(values, 'ctx', axis=0, tiled=True)  57 us
    reduce_scatter x1, waiting for transfers between devices, body(): lax.psum_scatter(grad_outer.astype(jnp.bfloat16), 'fsdp', scatter_dimensi...  50.5 us
  transfers between devices with their start and end apart: 17, of which 15 were waited for; matrix products, arithmetic and copies ran while one was open for 14% of the time, Pallas kernels for 0%

commit v1 on v0

--- a/solution.py
+++ b/solution.py
@@ -1,6 +1,10 @@
+import functools
+
 import jax
 import jax.numpy as jnp
 from jax import lax
+from jax.experimental import pallas as pl
+from jax.experimental.pallas import tpu as pltpu
 from jax.sharding import PartitionSpec as P
 
 HEADS = 12
@@ -163,8 +167,190 @@
     carry, unused = lax.scan(one_block, carry, jnp.arange(rows // width, dtype=jnp.int32) * width)
     return carry
 
+MESH=pl.DeviceIdType.MESH
+F32=jnp.float32; BF=jnp.bfloat16
+
+def places():
+    c=lax.axis_index("ctx"); f=lax.axis_index("fsdp")
+    z=c//2; x=c%2; y=f//2; k=f%2
+    return c,f,z,x,y,k
+
+def add_strips(rows, fn, step=16):
+    @pl.loop(0, rows//step)
+    def _(i):
+        fn(pl.ds(pl.multiple_of(i*step,step),step))
+
+def reduce_kernel(chunks, n_in, n_out, *refs):
+    n=len(chunks)
+    ins=refs[:n_in]; outs=refs[n_in:n_in+n_out]
+    scr=refs[n_in+n_out:]
+    loc=scr[0:n]; rc=scr[n:2*n]; ry=scr[2*n:3*n]; rx=scr[3*n:4*n]; cb=scr[4*n:5*n]; rz=scr[5*n:6*n]; res=scr[6*n:7*n]
+    (s_load,s_out,c_s,c_r,y_s,y_r,x_s,x_r,z_s,z_r,g_s,g_r,h_s,h_r)=scr[7*n:]
+    c,f,z,x,y,k=places()
+    sib=(c,y*2+(1-k)); yp=(c,(1-y)*2+k); xp=(z*2+(1-x),f)
+    zp=[(((z+d)%4)*2+x,f) for d in (1,2,3)]
+    bar=pltpu.get_barrier_semaphore()
+    for p in [sib,yp,xp]+zp:
+        pl.semaphore_signal(bar,inc=1,device_id=p,device_id_type=MESH)
+    pl.semaphore_wait(bar,6)
+    def remote(src,dst,ss,rs,dev):
+        return pltpu.make_async_remote_copy(src_ref=src,dst_ref=dst,send_sem=ss,recv_sem=rs,device_id=dev,device_id_type=MESH)
+    def cp_load(i,yy):
+        ii,slab,_,_,_,_=chunks[i]
+        return pltpu.make_async_copy(slab(ins[ii],yy*2+k),loc[i].at[yy],s_load.at[i,yy])
+    def cp_c(i,yy):
+        ii,slab,_,_,_,_=chunks[i]
+        return remote(slab(ins[ii],yy*2+(1-k)),rc[i].at[yy],c_s.at[i,yy],c_r.at[i,yy],sib)
+    def cp_y(i): return remote(loc[i].at[1-y],ry[i],y_s.at[i],y_r.at[i],yp)
+    def xhalf(i,xx):
+        w=chunks[i][5]//2
+        return pl.ds(pl.multiple_of(xx*w,128),w)
+    def zrows(i,zz):
+        r=chunks[i][4]//4
+        return pl.ds(pl.multiple_of(zz*r,r),r)
+    def cp_x(i): return remote(loc[i].at[y,:,xhalf(i,1-x)],rx[i],x_s.at[i],x_r.at[i],xp)
+    def cp_z(i,d): return remote(cb[i].at[zrows(i,(z+d)%4)],rz[i].at[d-1],z_s.at[i,d-1],z_r.at[i,d-1],zp[d-1])
+    def cp_g(i,d): return remote(res[i].at[x,zrows(i,z)],res[i].at[x,zrows(i,z)],g_s.at[i,d-1],g_r.at[i,d-1],zp[d-1])
+    def cp_g_in(i,d):
+        zz=(z+4-d)%4
+        return remote(res[i].at[x,zrows(i,zz)],res[i].at[x,zrows(i,zz)],g_s.at[i,d-1],g_r.at[i,d-1],zp[d-1])
+    def cp_h(i): return remote(res[i].at[x],res[i].at[x],h_s.at[i],h_r.at[i],xp)
+    def cp_h_in(i): return remote(res[i].at[1-x],res[i].at[1-x],h_s.at[i],h_r.at[i],xp)
+    def cp_out(i,xx):
+        _,_,oi,osl,r,w=chunks[i]
+        return pltpu.make_async_copy(res[i].at[xx],osl(outs[oi],xx),s_out.at[i,xx])
+    def start0(i):
+        for yy in (0,1):
+            cp_load(i,yy).start(); cp_c(i,yy).start()
+    def stage1(i):
+        for yy in (0,1):
+            cp_load(i,yy).wait(); cp_c(i,yy).wait()
+        r=chunks[i][4]
+        def go(s):
+            for yy in (0,1):
+                loc[i][yy,s]=(loc[i][yy,s].astype(F32)+rc[i][yy,s].astype(F32)).astype(BF)
+        add_strips(r,go)
+        cp_y(i).start()
+    def stage2(i):
+        cp_y(i).wait()
+        r=chunks[i][4]
+        def go(s):
+            loc[i][y,s]=(loc[i][y,s].astype(F32)+ry[i][s].astype(F32)).astype(BF)
+        add_strips(r,go)
+        cp_x(i).start()
+    def stage3(i):
+        cp_x(i).wait()
+        def go(s):
+            cb[i][s]=(loc[i][y,s,xhalf(i,x)].astype(F32)+rx[i][s].astype(F32)).astype(BF)
+        add_strips(chunks[i][4],go)
+        for d in (1,2,3): cp_z(i,d).start()
+    def stage4(i):
+        for d in (1,2,3): cp_z(i,d).wait()
+        r=chunks[i][4]//4
+        def go(j):
+            o=pl.multiple_of(z*r+j*16,16)
+            s=pl.ds(pl.multiple_of(j*16,16),16)
+            v=cb[i][pl.ds(o,16)].astype(F32)
+            for d in range(3): v=v+rz[i][d,s].astype(F32)
+            res[i][x,pl.ds(o,16)]=v.astype(BF)
+        pl.loop(0,r//16)(go)
+        for d in (1,2,3): cp_g(i,d).start()
+    def stage5(i):
+        for d in (1,2,3):
+            cp_g(i,d).wait_send(); cp_g_in(i,d).wait_recv()
+        cp_h(i).start()
+        cp_out(i,x).start()
+    def stage6(i):
+        cp_h(i).wait_send(); cp_h_in(i).wait_recv()
+        cp_out(i,1-x).start()
+    start0(0); start0(1)
+    stages=[stage1,stage2,stage3,stage4,stage5,stage6]
+    for t in range(n+5):
+        if t+2<n: start0(t+2)
+        for s,st in enumerate(stages):
+            if 0<=t-s<n: st(t-s)
+    for i in range(n):
+        for xx in (0,1): cp_out(i,xx).wait()
+
+def reduce_grads(gq,gk,gv,go,gin,gout,gvec,cid=1):
+    ins=[gq,gk,gv,go,gin,gout,gvec]
+    d=gq.shape[0]//4
+    w=gq.shape[1]
+    chunks=[]
+    fo=gout.shape[0]//4
+    for j in range(fo//d):
+        chunks.append((5,lambda r,f,j=j:r.at[pl.ds(pl.multiple_of(f*fo+j*d,d),d)],5,
+            lambda o,xx,j=j:o.at[pl.ds(j*d,d),pl.ds(pl.multiple_of(xx*(w//2),128),w//2)],d,w))
+    for j in range(gin.shape[1]//w):
+        chunks.append((4,lambda r,f,j=j:r.at[pl.ds(pl.multiple_of(f*d,d),d),pl.ds(j*w,w)],4,
+            lambda o,xx,j=j:o.at[:,pl.ds(pl.multiple_of(j*w+xx*(w//2),128),w//2)],d,w))
+    for m in (3,0,1,2):
+        chunks.append((m,lambda r,f:r.at[pl.ds(pl.multiple_of(f*d,d),d)],m,
+            lambda o,xx:o.at[:,pl.ds(pl.multiple_of(xx*(w//2),128),w//2)],d,w))
+    vr=gvec.shape[0]//4; vw=gvec.shape[1]
+    chunks.append((6,lambda r,f:r.at[pl.ds(pl.multiple_of(f*vr,vr),vr)],6,
+            lambda o,xx:o.at[:,pl.ds(pl.multiple_of(xx*(vw//2),128),vw//2)],vr,vw))
+    n=len(chunks)
+    scr=[]
+    scr+=[pltpu.VMEM((2,c[4],c[5]),BF) for c in chunks]
+    scr+=[pltpu.VMEM((2,c[4],c[5]),BF) for c in chunks]
+    scr+=[pltpu.VMEM((c[4],c[5]),BF) for c in chunks]
+    scr+=[pltpu.VMEM((c[4],c[5]//2),BF) for c in chunks]
+    scr+=[pltpu.VMEM((c[4],c[5]//2),BF) for c in chunks]
+    scr+=[pltpu.VMEM((3,c[4]//4,c[5]//2),BF) for c in chunks]
+    scr+=[pltpu.VMEM((2,c[4],c[5]//2),BF) for c in chunks]
+    D=pltpu.SemaphoreType.DMA
+    scr+=[D((n,2)),D((n,2)),D((n,2)),D((n,2)),D((n,)),D((n,)),D((n,)),D((n,)),D((n,3)),D((n,3)),D((n,3)),D((n,3)),D((n,)),D((n,))]
+    outs=[jax.ShapeDtypeStruct((a.shape[0]//4,a.shape[1]),BF) for a in ins]
+    return pl.pallas_call(functools.partial(reduce_kernel,chunks,7,7),out_shape=outs,
+        in_specs=[pl.BlockSpec(memory_space=pl.ANY)]*7,out_specs=[pl.BlockSpec(memory_space=pl.ANY)]*7,
+        scratch_shapes=scr,compiler_params=pltpu.CompilerParams(collective_id=cid,has_side_effects=True,vmem_limit_bytes=56*2**20),
+        cost_estimate=pl.CostEstimate(flops=10**7,bytes_accessed=2*10**8,transcendentals=0),name="grad_reduce")(*ins)
+
+
+def in_order(matrices, vectors, inner_bias):
+    return (
+        matrices[0],
+        matrices[1],
+        matrices[2],
+        matrices[3],
+        vectors[0],
+        vectors[1],
+        vectors[2],
+        vectors[3],
+        vectors[4],
+        matrices[4],
+        inner_bias,
+        matrices[5],
+        vectors[5],
+        vectors[6],
+        vectors[7],
+    )
+
+
+def reduce_plain(matrices, vectors, inner_bias):
+    out = []
+    for item in in_order(matrices, vectors, inner_bias):
+        share = lax.psum_scatter(item.astype(jnp.bfloat16), "fsdp", scatter_dimension=0, tiled=True)
+        out.append(lax.psum(share, "ctx").astype(jnp.float32))
+    return tuple(out)
+
+
+def reduce_fast(matrices, vectors, inner_bias):
+    width = vectors[0].shape[0]
+    stacked = jnp.transpose(jnp.stack(vectors).reshape(8, 4, width // 4), (1, 0, 2)).reshape(4, 2 * width)
+    packed = jnp.concatenate([stacked, inner_bias.reshape(4, -1)], axis=1)
+    used = packed.shape[1]
+    packed = jnp.pad(packed, ((0, 0), (0, 64 * 256 - used))).astype(jnp.bfloat16).reshape(256, 256)
+    done = reduce_grads(*[to_half(item) for item in matrices], packed)
+    done = [item.astype(jnp.float32) for item in done]
+    flat = done[6].reshape(-1)[:used]
+    rows = flat[: 2 * width].reshape(8, width // 4)
+    return in_order(done[:6], [rows[i] for i in range(8)], flat[2 * width :])
+
 
 def body(
+    fast,
     tokens,
     seq_lengths,
     deal,
@@ -353,70 +539,28 @@
             "te,de->td", grad_values_half, value_weight, preferred_element_type=jnp.float32
         )
     )
-    shares = (
-        lax.psum_scatter(
-            grad_query_weight.astype(jnp.bfloat16), "fsdp", scatter_dimension=0, tiled=True
-        ).astype(jnp.float32),
-        lax.psum_scatter(
-            grad_key_weight.astype(jnp.bfloat16), "fsdp", scatter_dimension=0, tiled=True
-        ).astype(jnp.float32),
-        lax.psum_scatter(
-            grad_value_weight.astype(jnp.bfloat16), "fsdp", scatter_dimension=0, tiled=True
-        ).astype(jnp.float32),
-        lax.psum_scatter(
-            grad_mix.astype(jnp.bfloat16), "fsdp", scatter_dimension=0, tiled=True
-        ).astype(jnp.float32),
-        lax.psum_scatter(
-            grad_query_bias.astype(jnp.bfloat16), "fsdp", scatter_dimension=0, tiled=True
-        ).astype(jnp.float32),
-        lax.psum_scatter(
-            grad_value_bias.astype(jnp.bfloat16), "fsdp", scatter_dimension=0, tiled=True
-        ).astype(jnp.float32),
-        lax.psum_scatter(
-            grad_mix_bias.astype(jnp.bfloat16), "fsdp", scatter_dimension=0, tiled=True
-        ).astype(jnp.float32),
-        lax.psum_scatter(
-            grad_gain_one.astype(jnp.bfloat16), "fsdp", scatter_dimension=0, tiled=True
-        ).astype(jnp.float32),
-        lax.psum_scatter(
-            grad_shift_one.astype(jnp.bfloat16), "fsdp", scatter_dimension=0, tiled=True
-        ).astype(jnp.float32),
-        lax.psum_scatter(
-            grad_inner.astype(jnp.bfloat16), "fsdp", scatter_dimension=0, tiled=True
-        ).astype(jnp.float32),
-        lax.psum_scatter(
-            grad_inner_bias.astype(jnp.bfloat16), "fsdp", scatter_dimension=0, tiled=True
-        ).astype(jnp.float32),
-        lax.psum_scatter(
-            grad_outer.astype(jnp.bfloat16), "fsdp", scatter_dimension=0, tiled=True
-        ).astype(jnp.float32),
-        lax.psum_scatter(
-            grad_outer_bias.astype(jnp.bfloat16), "fsdp", scatter_dimension=0, tiled=True
-        ).astype(jnp.float32),
-        lax.psum_scatter(
-            grad_gain_two.astype(jnp.bfloat16), "fsdp", scatter_dimension=0, tiled=True
-        ).astype(jnp.float32),
-        lax.psum_scatter(
-            grad_shift_two.astype(jnp.bfloat16), "fsdp", scatter_dimension=0, tiled=True
-        ).astype(jnp.float32),
-    )
-    summed = (
-        lax.psum(shares[0].astype(jnp.bfloat16), "ctx").astype(jnp.float32),
-        lax.psum(shares[1].astype(jnp.bfloat16), "ctx").astype(jnp.float32),
-        lax.psum(shares[2].astype(jnp.bfloat16), "ctx").astype(jnp.float32),
-        lax.psum(shares[3].astype(jnp.bfloat16), "ctx").astype(jnp.float32),
-        lax.psum(shares[4].astype(jnp.bfloat16), "ctx").astype(jnp.float32),
-        lax.psum(shares[5].astype(jnp.bfloat16), "ctx").astype(jnp.float32),
-        lax.psum(shares[6].astype(jnp.bfloat16), "ctx").astype(jnp.float32),
-        lax.psum(shares[7].astype(jnp.bfloat16), "ctx").astype(jnp.float32),
-        lax.psum(shares[8].astype(jnp.bfloat16), "ctx").astype(jnp.float32),
-        lax.psum(shares[9].astype(jnp.bfloat16), "ctx").astype(jnp.float32),
-        lax.psum(shares[10].astype(jnp.bfloat16), "ctx").astype(jnp.float32),
-        lax.psum(shares[11].astype(jnp.bfloat16), "ctx").astype(jnp.float32),
-        lax.psum(shares[12].astype(jnp.bfloat16), "ctx").astype(jnp.float32),
-        lax.psum(shares[13].astype(jnp.bfloat16), "ctx").astype(jnp.float32),
-        lax.psum(shares[14].astype(jnp.bfloat16), "ctx").astype(jnp.float32),
-    )
+    matrices = (
+        grad_query_weight,
+        grad_key_weight,
+        grad_value_weight,
+        grad_mix,
+        grad_inner,
+        grad_outer,
+    )
+    vectors = (
+        grad_query_bias,
+        grad_value_bias,
+        grad_mix_bias,
+        grad_gain_one,
+        grad_shift_one,
+        grad_outer_bias,
+        grad_gain_two,
+        grad_shift_two,
+    )
+    if fast:
+        summed = reduce_fast(matrices, vectors, grad_inner_bias)
+    else:
+        summed = reduce_plain(matrices, vectors, grad_inner_bias)
     return (
         layer_out.astype(jnp.bfloat16)[None],
         grad_inputs[None],
@@ -460,8 +604,9 @@
         P("fsdp"),
         P("fsdp", "ctx", None),
     )
+    fast = dict(mesh.shape) == {"ctx": 8, "fsdp": 4}
     return jax.shard_map(
-        body,
+        functools.partial(body, fast),
         mesh=mesh,
         in_specs=placed,
         out_specs=(

time: 1010 us -> 759 us (0.75)
  waiting for transfers between devices: 605 us -> 294 us
  Pallas kernels: 0 us -> 110 us
  blocking collectives: 50.6 us -> 16.1 us
  local copies, waits for them, and re-layouts: 122 us -> 108 us
    reduce_scatter x3 -> x0, waiting for transfers between devices: 127 us -> none  [the longest x1 50.5 us: body(): lax.psum_scatter(grad_outer.astype(jnp.bfloat16), 'fsdp', scatter_dimensi...]
    pallas_call x0 -> x1, Pallas kernels: none -> 110 us  [reduce_grads(): pl.pallas_call(functools.partial(reduce_kernel, chunks, 7, 7), out_shape=...]
    psum x1 -> x0, waiting for transfers between devices: 104 us -> none  [body(): lax.psum(shares[0].astype(jnp.bfloat16), 'ctx').astype(jnp.float32)]
    unnamed x20 -> x10, waiting for transfers between devices: 65.4 us -> 0.16 us
    psum x1 -> x0, blocking collectives: 23.2 us -> none  [body(): lax.psum(shares[4].astype(jnp.bfloat16), 'ctx').astype(jnp.float32)]
    reduce_scatter x1, waiting for transfers between devices: 74.6 us -> 54.6 us  [body(): lax.psum_scatter(grad_values_all.astype(jnp.bfloat16), 'ctx', scatter_dim...]
    unnamed x180 -> x165, local copies, waits for them, and re-layouts: 32.1 us -> 13.9 us
    unnamed x2 -> x1, blocking collectives: 22 us -> 10.8 us
  transfers between devices with their start and end apart: 17 -> 10, of which waited for: 15 -> 8; matrix products, arithmetic and copies ran while one was open for 14% -> 15% of each run, Pallas kernels for 0% -> 0%
where the time goes in v1:
time: 759 us; the launch traced here: 753 us
  waiting for transfers between devices  294 us (39%)
  matrix products  120 us (16%)
  Pallas kernels  110 us (14%)
  local copies, waits for them, and re-layouts  108 us (14%)
  other arithmetic  80.5 us (11%)
  blocking collectives  16.1 us (2%)
  between operations  16.1 us (2%)
  loops' own time  8.44 us (1%)
    pallas_call x1, Pallas kernels, reduce_grads(): pl.pallas_call(functools.partial(reduce_kernel, chunks, 7, 7), out_shape=...  110 us
    reduce_scatter x1, waiting for transfers between devices, body(): lax.psum_scatter(grad_keys_all.astype(jnp.bfloat16), 'ctx', scatter_dimen...  72.9 us
    all_gather x1, waiting for transfers between devices, body(): lax.all_gather(keys, 'ctx', axis=0, tiled=True)  61.2 us
    dynamic_update_slice x4, local copies, waits for them, and re-layouts, add_rows(): return lax.dynamic_update_slice_in_dim(total, current + term, at_row, 0)  59.1 us
    all_gather x1, waiting for transfers between devices, body(): lax.all_gather(values, 'ctx', axis=0, tiled=True)  56.9 us
    reduce_scatter x1, waiting for transfers between devices, body(): lax.psum_scatter(grad_values_all.astype(jnp.bfloat16), 'ctx', scatter_dim...  54.6 us
    all_gather x1, waiting for transfers between devices, body(): lax.all_gather(to_half(w_out), 'fsdp', axis=0, tiled=True)  26.7 us
    dot_general x2, matrix products, one_block(): jnp.einsum('hqk,qhd->khd', probs.astype(jnp.bfloat16), grad_heads, prefer...  18.8 us
  transfers between devices with their start and end apart: 10, of which 8 were waited for; matrix products, arithmetic and copies ran while one was open for 15% of the time, Pallas kernels for 0%

profile of v1, /device:TPU:0, one launch (start us, length us, event | category | flops | bytes accessed | tf_op | source)
XLA Modules:
  0.0 752.7 jit_solution(10133952931512511204)
XLA Ops:
  13.2 17.3 %all-gather.10.cloned.1.call-done = bf16[768,768]{1,0:T(8,128)(2,1)} async-done(((bf16[192,768]{1,0:T(8,128)(2,1)}), bf16[768,768]{1,0:T(8,128)(2,1)}) %all-gather.10.cloned.1.call-update) | async-done | bytes 1179664 | tf_op jit(solution)/shard_map/all_gather | solution.py:376
  36.1 10.8 %all-reduce.9 = (bf16[768]{0:T(1024)(128)(2,1)S(1)}, bf16[768]{0:T(1024)(128)(2,1)S(1)}, bf16[768]{0:T(1024)(128)(2,1)S(1)}, bf16[768]{0:T(1024)(128)(2,1)S(1)},...) all-reduce(bf16[768]{0:T(1024)(128)(2,1)S(1)} %dynamic-update-slice, ...), channel_id=1, replica_groups=mesh['ctx'=8,'fsdp'=4] {'fsdp'}, use_global_device_ids=true, to_apply=%add.1 | all-reduce | flops 6144 | bytes 24576
  46.9 3.3 all-gather.16.cloned.1.call-done
  53.6 2.8 convert_element_type.237
  56.5 2.8 convert_element_type.241
  60.1 5.4 all-gather
  71.9 61.2 %all-gather.12.cloned.1.call-done = bf16[2048,768]{1,0:T(8,128)(2,1)} async-done(((bf16[256,768]{1,0:T(8,128)(2,1)}), bf16[2048,768]{1,0:T(8,128)(2,1)}) %all-gather.12.cloned.1.call-update) | async-done | bytes 3145744 | tf_op jit(solution)/shard_map/all_gather | solution.py:436
  133.0 4.8 copy.96
  137.8 56.9 %all-gather.18.cloned.1.call-done = bf16[2048,768]{1,0:T(8,128)(2,1)} async-done(((bf16[256,768]{1,0:T(8,128)(2,1)}), bf16[2048,768]{1,0:T(8,128)(2,1)}) %all-gather.18.cloned.1.call-update) | async-done | bytes 3145744 | tf_op jit(solution)/shard_map/all_gather | solution.py:437
  194.8 4.8 copy.97
  199.5 49.0 %while.30 = (s32[]{:T(128)}, f32[12,256]{1,0:T(8,128)S(1)}, f32[12,256]{1,0:T(8,128)S(1)}, f32[256,12,64]{0,2,1:T(8,128)S(1)}, s32[256]{0:T(256)S(1)}, /*index=5...) while((s32[]{:T(128)}, f32[12,256]{1,0:T(8,128)S(1)}, ...), condition=%wide.region_7.8_spmd.clone, body=%wide.region_4.7_spmd.clone.sunk | while | flops 840779776 | bytes 100742368 | solution.py:119
  202.4 3.7 constant_dynamic-slice_fusion.7
  206.0 6.7 fusion.148
  212.8 7.2 fusion.150
  221.0 3.1 fusion.152
  227.0 3.4 constant_dynamic-slice_fusion.7
  230.4 6.7 fusion.148
  237.1 7.3 fusion.150
  245.4 3.1 fusion.152
  253.0 11.8 %multiply_convert_fusion = (bf16[256,3072]{1,0:T(8,128)(2,1)S(1)}, f32[256,3072]{1,0:T(8,128)}, f32[256,3072]{1,0:T(8,128)}) fusion(f32[3072]{0:T(1024)S(1)} %bitcast.224, bf16[768,3072]{1,0:T(8,128)(2,1)} %all-gather.22.cloned.1.call-done, f32[256,768]{1,0:T(8,128)S(1)} %get-tuple-element.439, f32[768]{0:T(1024)S(1)} %copy-done.36, ...), kind=kOutput, calls=%fused_computation.45 | convolution fusion | flops 1260847104 | bytes 13389824 | tf_op jit(solution)/shard_map/dot_general | solution.py:452
  264.8 26.7 %all-gather.24.cloned.1.call-done = bf16[3072,768]{1,0:T(8,128)(2,1)} async-done(((bf16[768,768]{1,0:T(8,128)(2,1)}), bf16[3072,768]{1,0:T(8,128)(2,1)}) %all-gather.24.cloned.1.call-update) | async-done | bytes 4718608 | tf_op jit(solution)/shard_map/all_gather | solution.py:386
  291.6 4.0 fusion.80
  308.5 3.4 broadcast.243
  311.9 3.5 broadcast.243.clone
  315.4 142.5 %while.31 = (s32[]{:T(128)}, f32[256,12,64]{0,2,1:T(8,128)}, f32[2048,768]{0,1:T(8,128)}, f32[2048,768]{0,1:T(8,128)}, s32[2]{0:T(128)S(1)}, /*index=5*/bf16[204...) while((s32[]{:T(128)}, f32[256,12,64]{0,2,1:T(8,128)}, ...), condition=%wide.region_17.18_spmd.clone, body=%wide.region_16.17_spmd.clone.sunk | while | flops 2047934464 | bytes 192349648 | solution.py:167
  323.4 3.5 constant_dynamic-slice_fusion.9
  327.0 7.1 fusion.164
  334.0 5.0 fusion.165
  339.0 9.4 %fusion.166 = f32[12,1024,64]{1,2,0:T(8,128)} fusion(bf16[256,12,64]{0,2,1:T(8,128)(2,1)} %get-tuple-element.686, f32[12,1024,256]{2,1,0:T(8,128)} %copy-done.1, f32[12,256]{1,0:T(8,128)S(1)} %copy-done.45, pred[256,1024]{0,1:T(8,128)(4,1)S(1)} %copy-done.9), kind=kOutput, calls=%fused_computation.26.clone.1 | convolution fusion | flops 415236096 | bytes 16396288 | tf_op jit(solution)/shard_map/while/body/eval_jaxpr/hqk,qhd->khd/dot_general | solution.py:155
  350.5 6.7 bitcast_add_fusion.3
  357.2 15.6 %dynamic_update_slice.10 = f32[2048,768]{0,1:T(8,128)} dynamic-update-slice(f32[2048,768]{0,1:T(8,128)} %get-tuple-element.661, f32[1024,768]{0,1:T(8,128)} %get-tuple-element.602, s32[]{:T(128)S(6)} %select_n.88, s32[]{:T(128)} %constant.74.clone.1..sunk.1) | dynamic-update-slice | bytes 6291460 | tf_op jit(solution)/shard_map/while/body/eval_jaxpr/dynamic_update_slice | solution.py:56
  372.8 14.9 %dynamic_update_slice.11 = f32[2048,768]{0,1:T(8,128)} dynamic-update-slice(f32[2048,768]{0,1:T(8,128)} %get-tuple-element.662, f32[1024,768]{0,1:T(8,128)S(1)} %get-tuple-element.603, s32[]{:T(128)S(6)} %select_n.88, s32[]{:T(128)} %constant.74.clone.1..sunk.1) | dynamic-update-slice | bytes 6291460 | tf_op jit(solution)/shard_map/while/body/eval_jaxpr/dynamic_update_slice | solution.py:56
  395.5 3.3 constant_dynamic-slice_fusion.9
  398.8 7.2 fusion.164
  406.0 5.1 fusion.165
  411.2 9.4 %fusion.166 = f32[12,1024,64]{1,2,0:T(8,128)} fusion(bf16[256,12,64]{0,2,1:T(8,128)(2,1)} %get-tuple-element.686, f32[12,1024,256]{2,1,0:T(8,128)} %copy-done.1, f32[12,256]{1,0:T(8,128)S(1)} %copy-done.45, pred[256,1024]{0,1:T(8,128)(4,1)S(1)} %copy-done.9), kind=kOutput, calls=%fused_computation.26.clone.1 | convolution fusion | flops 415236096 | bytes 16396288 | tf_op jit(solution)/shard_map/while/body/eval_jaxpr/hqk,qhd->khd/dot_general | solution.py:155
  422.6 6.5 bitcast_add_fusion.3
  429.1 14.8 %dynamic_update_slice.10 = f32[2048,768]{0,1:T(8,128)} dynamic-update-slice(f32[2048,768]{0,1:T(8,128)} %get-tuple-element.661, f32[1024,768]{0,1:T(8,128)} %get-tuple-element.602, s32[]{:T(128)S(6)} %select_n.88, s32[]{:T(128)} %constant.74.clone.1..sunk.1) | dynamic-update-slice | bytes 6291460 | tf_op jit(solution)/shard_map/while/body/eval_jaxpr/dynamic_update_slice | solution.py:56
  443.9 13.8 %dynamic_update_slice.11 = f32[2048,768]{0,1:T(8,128)} dynamic-update-slice(f32[2048,768]{0,1:T(8,128)} %get-tuple-element.662, f32[1024,768]{0,1:T(8,128)S(1)} %get-tuple-element.603, s32[]{:T(128)S(6)} %select_n.88, s32[]{:T(128)} %constant.74.clone.1..sunk.1) | dynamic-update-slice | bytes 6291460 | tf_op jit(solution)/shard_map/while/body/eval_jaxpr/dynamic_update_slice | solution.py:56
  457.9 5.0 convert_element_type.258
  463.0 5.0 convert_element_type.257
  476.0 3.6 convolution_convert_fusion.refs_5_
  479.7 3.7 convolution_convert_fusion.1.refs_4_
  483.4 54.6 %reduce-scatter.5.cloned.1.call-done = bf16[256,768]{0,1:T(8,128)(2,1)} async-done(((bf16[2048,768]{0,1:T(8,128)(2,1)}), bf16[256,768]{0,1:T(8,128)(2,1)}) %reduce-scatter.5.cloned.1.call-update) | async-done | bytes 393232 | tf_op jit(solution)/shard_map/reduce_scatter | solution.py:516
  542.7 72.9 %reduce-scatter.3.cloned.1.call-done = bf16[256,768]{0,1:T(8,128)(2,1)} async-done(((bf16[2048,768]{0,1:T(8,128)(2,1)}), bf16[256,768]{0,1:T(8,128)(2,1)}) %reduce-scatter.3.cloned.1.call-update) | async-done | bytes 393232 | tf_op jit(solution)/shard_map/reduce_scatter | solution.py:513
  618.1 109.6 %grad_reduce.1 = (bf16[192,768]{1,0:T(8,128)(2,1)}, bf16[192,768]{1,0:T(8,128)(2,1)}, bf16[192,768]{1,0:T(8,128)(2,1)}, bf16[192,768]{1,0:T(8,128)(2,1)}, bf16[1...) custom-call(bf16[768,768]{1,0:T(8,128)(2,1)} %fusion.33.refs_0_, ...), custom_call_target="tpu_custom_call" | custom-call | flops 10000000 | bytes 200000000 | tf_op jit(solution)/shard_map/grad_reduce/pallas_call | solution.py:305
  737.0 3.1 convert_element_type.278
  740.7 3.0 convert_element_type.279
  (343 shorter events, 84.7 us)
Async XLA Ops:
  7.2 26.0 %copy-start.69 = (u32[32]{0:T(128)S(1)}, u32[32]{0:T(128)}, u32[]{:S(2)}) copy-start(u32[32]{0:T(128)} %constant.169) | copy-start | bytes 388
  7.2 23.3 %copy-start.7 = (bf16[1,256,768]{2,1,0:T(8,128)(2,1)S(1)}, bf16[1,256,768]{2,1,0:T(8,128)(2,1)}, u32[]{:S(2)}) copy-start(bf16[1,256,768]{2,1,0:T(8,128)(2,1)} %param.23) | copy-start | bytes 1179652
  7.2 25.8 %copy-start.58 = (f32[192]{0:T(256)S(1)}, f32[192]{0:T(256)}, u32[]{:S(2)}) copy-start(f32[192]{0:T(256)} %param.30) | copy-start | bytes 2308
  7.2 25.8 %copy-start.59 = (f32[192]{0:T(256)S(1)}, f32[192]{0:T(256)}, u32[]{:S(2)}) copy-start(f32[192]{0:T(256)} %param.31) | copy-start | bytes 2308
  7.2 25.8 %copy-start.60 = (f32[192]{0:T(256)S(1)}, f32[192]{0:T(256)}, u32[]{:S(2)}) copy-start(f32[192]{0:T(256)} %param.32) | copy-start | bytes 2308
  7.2 25.9 %copy-start.61 = (f32[192]{0:T(256)S(1)}, f32[192]{0:T(256)}, u32[]{:S(2)}) copy-start(f32[192]{0:T(256)} %param.34) | copy-start | bytes 2308
  7.3 25.9 %copy-start.62 = (f32[192]{0:T(256)S(1)}, f32[192]{0:T(256)}, u32[]{:S(2)}) copy-start(f32[192]{0:T(256)} %param.33) | copy-start | bytes 2308
  7.3 25.9 %copy-start.63 = (f32[192]{0:T(256)S(1)}, f32[192]{0:T(256)}, u32[]{:S(2)}) copy-start(f32[192]{0:T(256)} %param.38) | copy-start | bytes 2308
  7.3 25.9 %copy-start.64 = (f32[192]{0:T(256)S(1)}, f32[192]{0:T(256)}, u32[]{:S(2)}) copy-start(f32[192]{0:T(256)} %param.40) | copy-start | bytes 2308
  7.3 25.9 %copy-start.65 = (f32[192]{0:T(256)S(1)}, f32[192]{0:T(256)}, u32[]{:S(2)}) copy-start(f32[192]{0:T(256)} %param.39) | copy-start | bytes 2308
  7.3 23.2 %all-gather.10.cloned.1.call-start = ((), (), s32[]{:S(2)}) async-start(), calls=%async_computation.2 | async-start | bytes 1474560 | tf_op jit(solution)/shard_map/all_gather | solution.py:376
  9.3 40.9 %all-gather.16.cloned.1.call-start = ((), (), s32[]{:S(2)}) async-start(), calls=%async_computation.5 | async-start | bytes 1474560 | tf_op jit(solution)/shard_map/all_gather | solution.py:377
  11.2 41.6 %copy-start.28 = (f32[192,768]{1,0:T(8,128)S(1)}, f32[192,768]{1,0:T(8,128)}, u32[]{:S(2)}) copy-start(f32[192,768]{1,0:T(8,128)} %param.29) | copy-start | bytes 1769476
  11.2 58.8 %all-gather.14.cloned.1.call-start = ((), (), s32[]{:S(2)}) async-start(), calls=%async_computation.4 | async-start | bytes 1474560 | tf_op jit(solution)/shard_map/all_gather | solution.py:375
  13.1 119.9 %all-gather.12.cloned.1.call-start = ((), (), s32[]{:S(2)}) async-start(), calls=%async_computation.3 | async-start | bytes 3538944 | tf_op jit(solution)/shard_map/all_gather | solution.py:436
  33.0 161.8 %all-gather.18.cloned.1.call-start = ((), (), s32[]{:S(2)}) async-start(), calls=%async_computation.6 | async-start | bytes 3538944 | tf_op jit(solution)/shard_map/all_gather | solution.py:437
  52.7 197.9 %all-gather.20.cloned.1.call-start = ((), (), s32[]{:S(2)}) async-start(), calls=%async_computation.7 | async-start | bytes 1474560 | tf_op jit(solution)/shard_map/all_gather | solution.py:378
  53.6 199.3 %all-gather.22.cloned.1.call-start = ((), (), s32[]{:S(2)}) async-start(), calls=%async_computation.8 | async-start | bytes 5898240 | tf_op jit(solution)/shard_map/all_gather | solution.py:384
  56.5 9.7 %copy-start.66 = (s32[1,16]{1,0:T(1,128)S(1)}, s32[1,16]{1,0:T(1,128)}, u32[]{:S(2)}) copy-start(s32[1,16]{1,0:T(1,128)} %param.25) | copy-start | bytes 196
  56.5 235.1 %all-gather.24.cloned.1.call-start = ((), (), s32[]{:S(2)}) async-start(), calls=%async_computation.9 | async-start | bytes 5898240 | tf_op jit(solution)/shard_map/all_gather | solution.py:386
  59.4 478.6 %reduce-scatter.5.cloned.1.call-start = ((), (), s32[]{:S(2)}) async-start(), calls=%async_computation.11 | async-start | bytes 3538944 | tf_op jit(solution)/shard_map/reduce_scatter | solution.py:516
  212.8 8.2 %copy-start = (f32[12,1024,256]{2,1,0:T(8,128)S(1)}, f32[12,1024,256]{2,1,0:T(8,128)}, u32[]{:S(2)}) copy-start(f32[12,1024,256]{2,1,0:T(8,128)} %get-tuple-element.586) | copy-start | bytes 37748740 | tf_op jit(solution)/shard_map/while
  237.1 8.3 %copy-start = (f32[12,1024,256]{2,1,0:T(8,128)S(1)}, f32[12,1024,256]{2,1,0:T(8,128)}, u32[]{:S(2)}) copy-start(f32[12,1024,256]{2,1,0:T(8,128)} %get-tuple-element.586) | copy-start | bytes 37748740 | tf_op jit(solution)/shard_map/while
  252.6 51.6 %copy-start.3 = (f32[256,768]{1,0:T(8,128)}, f32[256,768]{1,0:T(8,128)S(1)}, u32[]{:S(2)}) copy-start(f32[256,768]{1,0:T(8,128)S(1)} %get-tuple-element.439) | copy-start | bytes 2359300
  252.6 12.2 %copy-start.39 = (f32[256]{0:T(256)}, f32[256]{0:T(256)S(1)}, u32[]{:S(2)}) copy-start(f32[256]{0:T(256)S(1)} %broadcast_multiply_fusion.5) | copy-start | bytes 3076
  252.9 11.9 %copy-start.46 = (f32[256]{0:T(256)}, f32[256]{0:T(256)S(1)}, u32[]{:S(2)}) copy-start(f32[256]{0:T(256)S(1)} %add_rsqrt_fusion.1) | copy-start | bytes 3076
  264.8 30.8 %copy-start.12 = (bf16[256,3072]{1,0:T(8,128)(2,1)}, bf16[256,3072]{1,0:T(8,128)(2,1)S(1)}, u32[]{:S(2)}) copy-start(bf16[256,3072]{1,0:T(8,128)(2,1)S(1)} %get-tuple-element.421) | copy-start | bytes 4718596
  291.5 6.9 slice-start.4
  291.6 6.9 slice-start.5
  291.6 6.9 copy-start.71
  305.1 6.8 copy-start.5
  322.1 11.9 %copy-start.1 = (f32[12,1024,256]{2,1,0:T(8,128)}, f32[12,1024,256]{2,1,0:T(8,128)S(1)}, u32[]{:S(2)}) copy-start(f32[12,1024,256]{2,1,0:T(8,128)S(1)} %fusion.163) | copy-start | bytes 37748740 | tf_op jit(solution)/shard_map/while
  322.1 4.8 copy-start.42
  322.1 4.8 copy-start.44
  334.0 5.0 copy-start.9
  334.0 5.0 copy-start.45
  334.0 14.4 %slice-start = ((s8[6291456]{0:T(1024)(128)(4,1)}), s8[4194304]{0:T(1024)(128)(4,1)S(1)}, s32[]{:S(2)}) async-start(s8[6291456]{0:T(1024)(128)(4,1)} %bitcast.209), calls=%async_computation.12 | async-start | bytes 8388608 | tf_op jit(solution)/shard_map/while
  339.0 9.4 %slice-start.1 = ((s8[6291456]{0:T(1024)(128)(4,1)}), s8[2097152]{0:T(1024)(128)(4,1)S(1)}, s32[]{:S(2)}) async-start(s8[6291456]{0:T(1024)(128)(4,1)} %bitcast.209), calls=%async_computation.13 | async-start | bytes 4194304 | tf_op jit(solution)/shard_map/while
  394.1 11.9 %copy-start.1 = (f32[12,1024,256]{2,1,0:T(8,128)}, f32[12,1024,256]{2,1,0:T(8,128)S(1)}, u32[]{:S(2)}) copy-start(f32[12,1024,256]{2,1,0:T(8,128)S(1)} %fusion.163) | copy-start | bytes 37748740 | tf_op jit(solution)/shard_map/while
  394.1 4.6 copy-start.42
  394.2 4.6 copy-start.44
  406.0 5.2 copy-start.9
  406.0 5.2 copy-start.45
  406.0 14.6 %slice-start = ((s8[6291456]{0:T(1024)(128)(4,1)}), s8[4194304]{0:T(1024)(128)(4,1)S(1)}, s32[]{:S(2)}) async-start(s8[6291456]{0:T(1024)(128)(4,1)} %bitcast.209), calls=%async_computation.12 | async-start | bytes 8388608 | tf_op jit(solution)/shard_map/while
  411.2 9.4 %slice-start.1 = ((s8[6291456]{0:T(1024)(128)(4,1)}), s8[2097152]{0:T(1024)(128)(4,1)S(1)}, s32[]{:S(2)}) async-start(s8[6291456]{0:T(1024)(128)(4,1)} %bitcast.209), calls=%async_computation.13 | async-start | bytes 4194304 | tf_op jit(solution)/shard_map/while
  463.0 152.6 %reduce-scatter.3.cloned.1.call-start = ((), (), s32[]{:S(2)}) async-start(), calls=%async_computation.10 | async-start | bytes 3538944 | tf_op jit(solution)/shard_map/reduce_scatter | solution.py:513
  737.0 6.6 copy-start.10
  737.0 6.6 copy-start.22
  (49 other events, 161.0 us)
Sparse Core Ops, SparseCore 0:
  10.3 20.1 all-gather.9
  32.6 17.5 all-gather.15
  52.4 17.5 all-gather.13
  72.6 60.4 all-gather.11
  135.7 59.0 all-gather.17
  196.7 16.0 all-gather.19
  215.0 37.4 all-gather.21
  254.1 37.4 all-gather.23
  463.1 74.8 reduce-scatter.4
  541.4 74.1 reduce-scatter.2

commit v2 on v0

--- a/solution.py
+++ b/solution.py
@@ -1,6 +1,10 @@
+import functools
+
 import jax
 import jax.numpy as jnp
 from jax import lax
+from jax.experimental import pallas as pl
+from jax.experimental.pallas import tpu as pltpu
 from jax.sharding import PartitionSpec as P
 
 HEADS = 12
@@ -438,6 +442,988 @@
     )
 
 
+MESH=pl.DeviceIdType.MESH
+F32=jnp.float32; BF=jnp.bfloat16
+
+def places():
+    c=lax.axis_index("ctx"); f=lax.axis_index("fsdp")
+    z=c//2; x=c%2; y=f//2; k=f%2
+    return c,f,z,x,y,k
+
+def add_strips(rows, fn, step=16):
+    @pl.loop(0, rows//step)
+    def _(i):
+        fn(pl.ds(pl.multiple_of(i*step,step),step))
+
+def reduce_kernel(chunks, n_in, n_out, *refs):
+    n=len(chunks)
+    ins=refs[:n_in]; outs=refs[n_in:n_in+n_out]
+    scr=refs[n_in+n_out:]
+    loc=scr[0:n]; rc=scr[n:2*n]; ry=scr[2*n:3*n]; rx=scr[3*n:4*n]; cb=scr[4*n:5*n]; rz=scr[5*n:6*n]; res=scr[6*n:7*n]
+    (s_load,s_out,c_s,c_r,y_s,y_r,x_s,x_r,z_s,z_r,g_s,g_r,h_s,h_r)=scr[7*n:]
+    c,f,z,x,y,k=places()
+    sib=(c,y*2+(1-k)); yp=(c,(1-y)*2+k); xp=(z*2+(1-x),f)
+    zp=[(((z+d)%4)*2+x,f) for d in (1,2,3)]
+    bar=pltpu.get_barrier_semaphore()
+    for p in [sib,yp,xp]+zp:
+        pl.semaphore_signal(bar,inc=1,device_id=p,device_id_type=MESH)
+    pl.semaphore_wait(bar,6)
+    def remote(src,dst,ss,rs,dev):
+        return pltpu.make_async_remote_copy(src_ref=src,dst_ref=dst,send_sem=ss,recv_sem=rs,device_id=dev,device_id_type=MESH)
+    def cp_load(i,yy):
+        ii,slab,_,_,_,_=chunks[i]
+        return pltpu.make_async_copy(slab(ins[ii],yy*2+k),loc[i].at[yy],s_load.at[i,yy])
+    def cp_c(i,yy):
+        ii,slab,_,_,_,_=chunks[i]
+        return remote(slab(ins[ii],yy*2+(1-k)),rc[i].at[yy],c_s.at[i,yy],c_r.at[i,yy],sib)
+    def cp_y(i): return remote(loc[i].at[1-y],ry[i],y_s.at[i],y_r.at[i],yp)
+    def xhalf(i,xx):
+        w=chunks[i][5]//2
+        return pl.ds(pl.multiple_of(xx*w,128),w)
+    def zrows(i,zz):
+        r=chunks[i][4]//4
+        return pl.ds(pl.multiple_of(zz*r,r),r)
+    def cp_x(i): return remote(loc[i].at[y,:,xhalf(i,1-x)],rx[i],x_s.at[i],x_r.at[i],xp)
+    def cp_z(i,d): return remote(cb[i].at[zrows(i,(z+d)%4)],rz[i].at[d-1],z_s.at[i,d-1],z_r.at[i,d-1],zp[d-1])
+    def cp_g(i,d): return remote(res[i].at[x,zrows(i,z)],res[i].at[x,zrows(i,z)],g_s.at[i,d-1],g_r.at[i,d-1],zp[d-1])
+    def cp_g_in(i,d):
+        zz=(z+4-d)%4
+        return remote(res[i].at[x,zrows(i,zz)],res[i].at[x,zrows(i,zz)],g_s.at[i,d-1],g_r.at[i,d-1],zp[d-1])
+    def cp_h(i): return remote(res[i].at[x],res[i].at[x],h_s.at[i],h_r.at[i],xp)
+    def cp_h_in(i): return remote(res[i].at[1-x],res[i].at[1-x],h_s.at[i],h_r.at[i],xp)
+    def cp_out(i,xx):
+        _,_,oi,osl,r,w=chunks[i]
+        return pltpu.make_async_copy(res[i].at[xx],osl(outs[oi],xx),s_out.at[i,xx])
+    def start0(i):
+        for yy in (0,1):
+            cp_load(i,yy).start(); cp_c(i,yy).start()
+    def stage1(i):
+        for yy in (0,1):
+            cp_load(i,yy).wait(); cp_c(i,yy).wait()
+        r=chunks[i][4]
+        def go(s):
+            for yy in (0,1):
+                loc[i][yy,s]=(loc[i][yy,s].astype(F32)+rc[i][yy,s].astype(F32)).astype(BF)
+        add_strips(r,go)
+        cp_y(i).start()
+    def stage2(i):
+        cp_y(i).wait()
+        r=chunks[i][4]
+        def go(s):
+            loc[i][y,s]=(loc[i][y,s].astype(F32)+ry[i][s].astype(F32)).astype(BF)
+        add_strips(r,go)
+        cp_x(i).start()
+    def stage3(i):
+        cp_x(i).wait()
+        def go(s):
+            cb[i][s]=(loc[i][y,s,xhalf(i,x)].astype(F32)+rx[i][s].astype(F32)).astype(BF)
+        add_strips(chunks[i][4],go)
+        for d in (1,2,3): cp_z(i,d).start()
+    def stage4(i):
+        for d in (1,2,3): cp_z(i,d).wait()
+        r=chunks[i][4]//4
+        def go(j):
+            o=pl.multiple_of(z*r+j*16,16)
+            s=pl.ds(pl.multiple_of(j*16,16),16)
+            v=cb[i][pl.ds(o,16)].astype(F32)
+            for d in range(3): v=v+rz[i][d,s].astype(F32)
+            res[i][x,pl.ds(o,16)]=v.astype(BF)
+        pl.loop(0,r//16)(go)
+        for d in (1,2,3): cp_g(i,d).start()
+    def stage5(i):
+        for d in (1,2,3):
+            cp_g(i,d).wait_send(); cp_g_in(i,d).wait_recv()
+        cp_h(i).start()
+        cp_out(i,x).start()
+    def stage6(i):
+        cp_h(i).wait_send(); cp_h_in(i).wait_recv()
+        cp_out(i,1-x).start()
+    start0(0); start0(1)
+    stages=[stage1,stage2,stage3,stage4,stage5,stage6]
+    for t in range(n+5):
+        if t+2<n: start0(t+2)
+        for s,st in enumerate(stages):
+            if 0<=t-s<n: st(t-s)
+    for i in range(n):
+        for xx in (0,1): cp_out(i,xx).wait()
+
+
+def remote_copy(src, dst, send, recv, device):
+    return pltpu.make_async_remote_copy(
+        src_ref=src,
+        dst_ref=dst,
+        send_sem=send,
+        recv_sem=recv,
+        device_id=device,
+        device_id_type=MESH,
+    )
+
+
+def greet(peers):
+    barrier = pltpu.get_barrier_semaphore()
+    for peer in peers:
+        pl.semaphore_signal(barrier, inc=1, device_id=peer, device_id_type=MESH)
+    pl.semaphore_wait(barrier, len(peers))
+
+
+def at_row(value, size):
+    return pl.ds(pl.multiple_of(value, 16), size)
+
+
+def window_start(part):
+    return 192 * part - 64 * (part % 2)
+
+
+def lane_windows(parts):
+    first, second, third, fourth = parts
+    return jnp.concatenate(
+        [
+            first[:, :128],
+            first[:, 128:] + second[:, :128],
+            second[:, 128:],
+            third[:, :128],
+            third[:, 128:] + fourth[:, :128],
+            fourth[:, 128:],
+        ],
+        axis=1,
+    )
+
+
+GATHER_PIECES = ((True, 3), (True, 3), (False, 1), (True, 2), (False, 4))
+
+
+def gather_project_kernel(*refs):
+    (tok, wq_s, wkv_s, wo_s, win_s, wout_s, vec_s) = refs[:7]
+    (qg, kvg, wq_o, wkv_o, wo_o, win_o, wout_o, vec_o) = refs[7:15]
+    (wq_v, wkv_v, vec_v, send_kv, send_q) = refs[15:20]
+    (own_s, own_r, own_l, y_s, y_r, cy_s, cy_r, x_s, x_r, cx_s, cx_r) = refs[20:31]
+    (v_s, v_r, v_l, zk_s, zk_r, zq_s, zq_r, f_s, f_r, l_sem, out_sem) = refs[31:]
+    c, f, z, x, y, k = places()
+    sib = (c, y * 2 + (1 - k))
+    yp = (c, (1 - y) * 2 + k)
+    diag = (c, (1 - y) * 2 + (1 - k))
+    xp = (z * 2 + (1 - x), f)
+    zt = [(z + d) % 4 for d in (1, 2, 3)]
+    zp = [(item * 2 + x, f) for item in zt]
+    greet([sib, yp, diag, xp] + zp)
+    shards = (wq_s, wkv_s, wo_s, win_s, wout_s)
+    wholes = (wq_v, wkv_v, wo_o, win_o, wout_o)
+    fy = (1 - y) * 2 + k
+    first = [0]
+    for split, count in GATHER_PIECES:
+        first.append(first[-1] + count)
+
+    def piece_rows(u, j, xx):
+        rows = shards[u].shape[0]
+        split, count = GATHER_PIECES[u]
+        if split:
+            size = rows // 2 // count
+            return xx * (rows // 2) + j * size, size
+        size = rows // count
+        return j * size, size
+
+    def own(u):
+        rows = shards[u].shape[0]
+        there = wholes[u].at[at_row(f * rows, rows)]
+        return remote_copy(shards[u], there, own_s.at[u], own_r.at[u], sib)
+
+    def keep(u):
+        rows = shards[u].shape[0]
+        there = wholes[u].at[at_row(f * rows, rows)]
+        return pltpu.make_async_copy(shards[u], there, own_l.at[u])
+
+    def over_y(u, j):
+        rows = shards[u].shape[0]
+        start, size = piece_rows(u, j, x)
+        i = first[u] + j
+        return remote_copy(
+            shards[u].at[at_row(start, size)],
+            wholes[u].at[at_row(f * rows + start, size)],
+            y_s.at[i],
+            y_r.at[i],
+            yp,
+        )
+
+    def landed(u, j, xx):
+        rows = shards[u].shape[0]
+        start, size = piece_rows(u, j, xx)
+        return wholes[u].at[at_row(fy * rows + start, size)]
+
+    def relay_core(u, j):
+        i = first[u] + j
+        ref = landed(u, j, x)
+        return remote_copy(ref, ref, cy_s.at[i], cy_r.at[i], sib)
+
+    def relay_x(u, j):
+        i = first[u] + j
+        ref = landed(u, j, x)
+        return remote_copy(ref, ref, x_s.at[i], x_r.at[i], xp)
+
+    def relay_core_x(u, j):
+        i = first[u] + j
+        ref = landed(u, j, 1 - x)
+        return remote_copy(ref, ref, cx_s.at[i], cx_r.at[i], sib)
+
+    def on_y(u, j):
+        over_y(u, j).wait_recv()
+        relay_core(u, j).start()
+        if GATHER_PIECES[u][0]:
+            relay_x(u, j).start()
+
+    def on_x(u, j):
+        if GATHER_PIECES[u][0]:
+            relay_x(u, j).wait_recv()
+            relay_core_x(u, j).start()
+
+    def finish_recv(u):
+        own(u).wait_recv()
+        keep(u).wait()
+        for j in range(GATHER_PIECES[u][1]):
+            relay_core(u, j).wait_recv()
+            if GATHER_PIECES[u][0]:
+                relay_core_x(u, j).wait_recv()
+
+    def finish_send(u):
+        own(u).wait_send()
+        for j in range(GATHER_PIECES[u][1]):
+            over_y(u, j).wait_send()
+            relay_core(u, j).wait_send()
+            if GATHER_PIECES[u][0]:
+                relay_x(u, j).wait_send()
+                relay_core_x(u, j).wait_send()
+
+    def vec(i, device):
+        return remote_copy(vec_s, vec_v.at[f], v_s.at[i], v_r.at[i], device)
+
+    for j in range(3):
+        over_y(1, j).start()
+        over_y(0, j).start()
+    vec_peers = (sib, yp, diag)
+    for i in range(3):
+        vec(i, vec_peers[i]).start()
+    vec_keep = pltpu.make_async_copy(vec_s, vec_v.at[f], v_l)
+    vec_keep.start()
+    for u in (1, 0):
+        own(u).start()
+        keep(u).start()
+    for j in range(3):
+        on_y(1, j)
+        on_y(0, j)
+    for u in (3, 2, 4):
+        for j in range(GATHER_PIECES[u][1]):
+            over_y(u, j).start()
+        own(u).start()
+        keep(u).start()
+    for j in range(3):
+        on_x(1, j)
+        on_x(0, j)
+    for i in range(3):
+        vec(i, vec_peers[i]).wait_recv()
+    vec_keep.wait()
+    finish_recv(1)
+
+    def z_kv(d):
+        return remote_copy(
+            send_kv.at[zt[d]], kvg.at[c], zk_s.at[d], zk_r.at[d], zp[d]
+        )
+
+    def z_kv_in(d):
+        slot = ((z + 3 - d) % 4) * 2 + x
+        return remote_copy(kvg.at[slot], kvg.at[slot], zk_s.at[d], zk_r.at[d], zp[d])
+
+    def z_q(d):
+        return remote_copy(
+            send_q.at[zt[d]], qg.at[z], zq_s.at[d], zq_r.at[d], zp[d]
+        )
+
+    def own_x():
+        return remote_copy(send_kv.at[z], kvg.at[c], f_s.at[3], f_r.at[3], xp)
+
+    def fwd_x(d):
+        slot = ((z + 3 - d) % 4) * 2 + x
+        return remote_copy(kvg.at[slot], kvg.at[slot], f_s.at[d], f_r.at[d], xp)
+
+    inputs = tok[...]
+    for part in range(4):
+        lanes = pl.ds(384 * part, 384)
+        made = jnp.dot(inputs, wkv_v[:, lanes], preferred_element_type=jnp.float32)
+        made = made + vec_v[part, 1:2, :].astype(jnp.float32)
+        send_kv[part] = made.astype(jnp.bfloat16)
+    own_x().start()
+    for d in (1, 0, 2):
+        z_kv(d).start()
+    keep_kv = pltpu.make_async_copy(send_kv.at[z], kvg.at[c], l_sem.at[0])
+    keep_kv.start()
+    finish_recv(0)
+    bias = lane_windows([vec_v[part, 0:1, 0:256].astype(jnp.float32) for part in range(4)])
+    for part in range(4):
+        lanes = pl.ds(window_start(part), 256)
+        made = jnp.dot(inputs, wq_v[:, lanes], preferred_element_type=jnp.float32)
+        made = made + bias[:, window_start(part) : window_start(part) + 256]
+        send_q[part] = made.astype(jnp.bfloat16)
+    for d in (1, 0, 2):
+        z_q(d).start()
+    keep_q = pltpu.make_async_copy(send_q.at[z], qg.at[z], l_sem.at[1])
+    keep_q.start()
+    outs = (
+        pltpu.make_async_copy(wq_v, wq_o, out_sem.at[0]),
+        pltpu.make_async_copy(wkv_v, wkv_o, out_sem.at[1]),
+        pltpu.make_async_copy(vec_v, vec_o, out_sem.at[2]),
+    )
+    for item in outs:
+        item.start()
+    on_y(3, 0)
+    z_kv_in(0).wait_recv()
+    fwd_x(0).start()
+    z_kv_in(2).wait_recv()
+    fwd_x(2).start()
+    z_kv_in(1).wait_recv()
+    fwd_x(1).start()
+    on_y(3, 1)
+    on_y(2, 0)
+    on_x(3, 0)
+    on_x(3, 1)
+    for j in range(4):
+        on_y(4, j)
+    for d in range(3):
+        z_kv(d).wait_send()
+        z_q(d).wait()
+        fwd_x(d).wait()
+    own_x().wait()
+    keep_kv.wait()
+    keep_q.wait()
+    for u in (2, 3, 4):
+        finish_recv(u)
+    for u in range(5):
+        finish_send(u)
+    for i in range(3):
+        vec(i, vec_peers[i]).wait_send()
+    for item in outs:
+        item.wait()
+
+
+def any_specs(count):
+    return [pl.BlockSpec(memory_space=pl.ANY)] * count
+
+
+def vmem_specs(count):
+    return [pl.BlockSpec(memory_space=pltpu.VMEM)] * count
+
+
+def half(*shape):
+    return jax.ShapeDtypeStruct(shape, jnp.bfloat16)
+
+
+def full(*shape):
+    return jax.ShapeDtypeStruct(shape, jnp.float32)
+
+
+def gather_project(tok, wq, wkv, wo, win, wout, vec):
+    rows, width = tok.shape
+    d = pltpu.SemaphoreType.DMA
+    count = sum(item[1] for item in GATHER_PIECES)
+    return pl.pallas_call(
+        gather_project_kernel,
+        out_shape=[
+            half(4, rows, 256),
+            half(8, rows, 384),
+            half(width, width),
+            half(width, 2 * width),
+            half(width, width),
+            half(width, win.shape[1]),
+            half(4 * wout.shape[0], width),
+            half(4, 16, 384),
+        ],
+        in_specs=vmem_specs(1) + any_specs(6),
+        out_specs=any_specs(8),
+        scratch_shapes=[
+            pltpu.VMEM((width, width), jnp.bfloat16),
+            pltpu.VMEM((width, 2 * width), jnp.bfloat16),
+            pltpu.VMEM((4, 16, 384), jnp.bfloat16),
+            pltpu.VMEM((4, rows, 384), jnp.bfloat16),
+            pltpu.VMEM((4, rows, 256), jnp.bfloat16),
+            d((5,)),
+            d((5,)),
+            d((5,)),
+        ]
+        + [d((count,))] * 8
+        + [d((3,)), d((3,)), d, d((3,)), d((3,)), d((3,)), d((3,)), d((4,)), d((4,)), d((2,)), d((3,))],
+        compiler_params=pltpu.CompilerParams(
+            collective_id=2, has_side_effects=True, vmem_limit_bytes=40 * 2**20
+        ),
+        cost_estimate=pl.CostEstimate(flops=10**9, bytes_accessed=10**8, transcendentals=0),
+        name="gather_project",
+    )(tok, wq, wkv, wo, win, wout, vec)
+
+
+def pick(parity, value_side, by_window):
+    shape = (384, 256) if not by_window else (256, 384)
+    spread = lax.broadcasted_iota(jnp.int32, shape, 0 if not by_window else 1)
+    window = lax.broadcasted_iota(jnp.int32, shape, 1 if not by_window else 0)
+    lane = spread % 128
+    low = 64 if value_side else 0
+    target = (spread // 128) * 64 + (lane - low) + 64 * parity
+    inside = (lane >= low) & (lane < low + 64)
+    return jnp.where(inside & (target == window), 1.0, 0.0)
+
+
+def dot_nt(left, right):
+    return lax.dot_general(
+        left, right, (((1,), (1,)), ((), ())), preferred_element_type=jnp.float32
+    )
+
+
+def attention_kernel(deal, lengths, qg, kvg, owin, osave, lse, kvn, kvt, qt):
+    c = lax.axis_index("ctx")
+    z = c // 2
+    x = c % 2
+    scale = HEAD_DIM ** (-0.5)
+    span = 1024
+    for b in range(16):
+        natural = pl.multiple_of(deal[b] * BLOCK, BLOCK)
+        for h in range(3):
+            tile = kvg[b // 2, pl.ds((b % 2) * BLOCK, BLOCK), pl.ds(128 * h, 128)]
+            kvn[h, pl.ds(natural, BLOCK), :] = tile
+            kvt[h, :, pl.ds(natural, BLOCK)] = jnp.transpose(tile.astype(jnp.float32)).astype(
+                jnp.bfloat16
+            )
+    spread = (pick(z % 2, False, False) * scale).astype(jnp.bfloat16)
+    gather = pick(z % 2, True, False).astype(jnp.bfloat16)
+    for part in range(4):
+        qt[:, pl.ds(256 * part, 256)] = dot_nt(spread, qg[part]).astype(jnp.bfloat16)
+
+    @pl.loop(0, 8)
+    def _(b):
+        dealt = ((b // 2) * 2 + x) * 2 + b % 2
+        seq = deal[dealt] // 8
+        start = pl.multiple_of(seq * span, span)
+        length = lengths[seq]
+        here = pl.ds(pl.multiple_of(b * BLOCK, BLOCK), BLOCK)
+        rows = lax.broadcasted_iota(jnp.int32, (span, BLOCK), 0)
+        made = []
+        for h in range(3):
+            scores = jnp.dot(
+                kvn[h, pl.ds(start, span), :],
+                qt[pl.ds(128 * h, 128), here],
+                preferred_element_type=jnp.float32,
+            )
+            scores = jnp.where(rows < length, scores, NEG_FILL)
+            top = jnp.max(scores, axis=0, keepdims=True)
+            weights = jnp.exp(scores - top)
+            total = jnp.sum(weights, axis=0, keepdims=True)
+            mixed = jnp.dot(
+                kvt[h, :, pl.ds(start, span)],
+                weights.astype(jnp.bfloat16),
+                preferred_element_type=jnp.float32,
+            )
+            mixed = mixed / total
+            osave[h, b] = mixed[64:]
+            lse[h, b] = jnp.broadcast_to(top + jnp.log(total), (8, BLOCK))
+            made.append(jnp.transpose(mixed).astype(jnp.bfloat16))
+        joined = jnp.concatenate(made, axis=1)
+        owin[b // 2, pl.ds(pl.multiple_of((b % 2) * BLOCK, BLOCK), BLOCK), :] = jnp.dot(
+            joined, gather, preferred_element_type=jnp.float32
+        ).astype(jnp.bfloat16)
+
+
+def attention_forward(deal, lengths, qg, kvg):
+    smem = [pl.BlockSpec(memory_space=pltpu.SMEM)] * 2
+    return pl.pallas_call(
+        attention_kernel,
+        out_shape=[
+            half(4, 256, 256),
+            full(3, 8, 64, BLOCK),
+            full(3, 8, 8, BLOCK),
+            half(3, 2048, 128),
+            half(3, 128, 2048),
+        ],
+        in_specs=smem + vmem_specs(2),
+        out_specs=vmem_specs(5),
+        scratch_shapes=[pltpu.VMEM((384, 1024), jnp.bfloat16)],
+        compiler_params=pltpu.CompilerParams(vmem_limit_bytes=40 * 2**20),
+        cost_estimate=pl.CostEstimate(flops=2 * 10**9, bytes_accessed=10**7, transcendentals=3 * 10**6),
+        name="attention_forward",
+    )(deal, lengths, qg, kvg)
+
+
+def attention_back_kernel(
+    deal, lengths, qg, dog, osave, lse, kvn, kvt, dqwin, dkv, qt, dot_t, qd, acc
+):
+    c = lax.axis_index("ctx")
+    z = c // 2
+    x = c % 2
+    scale = HEAD_DIM ** (-0.5)
+    span = 1024
+    spread_q = (pick(z % 2, False, False) * scale).astype(jnp.bfloat16)
+    spread_o = pick(z % 2, True, False).astype(jnp.bfloat16)
+    gather_q = pick(z % 2, False, False).astype(jnp.bfloat16)
+    for part in range(4):
+        lanes = pl.ds(256 * part, 256)
+        qt[:, lanes] = dot_nt(spread_q, qg[part]).astype(jnp.bfloat16)
+        dot_t[:, lanes] = dot_nt(spread_o, dog[part]).astype(jnp.bfloat16)
+        q_rows = dot_nt(qg[part], spread_q).astype(jnp.bfloat16)
+        o_rows = dot_nt(dog[part], spread_o).astype(jnp.bfloat16)
+        for i in range(2):
+            qd[2 * part + i, pl.ds(0, BLOCK), :] = q_rows[i * BLOCK : (i + 1) * BLOCK]
+            qd[2 * part + i, pl.ds(BLOCK, BLOCK), :] = o_rows[i * BLOCK : (i + 1) * BLOCK]
+    for h in range(3):
+        acc[h] = jnp.zeros(acc.shape[1:], jnp.float32)
+
+    @pl.loop(0, 8)
+    def _(b):
+        dealt = ((b // 2) * 2 + x) * 2 + b % 2
+        seq = deal[dealt] // 8
+        start = pl.multiple_of(seq * span, span)
+        length = lengths[seq]
+        here = pl.ds(pl.multiple_of(b * BLOCK, BLOCK), BLOCK)
+        rows = lax.broadcasted_iota(jnp.int32, (span, BLOCK), 0)
+        made = []
+        for h in range(3):
+            lanes = pl.ds(128 * h, 128)
+            part = kvn[h, pl.ds(start, span), :]
+            scores = jnp.dot(part, qt[lanes, here], preferred_element_type=jnp.float32)
+            scores = jnp.where(rows < length, scores, NEG_FILL)
+            probs = jnp.exp(scores - lse[h, b, 0:1, :])
+            upstream = dot_t[lanes, here]
+            grad_probs = jnp.dot(part, upstream, preferred_element_type=jnp.float32)
+            delta = jnp.sum(
+                osave[h, b] * upstream[64:].astype(jnp.float32), axis=0, keepdims=True
+            )
+            grad_scores = (probs * (grad_probs - delta)).astype(jnp.bfloat16)
+            grad_query = jnp.dot(
+                kvt[h, :, pl.ds(start, span)], grad_scores, preferred_element_type=jnp.float32
+            )
+            made.append((jnp.transpose(grad_query) * scale).astype(jnp.bfloat16))
+            both = jnp.concatenate([grad_scores, probs.astype(jnp.bfloat16)], axis=1)
+            acc[h, pl.ds(start, span), :] += jnp.dot(
+                both, qd[b, :, lanes], preferred_element_type=jnp.float32
+            )
+        joined = jnp.concatenate(made, axis=1)
+        dqwin[b // 2, pl.ds(pl.multiple_of((b % 2) * BLOCK, BLOCK), BLOCK), :] = jnp.dot(
+            joined, gather_q, preferred_element_type=jnp.float32
+        ).astype(jnp.bfloat16)
+
+    for b in range(16):
+        natural = pl.multiple_of(deal[b] * BLOCK, BLOCK)
+        for h in range(3):
+            dkv[b // 2, pl.ds((b % 2) * BLOCK, BLOCK), pl.ds(128 * h, 128)] = acc[
+                h, pl.ds(natural, BLOCK), :
+            ].astype(jnp.bfloat16)
+
+
+def attention_backward(deal, lengths, qg, dog, osave, lse, kvn, kvt):
+    smem = [pl.BlockSpec(memory_space=pltpu.SMEM)] * 2
+    return pl.pallas_call(
+        attention_back_kernel,
+        out_shape=[half(4, 256, 256), half(8, 256, 384)],
+        in_specs=smem + vmem_specs(6),
+        out_specs=vmem_specs(2),
+        scratch_shapes=[
+            pltpu.VMEM((384, 1024), jnp.bfloat16),
+            pltpu.VMEM((384, 1024), jnp.bfloat16),
+            pltpu.VMEM((8, 256, 384), jnp.bfloat16),
+            pltpu.VMEM((3, 2048, 128), jnp.float32),
+        ],
+        compiler_params=pltpu.CompilerParams(vmem_limit_bytes=40 * 2**20),
+        cost_estimate=pl.CostEstimate(flops=5 * 10**9, bytes_accessed=10**7, transcendentals=3 * 10**6),
+        name="attention_backward",
+    )(deal, lengths, qg, dog, osave, lse, kvn, kvt)
+
+
+def heads_home_kernel(win, out, got, send, recv, local):
+    c, f, z, x, y, k = places()
+    zt = [(z + d) % 4 for d in (1, 2, 3)]
+    zp = [(item * 2 + x, f) for item in zt]
+    greet(zp)
+    copies = [
+        remote_copy(win.at[zt[d]], got.at[z], send.at[d], recv.at[d], zp[d]) for d in range(3)
+    ]
+    for d in (1, 0, 2):
+        copies[d].start()
+    keep = pltpu.make_async_copy(win.at[z], got.at[z], local)
+    keep.start()
+    keep.wait()
+    for item in copies:
+        item.wait()
+    out[...] = lane_windows([got[part] for part in range(4)])
+
+
+def heads_home(win):
+    d = pltpu.SemaphoreType.DMA
+    return pl.pallas_call(
+        heads_home_kernel,
+        out_shape=half(256, 768),
+        in_specs=vmem_specs(1),
+        out_specs=pl.BlockSpec(memory_space=pltpu.VMEM),
+        scratch_shapes=[pltpu.VMEM((4, 256, 256), jnp.bfloat16), d((3,)), d((3,)), d],
+        compiler_params=pltpu.CompilerParams(collective_id=3, has_side_effects=True, vmem_limit_bytes=16 * 2**20),
+        cost_estimate=pl.CostEstimate(flops=10**6, bytes_accessed=10**7, transcendentals=0),
+        name="heads_home",
+    )(win)
+
+
+def heads_away_kernel(rows, out, send, recv, local):
+    c, f, z, x, y, k = places()
+    zt = [(z + d) % 4 for d in (1, 2, 3)]
+    zp = [(item * 2 + x, f) for item in zt]
+    greet(zp)
+
+    def lanes(part):
+        return pl.ds(pl.multiple_of(window_start(part), 128), 256)
+
+    copies = [
+        remote_copy(rows.at[:, lanes(zt[d])], out.at[z], send.at[d], recv.at[d], zp[d])
+        for d in range(3)
+    ]
+    for d in (1, 0, 2):
+        copies[d].start()
+    keep = pltpu.make_async_copy(rows.at[:, lanes(z)], out.at[z], local)
+    keep.start()
+    keep.wait()
+    for item in copies:
+        item.wait()
+
+
+def heads_away(rows):
+    d = pltpu.SemaphoreType.DMA
+    return pl.pallas_call(
+        heads_away_kernel,
+        out_shape=half(4, 256, 256),
+        in_specs=vmem_specs(1),
+        out_specs=pl.BlockSpec(memory_space=pltpu.VMEM),
+        scratch_shapes=[d((3,)), d((3,)), d],
+        compiler_params=pltpu.CompilerParams(collective_id=4, has_side_effects=True, vmem_limit_bytes=16 * 2**20),
+        cost_estimate=pl.CostEstimate(flops=10**6, bytes_accessed=10**7, transcendentals=0),
+        name="heads_away",
+    )(rows)
+
+
+def grads_home_kernel(dqwin, dkv, dq, dkv_out, got_q, theirs, mine, got_kv, q_s, q_r, x_s, x_r, k_s, k_r, l_q, l_k, l_own):
+    c, f, z, x, y, k = places()
+    zt = [(z + d) % 4 for d in (1, 2, 3)]
+    zp = [(item * 2 + x, f) for item in zt]
+    xp = (z * 2 + (1 - x), f)
+    greet([xp] + zp)
+
+    def over_x(i, part):
+        return remote_copy(dkv.at[part * 2 + (1 - x)], theirs.at[i], x_s.at[i], x_r.at[i], xp)
+
+    order = [zt[1], zt[0], zt[2], z]
+    where = [1, 0, 2]
+    for i in range(4):
+        over_x(i, order[i]).start()
+        pltpu.make_async_copy(dkv.at[order[i] * 2 + x], mine.at[i], l_k.at[i]).start()
+
+    def q_copy(d):
+        return remote_copy(dqwin.at[zt[d]], got_q.at[z], q_s.at[d], q_r.at[d], zp[d])
+
+    for d in (1, 0, 2):
+        q_copy(d).start()
+    keep_q = pltpu.make_async_copy(dqwin.at[z], got_q.at[z], l_q)
+    keep_q.start()
+
+    def kv_copy(i):
+        d = where[i]
+        return remote_copy(mine.at[i], got_kv.at[z], k_s.at[d], k_r.at[d], zp[d])
+
+    for i in range(4):
+        over_x(i, order[i]).wait_recv()
+        pltpu.make_async_copy(dkv.at[order[i] * 2 + x], mine.at[i], l_k.at[i]).wait()
+
+        @pl.loop(0, 16)
+        def _(j, i=i):
+            rows = pl.ds(pl.multiple_of(j * 16, 16), 16)
+            mine[i, rows] = (
+                mine[i, rows].astype(jnp.float32) + theirs[i, rows].astype(jnp.float32)
+            ).astype(jnp.bfloat16)
+
+        if i < 3:
+            kv_copy(i).start()
+    own = pltpu.make_async_copy(mine.at[3], got_kv.at[z], l_own)
+    own.start()
+    keep_q.wait()
+    for d in range(3):
+        q_copy(d).wait()
+    dq[...] = lane_windows([got_q[part] for part in range(4)])
+    own.wait()
+    for i in range(3):
+        kv_copy(i).wait()
+    for part in range(4):
+        dkv_out[:, pl.ds(384 * part, 384)] = got_kv[part]
+    for i in range(4):
+        over_x(i, order[i]).wait_send()
+
+
+def grads_home(dqwin, dkv):
+    d = pltpu.SemaphoreType.DMA
+    return pl.pallas_call(
+        grads_home_kernel,
+        out_shape=[half(256, 768), half(256, 1536)],
+        in_specs=vmem_specs(2),
+        out_specs=vmem_specs(2),
+        scratch_shapes=[
+            pltpu.VMEM((4, 256, 256), jnp.bfloat16),
+            pltpu.VMEM((4, 256, 384), jnp.bfloat16),
+            pltpu.VMEM((4, 256, 384), jnp.bfloat16),
+            pltpu.VMEM((4, 256, 384), jnp.bfloat16),
+            d((3,)),
+            d((3,)),
+            d((4,)),
+            d((4,)),
+            d((3,)),
+            d((3,)),
+            d,
+            d((4,)),
+            d,
+        ],
+        compiler_params=pltpu.CompilerParams(collective_id=5, has_side_effects=True, vmem_limit_bytes=24 * 2**20),
+        cost_estimate=pl.CostEstimate(flops=10**7, bytes_accessed=5 * 10**7, transcendentals=0),
+        name="grads_home",
+    )(dqwin, dkv)
+
+
+def reduce_grads(grads):
+    chunks = []
+    for m, item in enumerate(grads):
+        shard = item.shape[0] // 4
+        high = min(shard, 192)
+        wide = min(item.shape[1], 768)
+        for i in range(shard // high):
+            for j in range(item.shape[1] // wide):
+
+                def slab(ref, f, i=i, j=j, shard=shard, high=high, wide=wide):
+                    rows = pl.ds(pl.multiple_of(f * shard + i * high, high), high)
+                    return ref.at[rows, pl.ds(j * wide, wide)]
+
+                def home(ref, xx, i=i, j=j, high=high, wide=wide):
+                    lanes = pl.ds(pl.multiple_of(j * wide + xx * (wide // 2), 128), wide // 2)
+                    return ref.at[pl.ds(i * high, high), lanes]
+
+                chunks.append((m, slab, m, home, high, wide))
+    n = len(chunks)
+    count = len(grads)
+    scratch = []
+    for lead, divide_rows, divide_lanes in (
+        ((2,), 1, 1),
+        ((2,), 1, 1),
+        ((), 1, 1),
+        ((), 1, 2),
+        ((), 1, 2),
+        ((3,), 4, 2),
+        ((2,), 1, 2),
+    ):
+        for item in chunks:
+            shape = lead + (item[4] // divide_rows, item[5] // divide_lanes)
+            scratch.append(pltpu.VMEM(shape, jnp.bfloat16))
+    d = pltpu.SemaphoreType.DMA
+    for lanes in (2, 2, 2, 2, 1, 1, 1, 1, 3, 3, 3, 3, 1, 1):
+        scratch.append(d((n, lanes)) if lanes > 1 else d((n,)))
+    return pl.pallas_call(
+        functools.partial(reduce_kernel, chunks, count, count),
+        out_shape=[half(item.shape[0] // 4, item.shape[1]) for item in grads],
+        in_specs=any_specs(count),
+        out_specs=any_specs(count),
+        scratch_shapes=scratch,
+        compiler_params=pltpu.CompilerParams(
+            collective_id=1, has_side_effects=True, vmem_limit_bytes=48 * 2**20
+        ),
+        cost_estimate=pl.CostEstimate(flops=10**7, bytes_accessed=10**8, transcendentals=0),
+        name="grad_reduce",
+    )(*grads)
+
+
+def body_fast(
+    tokens,
+    seq_lengths,
+    deal,
+    w_query,
+    w_key,
+    w_value,
+    w_attn_out,
+    b_query,
+    b_value,
+    b_attn_out,
+    norm1_gain,
+    norm1_bias,
+    w_in,
+    b_in,
+    w_out,
+    b_out,
+    norm2_gain,
+    norm2_bias,
+    cotangent,
+):
+    inputs = tokens[0]
+    width = inputs.shape[1]
+    part = width // 4
+    odd = lax.axis_index("fsdp") % 2 == 1
+    pair_shape = (part, HEADS, HEAD_DIM)
+    pair_weight = jnp.stack(
+        [to_half(w_key).reshape(pair_shape), to_half(w_value).reshape(pair_shape)], axis=2
+    ).reshape(part, 2 * width)
+    query_row = jnp.where(
+        odd, jnp.pad(b_query, (HEAD_DIM, 384 - 256)), jnp.pad(b_query, (0, 384 - 192))
+    )
+    value_heads = b_value.reshape(3, HEAD_DIM)
+    pair_row = jnp.stack([jnp.zeros_like(value_heads), value_heads], axis=1).reshape(384)
+    small = [query_row, pair_row]
+    for item in (b_attn_out, norm1_gain, norm1_bias, b_out, norm2_gain, norm2_bias):
+        small.append(jnp.pad(item, (0, 384 - part)))
+    packed = jnp.concatenate(
+        [jnp.stack(small), b_in.reshape(2, 384), jnp.zeros((6, 384), jnp.float32)], axis=0
+    )
+    (
+        query_groups,
+        pair_groups,
+        query_weight,
+        pair_weights,
+        mix_weight,
+        inner_weight,
+        outer_weight,
+        vectors,
+    ) = gather_project(
+        inputs,
+        to_half(w_query),
+        pair_weight,
+        to_half(w_attn_out),
+        to_half(w_in),
+        to_half(w_out),
+        to_half(packed),
+    )
+    vectors = vectors.astype(jnp.float32)
+    mix_bias, gain_one, shift_one, outer_bias, gain_two, shift_two = (
+        vectors[:, 2 + i, :part].reshape(width) for i in range(6)
+    )
+    inner_bias = vectors[:, 8:10, :].reshape(4 * width)
+    deal_row = deal[0]
+    lengths = seq_lengths[0]
+    out_windows, out_heads, log_totals, pairs, pairs_turned = attention_forward(
+        deal_row, lengths, query_groups, pair_groups
+    )
+    attn_in = heads_home(out_windows)
+    residual_one = (
+        inputs.astype(jnp.float32)
+        + jnp.dot(attn_in, mix_weight, preferred_element_type=jnp.float32)
+        + mix_bias
+    )
+    normal_one, normed_one, inverse_one = norm_forward(residual_one, gain_one, shift_one)
+    normal_half = normal_one.astype(jnp.bfloat16)
+    pre_act = jnp.dot(normal_half, inner_weight, preferred_element_type=jnp.float32) + inner_bias
+    activated, gelu_pull = jax.vjp(exact_gelu, pre_act)
+    hidden = activated.astype(jnp.bfloat16)
+    residual_two = (
+        normal_one
+        + jnp.dot(hidden, outer_weight, preferred_element_type=jnp.float32)
+        + outer_bias
+    )
+    layer_out, normed_two, inverse_two = norm_forward(residual_two, gain_two, shift_two)
+    upstream = cotangent[0].astype(jnp.float32)
+    grad_two, grad_gain_two, grad_shift_two = norm_backward(
+        upstream, gain_two, normed_two, inverse_two
+    )
+    grad_branch = grad_two.astype(jnp.bfloat16)
+    grad_outer_bias = jnp.sum(grad_branch.astype(jnp.float32), axis=0)
+    grad_outer = jnp.einsum("tf,td->fd", hidden, grad_branch, preferred_element_type=jnp.float32)
+    grad_hidden = jnp.einsum(
+        "td,fd->tf", grad_branch, outer_weight, preferred_element_type=jnp.float32
+    )
+    grad_pre = gelu_pull(grad_hidden)[0].astype(jnp.bfloat16)
+    grad_inner_bias = jnp.sum(grad_pre.astype(jnp.float32), axis=0)
+    grad_inner = jnp.einsum("td,tf->df", normal_half, grad_pre, preferred_element_type=jnp.float32)
+    grad_normal = grad_two + jnp.einsum(
+        "tf,df->td", grad_pre, inner_weight, preferred_element_type=jnp.float32
+    )
+    grad_one, grad_gain_one, grad_shift_one = norm_backward(
+        grad_normal, gain_one, normed_one, inverse_one
+    )
+    grad_attn = grad_one.astype(jnp.bfloat16)
+    grad_mix_bias = jnp.sum(grad_attn.astype(jnp.float32), axis=0)
+    grad_mix = jnp.einsum("td,te->de", attn_in, grad_attn, preferred_element_type=jnp.float32)
+    grad_mixed = jnp.einsum(
+        "te,de->td", grad_attn, mix_weight, preferred_element_type=jnp.float32
+    ).astype(jnp.bfloat16)
+    grad_groups = heads_away(grad_mixed)
+    query_back, pairs_back = attention_backward(
+        deal_row,
+        lengths,
+        query_groups,
+        grad_groups,
+        out_heads,
+        log_totals,
+        pairs,
+        pairs_turned,
+    )
+    grad_query, grad_pairs = grads_home(query_back, pairs_back)
+    grad_query_weight = jnp.einsum(
+        "td,te->de", inputs, grad_query, preferred_element_type=jnp.float32
+    )
+    grad_pair_weight = jnp.einsum(
+        "td,te->de", inputs, grad_pairs, preferred_element_type=jnp.float32
+    )
+    grad_query_bias = jnp.sum(grad_query.astype(jnp.float32), axis=0)
+    grad_pair_bias = jnp.sum(grad_pairs.astype(jnp.float32), axis=0)
+    grad_value_bias = grad_pair_bias.reshape(HEADS, 2, HEAD_DIM)[:, 1, :].reshape(width)
+    grad_inputs = (
+        grad_one
+        + jnp.einsum("te,de->td", grad_query, query_weight, preferred_element_type=jnp.float32)
+        + jnp.einsum("te,de->td", grad_pairs, pair_weights, preferred_element_type=jnp.float32)
+    )
+    rows = jnp.stack(
+        [
+            grad_query_bias,
+            grad_value_bias,
+            grad_mix_bias,
+            grad_gain_one,
+            grad_shift_one,
+            grad_outer_bias,
+            grad_gain_two,
+            grad_shift_two,
+        ]
+    )
+    shares = jnp.transpose(rows.reshape(8, 4, part), (1, 0, 2)).reshape(4, 2 * width)
+    shares = jnp.concatenate([shares, grad_inner_bias.reshape(4, width)], axis=1)
+    shares = jnp.pad(shares, ((0, 0), (0, 64 * 256 - 3 * width))).reshape(256, 256)
+    (
+        sum_query,
+        sum_pairs,
+        sum_mix,
+        sum_inner,
+        sum_outer,
+        sum_small,
+    ) = reduce_grads(
+        [
+            to_half(grad_query_weight),
+            to_half(grad_pair_weight),
+            to_half(grad_mix),
+            to_half(grad_inner),
+            to_half(grad_outer),
+            to_half(shares),
+        ]
+    )
+    sum_pairs = sum_pairs.astype(jnp.float32).reshape(part, HEADS, 2, HEAD_DIM)
+    flat = sum_small.astype(jnp.float32).reshape(-1)[: 3 * width]
+    small = flat[: 2 * width].reshape(8, part)
+    return (
+        layer_out.astype(jnp.bfloat16)[None],
+        grad_inputs[None],
+        sum_query.astype(jnp.float32),
+        sum_pairs[:, :, 0, :].reshape(part, width),
+        sum_pairs[:, :, 1, :].reshape(part, width),
+        sum_mix.astype(jnp.float32),
+        small[0],
+        small[1],
+        small[2],
+        small[3],
+        small[4],
+        sum_inner.astype(jnp.float32),
+        flat[2 * width :],
+        sum_outer.astype(jnp.float32),
+        small[5],
+        small[6],
+        small[7],
+    )
+
+
 def solution(mesh):
     placed = (
         P("fsdp", "ctx", None),
@@ -460,8 +1446,9 @@
         P("fsdp"),
         P("fsdp", "ctx", None),
     )
+    fast = dict(mesh.shape) == {"ctx": 8, "fsdp": 4}
     return jax.shard_map(
-        body,
+        body_fast if fast else body,
         mesh=mesh,
         in_specs=placed,
         out_specs=(

time: 1010 us -> 351 us (0.35)
  waiting for transfers between devices: 605 us -> 0 us
  Pallas kernels: 0 us -> 263 us
  local copies, waits for them, and re-layouts: 122 us -> 23.9 us
  matrix products: 120 us -> 41.9 us
  other arithmetic: 75.4 us -> 20.2 us
  blocking collectives: 50.6 us -> 0 us
  between operations: 17.1 us -> 1.19 us
    reduce_scatter x5 -> x0, waiting for transfers between devices: 269 us -> none  [the longest x1 74.6 us: body(): lax.psum_scatter(grad_values_all.astype(jnp.bfloat16), 'ctx', scatter_dim...]
    pallas_call x0 -> x7, Pallas kernels: none -> 263 us  [the longest x1 112 us: reduce_grads(): pl.pallas_call(functools.partial(reduce_kernel, chunks, count, count), ou...]
    all_gather x8 -> x0, waiting for transfers between devices: 167 us -> none  [the longest x1 61.2 us: body(): lax.all_gather(keys, 'ctx', axis=0, tiled=True)]
    psum x1 -> x0, waiting for transfers between devices: 104 us -> none  [body(): lax.psum(shares[0].astype(jnp.bfloat16), 'ctx').astype(jnp.float32)]
    dot_general x32 -> x13, matrix products: 120 us -> 41.9 us  [the longest x1 11.6 us: body_fast(): jnp.dot(normal_half, inner_weight, preferred_element_type=jnp.float32)]
    unnamed x20 -> x0, waiting for transfers between devices: 65.4 us -> none
    dynamic_update_slice x4 -> x0, local copies, waits for them, and re-layouts: 59.3 us -> none  [add_rows(): return lax.dynamic_update_slice_in_dim(total, current + term, at_row, 0)]
    psum x1 -> x0, blocking collectives: 23.2 us -> none  [body(): lax.psum(shares[4].astype(jnp.bfloat16), 'ctx').astype(jnp.float32)]
  transfers between devices with their start and end apart: 17 -> 0, of which waited for: 15 -> 0; matrix products, arithmetic and copies ran while one was open for 14% -> 0% of each run, Pallas kernels for 0% -> 0%
where the time goes in v2:
time: 351 us; the launch traced here: 350 us
  Pallas kernels  263 us (75%)
  matrix products  41.9 us (12%)
  local copies, waits for them, and re-layouts  23.9 us (7%)
  other arithmetic  20.2 us (6%)
    pallas_call x1, Pallas kernels, reduce_grads(): pl.pallas_call(functools.partial(reduce_kernel, chunks, count, count), ou...  112 us
    pallas_call x1, Pallas kernels, gather_project(): pl.pallas_call(gather_project_kernel, out_shape=[half(4, rows, 256), half...  64.2 us
    pallas_call x1, Pallas kernels, grads_home(): pl.pallas_call(grads_home_kernel, out_shape=[half(256, 768), half(256, 15...  29.6 us
    pallas_call x1, Pallas kernels, heads_home(): pl.pallas_call(heads_home_kernel, out_shape=half(256, 768), in_specs=vmem...  16.4 us
    unnamed x75, local copies, waits for them, and re-layouts  16.2 us
    pallas_call x1, Pallas kernels, attention_backward(): pl.pallas_call(attention_back_kernel, out_shape=[half(4, 256, 256), half(...  15.7 us
    pallas_call x1, Pallas kernels, heads_away(): pl.pallas_call(heads_away_kernel, out_shape=half(4, 256, 256), in_specs=v...  13.9 us
    dot_general x1, matrix products, body_fast(): jnp.dot(normal_half, inner_weight, preferred_element_type=jnp.float32)  11.6 us

profile of v2, /device:TPU:0, one launch (start us, length us, event | category | flops | bytes accessed | tf_op | source)
XLA Modules:
  0.0 350.2 jit_solution(1514933226732690972)
XLA Ops:
  0.7 0.8 select_convert_fusion
  1.5 0.7 convert.98
  2.4 0.7 convert.105
  3.1 0.7 convert.99
  3.8 0.7 convert.100
  4.5 0.7 convert.101
  5.2 0.7 convert.102
  5.9 0.7 convert.103
  6.6 0.7 convert.104
  7.3 1.2 copy.50
  8.6 1.2 copy.51
  10.3 2.0 convert_element_type.122.refs_4_
  13.0 0.7 copy-done
  13.8 64.2 %gather_project.1 = (bf16[4,256,256]{2,1,0:T(8,128)(2,1)S(1)}, bf16[8,256,384]{2,1,0:T(8,128)(2,1)S(1)}, bf16[768,768]{1,0:T(8,128)(2,1)S(1)}, bf16[768,1536]{1,...) custom-call(bf16[256,768]{1,0:T(8,128)(2,1)S(1)} %bitcast.56, ...), custom_call_target="tpu_custom_call" | custom-call | flops 1000000000 | bytes 100000000 | tf_op jit(solution)/shard_map/gather_project/pallas_call | solution.py:825
  78.0 1.4 copy-done.1
  79.4 1.0 copy-done.2
  80.4 11.1 %attention_forward.1 = (bf16[4,256,256]{2,1,0:T(8,128)(2,1)S(1)}, f32[3,8,64,128]{3,2,1,0:T(8,128)S(1)}, f32[3,8,8,128]{3,2,1,0:T(8,128)S(1)}, bf16[3,2048,128]{...) custom-call(s32[16]{0:T(128)S(1)} %bitcast.57, s32[2]{0:T(128)S(1)} %bitcast.59, bf16[4,256,256]{2,1,0:T(8,128)(2,1)S(1)} %get-tuple-element.40.qg, ...), custom_call_target="tpu_custom_call" | custom-call | flops 2000000000 | bytes 10000000 | tf_op jit(solution)/shard_map/attention_forward/pallas_call | solution.py:931
  91.5 1.1 copy-done.11
  92.7 1.2 copy-done.13
  93.8 16.4 %heads_home.1 = bf16[256,768]{1,0:T(8,128)(2,1)S(1)} custom-call(bf16[4,256,256]{2,1,0:T(8,128)(2,1)S(1)} %get-tuple-element.42.win), custom_call_target="tpu_custom_call" | custom-call | flops 1000000 | bytes 10000000 | tf_op jit(solution)/shard_map/heads_home/pallas_call | solution.py:1053
  111.4 11.6 %multiply_convert_fusion = (bf16[256,3072]{1,0:T(8,128)(2,1)}, f32[256,3072]{1,0:T(8,128)}, f32[256,3072]{1,0:T(8,128)}) fusion(f32[3072]{0:T(1024)S(1)} %add.114, bf16[768,3072]{1,0:T(8,128)(2,1)} %get-tuple-element.45, f32[256,768]{1,0:T(8,128)S(1)} %get-tuple-element.128, f32[768]{0:T(1024)S(1)} %add.111, f32[768]{0:T(1024)S(1)} %mul.127, ...), kind=kOutput, calls=%fused_computation.7 | convolution fusion | flops 1260847104 | bytes 13389824 | tf_op jit(solution)/shard_map/dot_general | solution.py:1311
  123.1 4.3 %fusion.39 = (f32[256]{0:T(256)S(1)}, f32[256,768]{1,0:T(8,128)S(1)}) fusion(f32[768]{0:T(1024)S(1)} %add.118, bf16[256,3072]{1,0:T(8,128)(2,1)} %get-tuple-element.114, bf16[3072,768]{1,0:T(8,128)(2,1)} %get-tuple-element.46, f32[768]{0:T(1024)S(1)} %add.111, f32[768]{0:T(1024)S(1)} %mul.127, f32[256]{0:T(256)S(1)} %add_rsqrt_fusion.1, ...), kind=kOutput, calls=%fused_computation.96 | convolution fusion | flops 1209335552 | bytes 7876608 | tf_op jit(solution)/shard_map/dot_general | solution.py:1316
  127.4 0.9 copy-done.21
  128.7 2.5 fusion.17
  131.2 1.7 convert_reduce_fusion.1
  132.9 5.8 %fusion.40 = (bf16[3072]{0:T(1024)(128)(2,1)S(1)}, bf16[256,3072]{1,0:T(8,128)(2,1)S(1)}) fusion(f32[256,3072]{1,0:T(8,128)S(1)} %copy-done.29, f32[256,3072]{1,0:T(8,128)} %get-tuple-element.129, bf16[3072,768]{1,0:T(8,128)(2,1)} %get-tuple-element.46, f32[256,768]{1,0:T(8,128)S(1)} %get-tuple-element.111), kind=kOutput, calls=%fused_computation.97 | convolution fusion | flops 1219949568 | bytes 13375488 | tf_op jit(solution)/shard_map/td,fd->tf/dot_general | solution.py:1327
  138.8 1.8 multiply_reduce_fusion
  141.4 13.9 %heads_away.1.dog = bf16[4,256,256]{2,1,0:T(8,128)(2,1)S(1)} custom-call(bf16[256,768]{1,0:T(8,128)(2,1)S(1)} %convolution_convert_fusion.5.rows), custom_call_target="tpu_custom_call" | custom-call | flops 1000000 | bytes 10000000 | tf_op jit(solution)/shard_map/heads_away/pallas_call | solution.py:1089
  155.4 15.7 %attention_backward.1 = (bf16[4,256,256]{2,1,0:T(8,128)(2,1)S(1)}, bf16[8,256,384]{2,1,0:T(8,128)(2,1)S(1)}) custom-call(s32[16]{0:T(128)S(1)} %bitcast.58, s32[2]{0:T(128)S(1)} %bitcast.60, bf16[4,256,256]{2,1,0:T(8,128)(2,1)S(1)} %get-tuple-element.40.qg, bf16[4,256,256]{2,1,0:T(8,128)(2,1)S(1)} %heads_away.1.dog, f32[3,8,64,128]{3,2,1,0:T(8,128)S(1)} %copy-done.16, ...), custom_call_target="tpu_custom_call" | custom-call | flops 5000000000 | bytes 10000000 | tf_op jit(solution)/shard_map/attention_backward/pallas_call | solution.py:1016
  171.1 29.6 %grads_home.1 = (bf16[256,768]{1,0:T(8,128)(2,1)S(1)}, bf16[256,1536]{1,0:T(8,128)(2,1)S(1)}) custom-call(bf16[4,256,256]{2,1,0:T(8,128)(2,1)S(1)} %get-tuple-element.51.dqwin, bf16[8,256,384]{2,1,0:T(8,128)(2,1)S(1)} %get-tuple-element.52.dkv), custom_call_target="tpu_custom_call" | custom-call | flops 10000000 | bytes 50000000 | tf_op jit(solution)/shard_map/grads_home/pallas_call | solution.py:1159
  202.2 5.3 %convolution_convert_fusion.refs_4_ = bf16[3072,768]{1,0:T(8,128)(2,1)} fusion(bf16[256,3072]{1,0:T(8,128)(2,1)} %get-tuple-element.114, f32[256,768]{1,0:T(8,128)} %copy-done.23), kind=kOutput, calls=%fused_computation | convolution fusion | flops 1210515456 | bytes 7077888 | tf_op jit(solution)/shard_map/tf,td->fd/dot_general | solution.py:1326
  207.6 3.7 %convolution_convert_fusion.1.refs_3_ = bf16[768,3072]{1,0:T(8,128)(2,1)} fusion(bf16[256,3072]{1,0:T(8,128)(2,1)S(1)} %copy-done.26, f32[256,768]{1,0:T(8,128)S(1)} %copy-done.18, f32[768]{0:T(1024)S(1)} %add.111, f32[768]{0:T(1024)S(1)} %mul.127, f32[256]{0:T(256)S(1)} %add_rsqrt_fusion.1, f32[256]{0:T(256)S(1)} %broadcast_multiply_fusion.5), kind=kOutput, calls=%fused_computation.1 | convolution fusion | flops 1211301888 | bytes 7086080 | tf_op jit(solution)/shard_map/td,tf->df/dot_general | solution.py:1332
  211.8 2.2 fusion.6.refs_1_
  214.6 112.1 %grad_reduce.1 = (bf16[192,768]{1,0:T(8,128)(2,1)S(1)}, bf16[192,1536]{1,0:T(8,128)(2,1)S(1)}, bf16[192,768]{1,0:T(8,128)(2,1)S(1)}, bf16[192,3072]{1,0:T(8,128)...) custom-call(bf16[768,768]{1,0:T(8,128)(2,1)S(1)} %fusion.7.refs_0_, ...), custom_call_target="tpu_custom_call" | custom-call | flops 10000000 | bytes 100000000 | tf_op jit(solution)/shard_map/grad_reduce/pallas_call | solution.py:1221
  326.7 1.0 copy-done.4
  327.7 0.7 copy-done.5
  328.4 0.7 copy-done.7
  329.1 1.4 copy.58
  330.5 2.7 fusion.36
  333.2 2.2 copy.59
  335.4 2.2 copy.60
  337.6 1.7 convert_element_type.150
  339.3 2.9 convert_element_type.151
  342.2 0.9 convert_element_type.147
  343.1 0.9 convert_element_type.148
  344.6 0.6 slice.86
  345.2 1.6 convolution_add_fusion.2
  346.9 3.4 fusion.8
  (135 shorter events, 7.2 us)
Async XLA Ops:
  10.3 2.4 copy-start.24
  10.3 2.5 copy-start.27
  10.3 2.6 copy-start.28
  12.7 1.1 copy-start
  12.8 67.6 %copy-start.9 = (s32[1,16]{1,0:T(1,128)S(1)}, s32[1,16]{1,0:T(1,128)}, u32[]{:S(2)}) copy-start(s32[1,16]{1,0:T(1,128)} %param.21) | copy-start | bytes 196
  12.8 67.6 %copy-start.10 = (s32[1,2]{1,0:T(1,128)S(1)}, s32[1,2]{1,0:T(1,128)}, u32[]{:S(2)}) copy-start(s32[1,2]{1,0:T(1,128)} %param.20) | copy-start | bytes 28
  78.0 1.4 copy-start.1
  79.4 1.0 copy-start.2
  91.5 1.1 copy-start.11
  92.7 1.2 copy-start.13
  93.8 16.4 %copy-start.15 = (f32[3,8,64,128]{3,2,1,0:T(8,128)}, f32[3,8,64,128]{3,2,1,0:T(8,128)S(1)}, u32[]{:S(2)}) copy-start(f32[3,8,64,128]{3,2,1,0:T(8,128)S(1)} %get-tuple-element.47.osave) | copy-start | bytes 2359300
  111.0 29.6 %copy-start.17 = (f32[256,768]{1,0:T(8,128)}, f32[256,768]{1,0:T(8,128)S(1)}, u32[]{:S(2)}) copy-start(f32[256,768]{1,0:T(8,128)S(1)} %get-tuple-element.128) | copy-start | bytes 2359300
  127.4 0.9 copy-start.21
  128.7 4.2 %copy-start.29 = (f32[256,3072]{1,0:T(8,128)S(1)}, f32[256,3072]{1,0:T(8,128)}, u32[]{:S(2)}) copy-start(f32[256,3072]{1,0:T(8,128)} %get-tuple-element.115) | copy-start | bytes 9437188
  131.2 7.5 %slice-start = ((s8[4718592]{0:T(1024)(128)(4,1)}), s8[4194304]{0:T(1024)(128)(4,1)S(1)}, s32[]{:S(2)}) async-start(s8[4718592]{0:T(1024)(128)(4,1)} %bitcast.76), calls=%async_computation | async-start | bytes 8388608
  132.9 5.8 %copy-start.23 = (f32[256,768]{1,0:T(8,128)}, f32[256,768]{1,0:T(8,128)S(1)}, u32[]{:S(2)}) copy-start(f32[256,768]{1,0:T(8,128)S(1)} %get-tuple-element.111) | copy-start | bytes 2359300
  132.9 5.8 %slice-start.1 = ((s8[4718592]{0:T(1024)(128)(4,1)}), s8[524288]{0:T(1024)(128)(4,1)S(1)}, s32[]{:S(2)}) async-start(s8[4718592]{0:T(1024)(128)(4,1)} %bitcast.76), calls=%async_computation.1 | async-start | bytes 1048576
  138.7 1.8 copy-start.25
  140.5 14.9 %copy-start.12 = (bf16[3,2048,128]{2,1,0:T(8,128)(2,1)S(1)}, bf16[3,2048,128]{2,1,0:T(8,128)(2,1)}, u32[]{:S(2)}) copy-start(bf16[3,2048,128]{2,1,0:T(8,128)(2,1)} %copy-done.11) | copy-start | bytes 4718596
  140.5 14.9 %copy-start.14 = (bf16[3,128,2048]{2,1,0:T(8,128)(2,1)S(1)}, bf16[3,128,2048]{2,1,0:T(8,128)(2,1)}, u32[]{:S(2)}) copy-start(bf16[3,128,2048]{2,1,0:T(8,128)(2,1)} %copy-done.13) | copy-start | bytes 4718596
  140.6 14.9 %copy-start.16 = (f32[3,8,64,128]{3,2,1,0:T(8,128)S(1)}, f32[3,8,64,128]{3,2,1,0:T(8,128)}, u32[]{:S(2)}) copy-start(f32[3,8,64,128]{3,2,1,0:T(8,128)} %copy-done.15) | copy-start | bytes 2359300
  140.9 14.5 %copy-start.19 = (f32[256,768]{1,0:T(8,128)}, f32[256,768]{1,0:T(8,128)S(1)}, u32[]{:S(2)}) copy-start(f32[256,768]{1,0:T(8,128)S(1)} %get-tuple-element.113) | copy-start | bytes 2359300
  171.1 30.7 %copy-start.22 = (bf16[1,256,768]{2,1,0:T(8,128)(2,1)S(1)}, bf16[1,256,768]{2,1,0:T(8,128)(2,1)}, u32[]{:S(2)}) copy-start(bf16[1,256,768]{2,1,0:T(8,128)(2,1)} %param.37) | copy-start | bytes 1179652
  202.2 5.4 %copy-start.18 = (f32[256,768]{1,0:T(8,128)S(1)}, f32[256,768]{1,0:T(8,128)}, u32[]{:S(2)}) copy-start(f32[256,768]{1,0:T(8,128)} %copy-done.17) | copy-start | bytes 2359300
  202.2 5.3 %copy-start.26 = (bf16[256,3072]{1,0:T(8,128)(2,1)S(1)}, bf16[256,3072]{1,0:T(8,128)(2,1)}, u32[]{:S(2)}) copy-start(bf16[256,3072]{1,0:T(8,128)(2,1)} %copy-done.25) | copy-start | bytes 4718596
  207.6 3.7 %copy-start.20 = (f32[256,768]{1,0:T(8,128)S(1)}, f32[256,768]{1,0:T(8,128)}, u32[]{:S(2)}) copy-start(f32[256,768]{1,0:T(8,128)} %copy-done.19) | copy-start | bytes 2359300
  326.7 1.0 copy-start.4
  327.7 0.7 copy-start.5
  328.4 0.7 copy-start.7
  337.6 4.6 %copy-start.8 = (bf16[192,768]{1,0:T(8,128)(2,1)S(1)}, bf16[192,768]{1,0:T(8,128)(2,1)}, u32[]{:S(2)}) copy-start(bf16[192,768]{1,0:T(8,128)(2,1)} %copy-done.7) | copy-start | bytes 884740
  337.6 5.5 %copy-start.6 = (bf16[192,768]{1,0:T(8,128)(2,1)S(1)}, bf16[192,768]{1,0:T(8,128)(2,1)}, u32[]{:S(2)}) copy-start(bf16[192,768]{1,0:T(8,128)(2,1)} %copy-done.5) | copy-start | bytes 884740
  339.3 5.9 %copy-start.3 = (bf16[768,768]{1,0:T(8,128)(2,1)S(1)}, bf16[768,768]{1,0:T(8,128)(2,1)}, u32[]{:S(2)}) copy-start(bf16[768,768]{1,0:T(8,128)(2,1)} %copy-done.2) | copy-start | bytes 3538948

commit v3 on v2

--- a/solution.py
+++ b/solution.py
@@ -455,99 +455,6 @@
     def _(i):
         fn(pl.ds(pl.multiple_of(i*step,step),step))
 
-def reduce_kernel(chunks, n_in, n_out, *refs):
-    n=len(chunks)
-    ins=refs[:n_in]; outs=refs[n_in:n_in+n_out]
-    scr=refs[n_in+n_out:]
-    loc=scr[0:n]; rc=scr[n:2*n]; ry=scr[2*n:3*n]; rx=scr[3*n:4*n]; cb=scr[4*n:5*n]; rz=scr[5*n:6*n]; res=scr[6*n:7*n]
-    (s_load,s_out,c_s,c_r,y_s,y_r,x_s,x_r,z_s,z_r,g_s,g_r,h_s,h_r)=scr[7*n:]
-    c,f,z,x,y,k=places()
-    sib=(c,y*2+(1-k)); yp=(c,(1-y)*2+k); xp=(z*2+(1-x),f)
-    zp=[(((z+d)%4)*2+x,f) for d in (1,2,3)]
-    bar=pltpu.get_barrier_semaphore()
-    for p in [sib,yp,xp]+zp:
-        pl.semaphore_signal(bar,inc=1,device_id=p,device_id_type=MESH)
-    pl.semaphore_wait(bar,6)
-    def remote(src,dst,ss,rs,dev):
-        return pltpu.make_async_remote_copy(src_ref=src,dst_ref=dst,send_sem=ss,recv_sem=rs,device_id=dev,device_id_type=MESH)
-    def cp_load(i,yy):
-        ii,slab,_,_,_,_=chunks[i]
-        return pltpu.make_async_copy(slab(ins[ii],yy*2+k),loc[i].at[yy],s_load.at[i,yy])
-    def cp_c(i,yy):
-        ii,slab,_,_,_,_=chunks[i]
-        return remote(slab(ins[ii],yy*2+(1-k)),rc[i].at[yy],c_s.at[i,yy],c_r.at[i,yy],sib)
-    def cp_y(i): return remote(loc[i].at[1-y],ry[i],y_s.at[i],y_r.at[i],yp)
-    def xhalf(i,xx):
-        w=chunks[i][5]//2
-        return pl.ds(pl.multiple_of(xx*w,128),w)
-    def zrows(i,zz):
-        r=chunks[i][4]//4
-        return pl.ds(pl.multiple_of(zz*r,r),r)
-    def cp_x(i): return remote(loc[i].at[y,:,xhalf(i,1-x)],rx[i],x_s.at[i],x_r.at[i],xp)
-    def cp_z(i,d): return remote(cb[i].at[zrows(i,(z+d)%4)],rz[i].at[d-1],z_s.at[i,d-1],z_r.at[i,d-1],zp[d-1])
-    def cp_g(i,d): return remote(res[i].at[x,zrows(i,z)],res[i].at[x,zrows(i,z)],g_s.at[i,d-1],g_r.at[i,d-1],zp[d-1])
-    def cp_g_in(i,d):
-        zz=(z+4-d)%4
-        return remote(res[i].at[x,zrows(i,zz)],res[i].at[x,zrows(i,zz)],g_s.at[i,d-1],g_r.at[i,d-1],zp[d-1])
-    def cp_h(i): return remote(res[i].at[x],res[i].at[x],h_s.at[i],h_r.at[i],xp)
-    def cp_h_in(i): return remote(res[i].at[1-x],res[i].at[1-x],h_s.at[i],h_r.at[i],xp)
-    def cp_out(i,xx):
-        _,_,oi,osl,r,w=chunks[i]
-        return pltpu.make_async_copy(res[i].at[xx],osl(outs[oi],xx),s_out.at[i,xx])
-    def start0(i):
-        for yy in (0,1):
-            cp_load(i,yy).start(); cp_c(i,yy).start()
-    def stage1(i):
-        for yy in (0,1):
-            cp_load(i,yy).wait(); cp_c(i,yy).wait()
-        r=chunks[i][4]
-        def go(s):
-            for yy in (0,1):
-                loc[i][yy,s]=(loc[i][yy,s].astype(F32)+rc[i][yy,s].astype(F32)).astype(BF)
-        add_strips(r,go)
-        cp_y(i).start()
-    def stage2(i):
-        cp_y(i).wait()
-        r=chunks[i][4]
-        def go(s):
-            loc[i][y,s]=(loc[i][y,s].astype(F32)+ry[i][s].astype(F32)).astype(BF)
-        add_strips(r,go)
-        cp_x(i).start()
-    def stage3(i):
-        cp_x(i).wait()
-        def go(s):
-            cb[i][s]=(loc[i][y,s,xhalf(i,x)].astype(F32)+rx[i][s].astype(F32)).astype(BF)
-        add_strips(chunks[i][4],go)
-        for d in (1,2,3): cp_z(i,d).start()
-    def stage4(i):
-        for d in (1,2,3): cp_z(i,d).wait()
-        r=chunks[i][4]//4
-        def go(j):
-            o=pl.multiple_of(z*r+j*16,16)
-            s=pl.ds(pl.multiple_of(j*16,16),16)
-            v=cb[i][pl.ds(o,16)].astype(F32)
-            for d in range(3): v=v+rz[i][d,s].astype(F32)
-            res[i][x,pl.ds(o,16)]=v.astype(BF)
-        pl.loop(0,r//16)(go)
-        for d in (1,2,3): cp_g(i,d).start()
-    def stage5(i):
-        for d in (1,2,3):
-            cp_g(i,d).wait_send(); cp_g_in(i,d).wait_recv()
-        cp_h(i).start()
-        cp_out(i,x).start()
-    def stage6(i):
-        cp_h(i).wait_send(); cp_h_in(i).wait_recv()
-        cp_out(i,1-x).start()
-    start0(0); start0(1)
-    stages=[stage1,stage2,stage3,stage4,stage5,stage6]
-    for t in range(n+5):
-        if t+2<n: start0(t+2)
-        for s,st in enumerate(stages):
-            if 0<=t-s<n: st(t-s)
-    for i in range(n):
-        for xx in (0,1): cp_out(i,xx).wait()
-
-
 def remote_copy(src, dst, send, recv, device):
     return pltpu.make_async_remote_copy(
         src_ref=src,
@@ -880,11 +787,12 @@
     scale = HEAD_DIM ** (-0.5)
     span = 1024
     for b in range(16):
-        natural = pl.multiple_of(deal[b] * BLOCK, BLOCK)
+        seq = deal[b] // 8
+        natural = pl.multiple_of((deal[b] % 8) * BLOCK, BLOCK)
         for h in range(3):
             tile = kvg[b // 2, pl.ds((b % 2) * BLOCK, BLOCK), pl.ds(128 * h, 128)]
-            kvn[h, pl.ds(natural, BLOCK), :] = tile
-            kvt[h, :, pl.ds(natural, BLOCK)] = jnp.transpose(tile.astype(jnp.float32)).astype(
+            kvn[h, seq, pl.ds(natural, BLOCK), :] = tile
+            kvt[h, seq, :, pl.ds(natural, BLOCK)] = jnp.transpose(tile.astype(jnp.float32)).astype(
                 jnp.bfloat16
             )
     spread = (pick(z % 2, False, False) * scale).astype(jnp.bfloat16)
@@ -896,14 +804,13 @@
     def _(b):
         dealt = ((b // 2) * 2 + x) * 2 + b % 2
         seq = deal[dealt] // 8
-        start = pl.multiple_of(seq * span, span)
         length = lengths[seq]
         here = pl.ds(pl.multiple_of(b * BLOCK, BLOCK), BLOCK)
         rows = lax.broadcasted_iota(jnp.int32, (span, BLOCK), 0)
         made = []
         for h in range(3):
             scores = jnp.dot(
-                kvn[h, pl.ds(start, span), :],
+                kvn[h, seq],
                 qt[pl.ds(128 * h, 128), here],
                 preferred_element_type=jnp.float32,
             )
@@ -912,7 +819,7 @@
             weights = jnp.exp(scores - top)
             total = jnp.sum(weights, axis=0, keepdims=True)
             mixed = jnp.dot(
-                kvt[h, :, pl.ds(start, span)],
+                kvt[h, seq],
                 weights.astype(jnp.bfloat16),
                 preferred_element_type=jnp.float32,
             )
@@ -934,8 +841,8 @@
             half(4, 256, 256),
             full(3, 8, 64, BLOCK),
             full(3, 8, 8, BLOCK),
-            half(3, 2048, 128),
-            half(3, 128, 2048),
+            half(3, 2, 1024, 128),
+            half(3, 2, 128, 1024),
         ],
         in_specs=smem + vmem_specs(2),
         out_specs=vmem_specs(5),
@@ -944,90 +851,6 @@
         cost_estimate=pl.CostEstimate(flops=2 * 10**9, bytes_accessed=10**7, transcendentals=3 * 10**6),
         name="attention_forward",
     )(deal, lengths, qg, kvg)
-
-
-def attention_back_kernel(
-    deal, lengths, qg, dog, osave, lse, kvn, kvt, dqwin, dkv, qt, dot_t, qd, acc
-):
-    c = lax.axis_index("ctx")
-    z = c // 2
-    x = c % 2
-    scale = HEAD_DIM ** (-0.5)
-    span = 1024
-    spread_q = (pick(z % 2, False, False) * scale).astype(jnp.bfloat16)
-    spread_o = pick(z % 2, True, False).astype(jnp.bfloat16)
-    gather_q = pick(z % 2, False, False).astype(jnp.bfloat16)
-    for part in range(4):
-        lanes = pl.ds(256 * part, 256)
-        qt[:, lanes] = dot_nt(spread_q, qg[part]).astype(jnp.bfloat16)
-        dot_t[:, lanes] = dot_nt(spread_o, dog[part]).astype(jnp.bfloat16)
-        q_rows = dot_nt(qg[part], spread_q).astype(jnp.bfloat16)
-        o_rows = dot_nt(dog[part], spread_o).astype(jnp.bfloat16)
-        for i in range(2):
-            qd[2 * part + i, pl.ds(0, BLOCK), :] = q_rows[i * BLOCK : (i + 1) * BLOCK]
-            qd[2 * part + i, pl.ds(BLOCK, BLOCK), :] = o_rows[i * BLOCK : (i + 1) * BLOCK]
-    for h in range(3):
-        acc[h] = jnp.zeros(acc.shape[1:], jnp.float32)
-
-    @pl.loop(0, 8)
-    def _(b):
-        dealt = ((b // 2) * 2 + x) * 2 + b % 2
-        seq = deal[dealt] // 8
-        start = pl.multiple_of(seq * span, span)
-        length = lengths[seq]
-        here = pl.ds(pl.multiple_of(b * BLOCK, BLOCK), BLOCK)
-        rows = lax.broadcasted_iota(jnp.int32, (span, BLOCK), 0)
-        made = []
-        for h in range(3):
-            lanes = pl.ds(128 * h, 128)
-            part = kvn[h, pl.ds(start, span), :]
-            scores = jnp.dot(part, qt[lanes, here], preferred_element_type=jnp.float32)
-            scores = jnp.where(rows < length, scores, NEG_FILL)
-            probs = jnp.exp(scores - lse[h, b, 0:1, :])
-            upstream = dot_t[lanes, here]
-            grad_probs = jnp.dot(part, upstream, preferred_element_type=jnp.float32)
-            delta = jnp.sum(
-                osave[h, b] * upstream[64:].astype(jnp.float32), axis=0, keepdims=True
-            )
-            grad_scores = (probs * (grad_probs - delta)).astype(jnp.bfloat16)
-            grad_query = jnp.dot(
-                kvt[h, :, pl.ds(start, span)], grad_scores, preferred_element_type=jnp.float32
-            )
-            made.append((jnp.transpose(grad_query) * scale).astype(jnp.bfloat16))
-            both = jnp.concatenate([grad_scores, probs.astype(jnp.bfloat16)], axis=1)
-            acc[h, pl.ds(start, span), :] += jnp.dot(
-                both, qd[b, :, lanes], preferred_element_type=jnp.float32
-            )
-        joined = jnp.concatenate(made, axis=1)
-        dqwin[b // 2, pl.ds(pl.multiple_of((b % 2) * BLOCK, BLOCK), BLOCK), :] = jnp.dot(
-            joined, gather_q, preferred_element_type=jnp.float32
-        ).astype(jnp.bfloat16)
-
-    for b in range(16):
-        natural = pl.multiple_of(deal[b] * BLOCK, BLOCK)
-        for h in range(3):
-            dkv[b // 2, pl.ds((b % 2) * BLOCK, BLOCK), pl.ds(128 * h, 128)] = acc[
-                h, pl.ds(natural, BLOCK), :
-            ].astype(jnp.bfloat16)
-
-
-def attention_backward(deal, lengths, qg, dog, osave, lse, kvn, kvt):
-    smem = [pl.BlockSpec(memory_space=pltpu.SMEM)] * 2
-    return pl.pallas_call(
-        attention_back_kernel,
-        out_shape=[half(4, 256, 256), half(8, 256, 384)],
-        in_specs=smem + vmem_specs(6),
-        out_specs=vmem_specs(2),
-        scratch_shapes=[
-            pltpu.VMEM((384, 1024), jnp.bfloat16),
-            pltpu.VMEM((384, 1024), jnp.bfloat16),
-            pltpu.VMEM((8, 256, 384), jnp.bfloat16),
-            pltpu.VMEM((3, 2048, 128), jnp.float32),
-        ],
-        compiler_params=pltpu.CompilerParams(vmem_limit_bytes=40 * 2**20),
-        cost_estimate=pl.CostEstimate(flops=5 * 10**9, bytes_accessed=10**7, transcendentals=3 * 10**6),
-        name="attention_backward",
-    )(deal, lengths, qg, dog, osave, lse, kvn, kvt)
 
 
 def heads_home_kernel(win, out, got, send, recv, local):
@@ -1062,134 +885,196 @@
     )(win)
 
 
-def heads_away_kernel(rows, out, send, recv, local):
-    c, f, z, x, y, k = places()
-    zt = [(z + d) % 4 for d in (1, 2, 3)]
-    zp = [(item * 2 + x, f) for item in zt]
-    greet(zp)
-
-    def lanes(part):
-        return pl.ds(pl.multiple_of(window_start(part), 128), 256)
-
-    copies = [
-        remote_copy(rows.at[:, lanes(zt[d])], out.at[z], send.at[d], recv.at[d], zp[d])
-        for d in range(3)
-    ]
-    for d in (1, 0, 2):
-        copies[d].start()
-    keep = pltpu.make_async_copy(rows.at[:, lanes(z)], out.at[z], local)
-    keep.start()
-    keep.wait()
-    for item in copies:
-        item.wait()
-
-
-def heads_away(rows):
-    d = pltpu.SemaphoreType.DMA
-    return pl.pallas_call(
-        heads_away_kernel,
-        out_shape=half(4, 256, 256),
-        in_specs=vmem_specs(1),
-        out_specs=pl.BlockSpec(memory_space=pltpu.VMEM),
-        scratch_shapes=[d((3,)), d((3,)), d],
-        compiler_params=pltpu.CompilerParams(collective_id=4, has_side_effects=True, vmem_limit_bytes=16 * 2**20),
-        cost_estimate=pl.CostEstimate(flops=10**6, bytes_accessed=10**7, transcendentals=0),
-        name="heads_away",
-    )(rows)
-
-
-def grads_home_kernel(dqwin, dkv, dq, dkv_out, got_q, theirs, mine, got_kv, q_s, q_r, x_s, x_r, k_s, k_r, l_q, l_k, l_own):
-    c, f, z, x, y, k = places()
-    zt = [(z + d) % 4 for d in (1, 2, 3)]
-    zp = [(item * 2 + x, f) for item in zt]
-    xp = (z * 2 + (1 - x), f)
-    greet([xp] + zp)
-
-    def over_x(i, part):
-        return remote_copy(dkv.at[part * 2 + (1 - x)], theirs.at[i], x_s.at[i], x_r.at[i], xp)
-
-    order = [zt[1], zt[0], zt[2], z]
-    where = [1, 0, 2]
-    for i in range(4):
-        over_x(i, order[i]).start()
-        pltpu.make_async_copy(dkv.at[order[i] * 2 + x], mine.at[i], l_k.at[i]).start()
-
-    def q_copy(d):
-        return remote_copy(dqwin.at[zt[d]], got_q.at[z], q_s.at[d], q_r.at[d], zp[d])
-
-    for d in (1, 0, 2):
-        q_copy(d).start()
-    keep_q = pltpu.make_async_copy(dqwin.at[z], got_q.at[z], l_q)
-    keep_q.start()
-
-    def kv_copy(i):
-        d = where[i]
-        return remote_copy(mine.at[i], got_kv.at[z], k_s.at[d], k_r.at[d], zp[d])
-
-    for i in range(4):
-        over_x(i, order[i]).wait_recv()
-        pltpu.make_async_copy(dkv.at[order[i] * 2 + x], mine.at[i], l_k.at[i]).wait()
-
-        @pl.loop(0, 16)
-        def _(j, i=i):
-            rows = pl.ds(pl.multiple_of(j * 16, 16), 16)
-            mine[i, rows] = (
-                mine[i, rows].astype(jnp.float32) + theirs[i, rows].astype(jnp.float32)
-            ).astype(jnp.bfloat16)
-
-        if i < 3:
-            kv_copy(i).start()
-    own = pltpu.make_async_copy(mine.at[3], got_kv.at[z], l_own)
-    own.start()
-    keep_q.wait()
-    for d in range(3):
-        q_copy(d).wait()
-    dq[...] = lane_windows([got_q[part] for part in range(4)])
-    own.wait()
-    for i in range(3):
-        kv_copy(i).wait()
-    for part in range(4):
-        dkv_out[:, pl.ds(384 * part, 384)] = got_kv[part]
-    for i in range(4):
-        over_x(i, order[i]).wait_send()
-
-
-def grads_home(dqwin, dkv):
-    d = pltpu.SemaphoreType.DMA
-    return pl.pallas_call(
-        grads_home_kernel,
-        out_shape=[half(256, 768), half(256, 1536)],
-        in_specs=vmem_specs(2),
-        out_specs=vmem_specs(2),
-        scratch_shapes=[
-            pltpu.VMEM((4, 256, 256), jnp.bfloat16),
-            pltpu.VMEM((4, 256, 384), jnp.bfloat16),
-            pltpu.VMEM((4, 256, 384), jnp.bfloat16),
-            pltpu.VMEM((4, 256, 384), jnp.bfloat16),
-            d((3,)),
-            d((3,)),
-            d((4,)),
-            d((4,)),
-            d((3,)),
-            d((3,)),
-            d,
-            d((4,)),
-            d,
-        ],
-        compiler_params=pltpu.CompilerParams(collective_id=5, has_side_effects=True, vmem_limit_bytes=24 * 2**20),
-        cost_estimate=pl.CostEstimate(flops=10**7, bytes_accessed=5 * 10**7, transcendentals=0),
-        name="grads_home",
-    )(dqwin, dkv)
-
-
-def reduce_grads(grads):
+class Reducer:
+    def __init__(self, chunks, ins, outs, scr):
+        n = len(chunks)
+        self.chunks, self.ins, self.outs, self.n = chunks, ins, outs, n
+        groups = [scr[n * i : n * (i + 1)] for i in range(8)]
+        self.loc, self.rc, self.ry, self.rx, self.cb, self.rz, self.re, self.res = groups
+        self.sems = scr[8 * n :]
+        c, f, z, x, y, k = places()
+        self.side = jnp.where((z == 1) | (z == 2), 1, 0)
+        self.deep = z // 2
+        self.near = ((z + 1 - 2 * (z % 2)) * 2 + x, f)
+        self.far = ((3 - z) * 2 + x, f)
+        self.z, self.x, self.y, self.k = z, x, y, k
+        self.sib = (c, y * 2 + (1 - k))
+        self.yp = (c, (1 - y) * 2 + k)
+        self.xp = (z * 2 + (1 - x), f)
+
+    def slab(self, i, f):
+        m, slab = self.chunks[i][:2]
+        return slab(self.ins[m], f)
+
+    def load(self, i, yy):
+        sem = self.sems[0].at[i, yy]
+        return pltpu.make_async_copy(self.slab(i, yy * 2 + self.k), self.loc[i].at[yy], sem)
+
+    def core(self, i, yy):
+        src = self.slab(i, yy * 2 + (1 - self.k))
+        send, recv = self.sems[2].at[i, yy], self.sems[3].at[i, yy]
+        return remote_copy(src, self.rc[i].at[yy], send, recv, self.sib)
+
+    def over_y(self, i):
+        send, recv = self.sems[4].at[i], self.sems[5].at[i]
+        return remote_copy(self.loc[i].at[1 - self.y], self.ry[i], send, recv, self.yp)
+
+    def lanes(self, i, xx):
+        wide = self.chunks[i][5] // 2
+        return pl.ds(pl.multiple_of(xx * wide, 128), wide)
+
+    def span(self, i, side, deep=None):
+        high = self.chunks[i][4]
+        if deep is None:
+            return pl.ds(pl.multiple_of(side * (high // 2), high // 2), high // 2)
+        base = side * (high // 2) + deep * (high // 4)
+        return pl.ds(pl.multiple_of(base, high // 4), high // 4)
+
+    def over_x(self, i):
+        src = self.loc[i].at[self.y, :, self.lanes(i, 1 - self.x)]
+        send, recv = self.sems[6].at[i], self.sems[7].at[i]
+        return remote_copy(src, self.rx[i], send, recv, self.xp)
+
+    def to_near(self, i):
+        src = self.cb[i].at[self.span(i, 1 - self.side)]
+        send, recv = self.sems[8].at[i], self.sems[9].at[i]
+        return remote_copy(src, self.rz[i], send, recv, self.near)
+
+    def to_far(self, i):
+        src = self.cb[i].at[self.span(i, self.side, 1 - self.deep)]
+        send, recv = self.sems[10].at[i], self.sems[11].at[i]
+        return remote_copy(src, self.re[i], send, recv, self.far)
+
+    def share_far(self, i, deep):
+        ref = self.res[i].at[self.x, self.span(i, self.side, deep)]
+        send, recv = self.sems[14].at[i], self.sems[15].at[i]
+        return remote_copy(ref, ref, send, recv, self.far)
+
+    def share_near(self, i, side):
+        ref = self.res[i].at[self.x, self.span(i, side)]
+        send, recv = self.sems[16].at[i], self.sems[17].at[i]
+        return remote_copy(ref, ref, send, recv, self.near)
+
+    def share_x(self, i, xx):
+        ref = self.res[i].at[xx]
+        send, recv = self.sems[12].at[i], self.sems[13].at[i]
+        return remote_copy(ref, ref, send, recv, self.xp)
+
+    def out(self, i, xx):
+        m, home = self.chunks[i][2:4]
+        sem = self.sems[1].at[i, xx]
+        return pltpu.make_async_copy(self.res[i].at[xx], home(self.outs[m], xx), sem)
+
+    def start(self, i):
+        for yy in (0, 1):
+            self.core(i, yy).start()
+            self.load(i, yy).start()
+
+    def stage0(self, i):
+        for yy in (0, 1):
+            self.load(i, yy).wait()
+            self.core(i, yy).wait()
+
+        def add(s):
+            for yy in (0, 1):
+                total = self.loc[i][yy, s].astype(jnp.float32) + self.rc[i][yy, s].astype(jnp.float32)
+                self.loc[i][yy, s] = total.astype(jnp.bfloat16)
+
+        add_strips(self.chunks[i][4], add)
+        self.over_y(i).start()
+
+    def stage1(self, i):
+        self.over_y(i).wait()
+
+        def add(s):
+            total = self.loc[i][self.y, s].astype(jnp.float32) + self.ry[i][s].astype(jnp.float32)
+            self.loc[i][self.y, s] = total.astype(jnp.bfloat16)
+
+        add_strips(self.chunks[i][4], add)
+        self.over_x(i).start()
+
+    def stage2(self, i):
+        self.over_x(i).wait()
+        mine = self.lanes(i, self.x)
+
+        def add(s):
+            total = self.loc[i][self.y, s, mine].astype(jnp.float32) + self.rx[i][s].astype(jnp.float32)
+            self.cb[i][s] = total.astype(jnp.bfloat16)
+
+        add_strips(self.chunks[i][4], add)
+        self.to_near(i).start()
+
+    def stage3(self, i):
+        self.to_near(i).wait()
+        high = self.chunks[i][4] // 2
+
+        @pl.loop(0, high // 16)
+        def _(j):
+            own = pl.ds(pl.multiple_of(self.side * high + j * 16, 16), 16)
+            s = pl.ds(pl.multiple_of(j * 16, 16), 16)
+            total = self.cb[i][own].astype(jnp.float32) + self.rz[i][s].astype(jnp.float32)
+            self.cb[i][own] = total.astype(jnp.bfloat16)
+
+        self.to_far(i).start()
+
+    def stage4(self, i):
+        self.to_far(i).wait()
+        high = self.chunks[i][4] // 4
+
+        @pl.loop(0, high // 16)
+        def _(j):
+            base = self.side * (2 * high) + self.deep * high + j * 16
+            own = pl.ds(pl.multiple_of(base, 16), 16)
+            s = pl.ds(pl.multiple_of(j * 16, 16), 16)
+            total = self.cb[i][own].astype(jnp.float32) + self.re[i][s].astype(jnp.float32)
+            self.res[i][self.x, own] = total.astype(jnp.bfloat16)
+
+        self.share_far(i, self.deep).start()
+
+    def stage5(self, i):
+        self.share_far(i, self.deep).wait_send()
+        self.share_far(i, 1 - self.deep).wait_recv()
+        self.share_near(i, self.side).start()
+
+    def stage6(self, i):
+        self.share_near(i, self.side).wait_send()
+        self.share_near(i, 1 - self.side).wait_recv()
+        self.share_x(i, self.x).start()
+        self.out(i, self.x).start()
+
+    def stage7(self, i):
+        self.share_x(i, self.x).wait_send()
+        self.share_x(i, 1 - self.x).wait_recv()
+        self.out(i, 1 - self.x).start()
+
+    def tick(self, t):
+        for lag, stage in (
+            (0, self.stage0),
+            (8, self.stage7),
+            (7, self.stage6),
+            (6, self.stage5),
+            (5, self.stage4),
+            (4, self.stage3),
+            (3, self.stage2),
+            (2, self.stage1),
+        ):
+            if 0 <= t - lag < self.n:
+                stage(t - lag)
+
+    def finish(self):
+        for i in range(self.n):
+            for xx in (0, 1):
+                self.out(i, xx).wait()
+
+
+def reduce_plan(shapes):
     chunks = []
-    for m, item in enumerate(grads):
-        shard = item.shape[0] // 4
+    for m, (rows, width) in enumerate(shapes):
+        shard = rows // 4
         high = min(shard, 192)
-        wide = min(item.shape[1], 768)
+        wide = min(width, 768)
         for i in range(shard // high):
-            for j in range(item.shape[1] // wide):
+            for j in range(width // wide):
 
                 def slab(ref, f, i=i, j=j, shard=shard, high=high, wide=wide):
                     rows = pl.ds(pl.multiple_of(f * shard + i * high, high), high)
@@ -1200,8 +1085,10 @@
                     return ref.at[pl.ds(i * high, high), lanes]
 
                 chunks.append((m, slab, m, home, high, wide))
-    n = len(chunks)
-    count = len(grads)
+    return chunks
+
+
+def reduce_scratch(chunks):
     scratch = []
     for lead, divide_rows, divide_lanes in (
         ((2,), 1, 1),
@@ -1209,27 +1096,354 @@
         ((), 1, 1),
         ((), 1, 2),
         ((), 1, 2),
-        ((3,), 4, 2),
+        ((), 2, 2),
+        ((), 4, 2),
         ((2,), 1, 2),
     ):
         for item in chunks:
             shape = lead + (item[4] // divide_rows, item[5] // divide_lanes)
             scratch.append(pltpu.VMEM(shape, jnp.bfloat16))
-    d = pltpu.SemaphoreType.DMA
-    for lanes in (2, 2, 2, 2, 1, 1, 1, 1, 3, 3, 3, 3, 1, 1):
-        scratch.append(d((n, lanes)) if lanes > 1 else d((n,)))
+    for lanes in (2, 2, 2, 2) + (1,) * 14:
+        shape = (len(chunks), lanes) if lanes > 1 else (len(chunks),)
+        scratch.append(pltpu.SemaphoreType.DMA(shape))
+    return scratch
+
+
+def split_pairs():
+    src = lax.broadcasted_iota(jnp.int32, (256, 256), 0)
+    dst = lax.broadcasted_iota(jnp.int32, (256, 256), 1)
+    piece = src // 64
+    moved = (piece % 2) * 128 + (piece // 2) * 64 + src % 64
+    return jnp.where(moved == dst, 1.0, 0.0).astype(jnp.bfloat16)
+
+
+def dot_tn(left, right):
+    return lax.dot_general(
+        left, right, (((0,), (0,)), ((), ())), preferred_element_type=jnp.float32
+    )
+
+
+def backward_kernel(chunks, *refs):
+    deal, lengths, seqs = refs[:3]
+    refs = refs[1:]
+    (gm, qg_h, os_h, lse_h, kvn_h, kvt_h, tok_h, wq_h, wkv_h, gone_h, gout, gin, gmix) = refs[2:15]
+    small_h = refs[15:22]
+    gtok = refs[22]
+    outs = refs[23:30]
+    (qg, osave, lse, kvn, kvt, tok, wq, wkv, gone) = refs[30:39]
+    small = refs[39:46]
+    gvec = refs[46]
+    (dog, qt, dot_t, qd, acc, dqw, give, theirs, mine, got_q, got_kv, gq, gk, gv, tok_out) = refs[47:62]
+    (load_sem, o_s, o_r, o_l, q_s, q_r, q_l, x_s, x_r, k_s, k_r, k_l, t_l) = refs[62:75]
+    ins = (gout, gin, gmix, gq, gk, gv, gvec)
+    red = Reducer(chunks, ins, outs, refs[75:])
+    c, f, z, x, y, k = places()
+    zt = [(z + d) % 4 for d in (1, 2, 3)]
+    zp = [(item * 2 + x, f) for item in zt]
+    xp = red.xp
+    loads = [
+        pltpu.make_async_copy(src, dst, load_sem.at[i])
+        for i, (src, dst) in enumerate(
+            (
+                (qg_h, qg),
+                (kvn_h, kvn),
+                (kvt_h, kvt),
+                (os_h, osave),
+                (lse_h, lse),
+                (tok_h, tok),
+                (wq_h, wq),
+                (wkv_h, wkv),
+                (gone_h, gone),
+            )
+            + tuple(zip(small_h, small))
+        )
+    ]
+    for item in loads[:5]:
+        item.start()
+    greet([red.sib, red.yp, xp] + zp)
+
+    def window(part):
+        return pl.ds(pl.multiple_of(window_start(part), 128), 256)
+
+    def o_copy(d):
+        return remote_copy(gm.at[:, window(zt[d])], dog.at[z], o_s.at[d], o_r.at[d], zp[d])
+
+    for d in (1, 0, 2):
+        o_copy(d).start()
+    keep_o = pltpu.make_async_copy(gm.at[:, window(z)], dog.at[z], o_l)
+    keep_o.start()
+    for i in range(3):
+        red.start(i)
+    red.tick(0)
+    red.start(3)
+    red.tick(1)
+    red.start(4)
+    for item in loads[5:]:
+        item.start()
+
+    scale = HEAD_DIM ** (-0.5)
+    span = 1024
+    spread_q = (pick(z % 2, False, False) * scale).astype(jnp.bfloat16)
+    spread_o = pick(z % 2, True, False).astype(jnp.bfloat16)
+    gather_q = pick(z % 2, False, False).astype(jnp.bfloat16)
+
+    def place(b):
+        return seqs[((b // 2) * 2 + x) * 2 + b % 2]
+
+    def masked(rows, b, base):
+        later = place(b).astype(jnp.float32)
+        for s in range(2):
+            keep = later if s == 1 else 1.0 - later
+            kept = (rows * keep).astype(jnp.bfloat16)
+            for h in range(3):
+                qd[b, pl.ds(base, BLOCK), pl.ds(256 * h + 128 * s, 128)] = kept[
+                    :, 128 * h : 128 * (h + 1)
+                ]
+
+    loads[0].wait()
+    for part in range(4):
+        qt[:, pl.ds(256 * part, 256)] = dot_nt(spread_q, qg[part]).astype(jnp.bfloat16)
+        rows = dot_nt(qg[part], spread_q)
+        for i in range(2):
+            masked(rows[i * BLOCK : (i + 1) * BLOCK], 2 * part + i, 0)
+    for h in range(3):
+        acc[h] = jnp.zeros(acc.shape[1:], jnp.float32)
+    red.tick(2)
+    red.start(5)
+    keep_o.wait()
+    for d in range(3):
+        o_copy(d).wait()
+    for part in range(4):
+        dot_t[:, pl.ds(256 * part, 256)] = dot_nt(spread_o, dog[part]).astype(jnp.bfloat16)
+        rows = dot_nt(dog[part], spread_o)
+        for i in range(2):
+            masked(rows[i * BLOCK : (i + 1) * BLOCK], 2 * part + i, BLOCK)
+    for item in loads[1:5]:
+        item.wait()
+    red.tick(3)
+    red.start(6)
+
+    def pair(p):
+        key_rows = lax.broadcasted_iota(jnp.int32, (span, BLOCK), 0)
+        made = ([], [])
+        for h in range(3):
+            lanes = pl.ds(128 * h, 128)
+            both = []
+            for i in range(2):
+                b = 2 * p + i
+                seq = place(b)
+                length = lengths[seq]
+                here = pl.ds(pl.multiple_of(b * BLOCK, BLOCK), BLOCK)
+                part = kvn[h, seq]
+                scores = jnp.dot(part, qt[lanes, here], preferred_element_type=jnp.float32)
+                scores = jnp.where(key_rows < length, scores, NEG_FILL)
+                probs = jnp.exp(scores - lse[h, b, 0:1, :])
+                upstream = dot_t[lanes, here]
+                grad_probs = jnp.dot(part, upstream, preferred_element_type=jnp.float32)
+                delta = jnp.sum(
+                    osave[h, b] * upstream[64:].astype(jnp.float32), axis=0, keepdims=True
+                )
+                grad_scores = (probs * (grad_probs - delta)).astype(jnp.bfloat16)
+                grad_query = jnp.dot(
+                    kvt[h, seq], grad_scores, preferred_element_type=jnp.float32
+                )
+                made[i].append((jnp.transpose(grad_query) * scale).astype(jnp.bfloat16))
+                both += [grad_scores, probs.astype(jnp.bfloat16)]
+            right = jnp.concatenate(
+                [qd[2 * p, :, pl.ds(256 * h, 256)], qd[2 * p + 1, :, pl.ds(256 * h, 256)]], axis=0
+            )
+            found = jnp.dot(
+                jnp.concatenate(both, axis=1), right, preferred_element_type=jnp.float32
+            )
+            acc[h, pl.ds(0, 8)] += found[:, :128].reshape(8, BLOCK, 128)
+            acc[h, pl.ds(8, 8)] += found[:, 128:].reshape(8, BLOCK, 128)
+        for i in range(2):
+            dqw[p, pl.ds(i * BLOCK, BLOCK), :] = jnp.dot(
+                jnp.concatenate(made[i], axis=1), gather_q, preferred_element_type=jnp.float32
+            ).astype(jnp.bfloat16)
+
+    pl.loop(0, 3)(pair)
+    red.tick(4)
+    red.start(7)
+    pl.loop(3, 4)(pair)
+
+    def q_copy(d):
+        return remote_copy(dqw.at[zt[d]], got_q.at[z], q_s.at[d], q_r.at[d], zp[d])
+
+    for d in (1, 0, 2):
+        q_copy(d).start()
+    keep_q = pltpu.make_async_copy(dqw.at[z], got_q.at[z], q_l)
+    keep_q.start()
+    order = [zt[1], zt[0], zt[2], z]
+    where = [1, 0, 2]
+
+    def over_x(i):
+        return remote_copy(give.at[i], theirs.at[i], x_s.at[i], x_r.at[i], xp)
+
+    def collect(out, i, part, xx):
+        for j in range(2):
+            natural = deal[(part * 2 + xx) * 2 + j]
+            for h in range(3):
+                out[i, pl.ds(j * BLOCK, BLOCK), pl.ds(128 * h, 128)] = acc[
+                    h, natural
+                ].astype(jnp.bfloat16)
+
+    for i in range(4):
+        collect(give, i, order[i], 1 - x)
+        over_x(i).start()
+    red.tick(5)
+    red.start(8)
+    for i in range(4):
+        collect(mine, i, order[i], x)
+
+    def kv_copy(i):
+        d = where[i]
+        return remote_copy(mine.at[i], got_kv.at[z], k_s.at[d], k_r.at[d], zp[d])
+
+    for i in range(4):
+        over_x(i).wait_recv()
+
+        @pl.loop(0, 16)
+        def _(j, i=i):
+            rows = pl.ds(pl.multiple_of(j * 16, 16), 16)
+            mine[i, rows] = (
+                mine[i, rows].astype(jnp.float32) + theirs[i, rows].astype(jnp.float32)
+            ).astype(jnp.bfloat16)
+
+        if i < 3:
+            kv_copy(i).start()
+        if i == 1:
+            red.tick(6)
+    keep_kv = pltpu.make_async_copy(mine.at[3], got_kv.at[z], k_l)
+    keep_kv.start()
+    keep_q.wait()
+    for d in range(3):
+        q_copy(d).wait()
+    for item in loads[5:]:
+        item.wait()
+    dq = lane_windows([got_q[part] for part in range(4)])
+    tokens = tok[...]
+    gq[...] = dot_tn(tokens, dq).astype(jnp.bfloat16)
+    red.start(9)
+    total = gone[...] + dot_nt(dq, wq[...])
+    red.tick(7)
+    keep_kv.wait()
+    for i in range(3):
+        kv_copy(i).wait()
+    split = split_pairs()
+    keys, values = [], []
+    for part in range(4):
+        block = got_kv[part]
+        total = total + dot_nt(block, wkv[:, pl.ds(384 * part, 384)])
+    joined = jnp.concatenate([got_kv[part] for part in range(4)], axis=1)
+    for i in range(6):
+        apart = jnp.dot(
+            joined[:, 256 * i : 256 * (i + 1)], split, preferred_element_type=jnp.float32
+        ).astype(jnp.bfloat16)
+        keys.append(apart[:, :128])
+        values.append(apart[:, 128:])
+    dk = jnp.concatenate(keys, axis=1)
+    dv = jnp.concatenate(values, axis=1)
+    gk[...] = dot_tn(tokens, dk).astype(jnp.bfloat16)
+    red.start(10)
+    gv[...] = dot_tn(tokens, dv).astype(jnp.bfloat16)
+    red.start(11)
+    q_bias = jnp.sum(dq.astype(jnp.float32), axis=0, keepdims=True)
+    v_bias = jnp.sum(dv.astype(jnp.float32), axis=0, keepdims=True)
+    line = lax.broadcasted_iota(jnp.int32, (16, 256), 0)
+    lines = [q_bias, v_bias] + [item[...] for item in small[:6]]
+    for part in range(4):
+        lanes = slice(window_start(part), window_start(part) + 256)
+        top = jnp.zeros((16, 256), jnp.float32)
+        for i, item in enumerate(lines):
+            top = jnp.where(line == i, item[:, lanes], top)
+        for i in range(3):
+            base = 768 * part + 256 * i
+            top = jnp.where(line == 8 + i, small[6][:, base : base + 256], top)
+        gvec[pl.ds(64 * part, 16), :] = top.astype(jnp.bfloat16)
+        gvec[pl.ds(64 * part + 16, 48), :] = jnp.zeros((48, 256), jnp.bfloat16)
+    red.start(12)
+    tok_out[...] = total
+    keep_tok = pltpu.make_async_copy(tok_out, gtok, t_l)
+    keep_tok.start()
+    for t in range(8, red.n + 8):
+        red.tick(t)
+    red.finish()
+    keep_tok.wait()
+    for i in range(4):
+        over_x(i).wait_send()
+
+
+def backward(deal, lengths, seqs, gm, qg, osave, lse, kvn, kvt, tok, wq, wkv, gone, gout, gin, gmix, small):
+    chunks = reduce_plan(
+        [gout.shape, gin.shape, gmix.shape, (768, 768), (768, 768), (768, 768), (256, 256)]
+    )
+    bf, f32, d = jnp.bfloat16, jnp.float32, pltpu.SemaphoreType.DMA
+    v = pltpu.VMEM
+    scratch = [
+        v((4, 256, 256), bf),
+        v((3, 8, 64, BLOCK), f32),
+        v((3, 8, 8, BLOCK), f32),
+        v((3, 2, 1024, 128), bf),
+        v((3, 2, 128, 1024), bf),
+        v((256, 768), bf),
+        v((768, 768), bf),
+        v((768, 1536), bf),
+        v((256, 768), f32),
+    ]
+    scratch += [v(item.shape, f32) for item in small]
+    scratch += [
+        v((256, 256), bf),
+        v((4, 256, 256), bf),
+        v((384, 1024), bf),
+        v((384, 1024), bf),
+        v((8, 256, 768), bf),
+        v((3, 16, BLOCK, 128), f32),
+        v((4, 256, 256), bf),
+        v((4, 256, 384), bf),
+        v((4, 256, 384), bf),
+        v((4, 256, 384), bf),
+        v((4, 256, 256), bf),
+        v((4, 256, 384), bf),
+        v((768, 768), bf),
+        v((768, 768), bf),
+        v((768, 768), bf),
+        v((256, 768), f32),
+        d((16,)),
+        d((3,)),
+        d((3,)),
+        d,
+        d((3,)),
+        d((3,)),
+        d,
+        d((4,)),
+        d((4,)),
+        d((3,)),
+        d((3,)),
+        d,
+        d,
+    ]
     return pl.pallas_call(
-        functools.partial(reduce_kernel, chunks, count, count),
-        out_shape=[half(item.shape[0] // 4, item.shape[1]) for item in grads],
-        in_specs=any_specs(count),
-        out_specs=any_specs(count),
-        scratch_shapes=scratch,
+        functools.partial(backward_kernel, chunks),
+        out_shape=[
+            full(256, 768),
+            half(768, 768),
+            half(192, 3072),
+            half(192, 768),
+            half(192, 768),
+            half(192, 768),
+            half(192, 768),
+            half(64, 256),
+        ],
+        in_specs=[pl.BlockSpec(memory_space=pltpu.SMEM)] * 3 + any_specs(20),
+        out_specs=any_specs(8),
+        scratch_shapes=scratch + reduce_scratch(chunks),
         compiler_params=pltpu.CompilerParams(
-            collective_id=1, has_side_effects=True, vmem_limit_bytes=48 * 2**20
+            collective_id=6, has_side_effects=True, vmem_limit_bytes=60 * 2**20
         ),
-        cost_estimate=pl.CostEstimate(flops=10**7, bytes_accessed=10**8, transcendentals=0),
-        name="grad_reduce",
-    )(*grads)
+        cost_estimate=pl.CostEstimate(flops=10**10, bytes_accessed=10**8, transcendentals=3 * 10**6),
+        name="backward",
+    )(deal, lengths, seqs, gm, qg, osave, lse, kvn, kvt, tok, wq, wkv, gone, gout, gin, gmix, *small)
 
 
 def body_fast(
@@ -1342,85 +1556,66 @@
     grad_mixed = jnp.einsum(
         "te,de->td", grad_attn, mix_weight, preferred_element_type=jnp.float32
     ).astype(jnp.bfloat16)
-    grad_groups = heads_away(grad_mixed)
-    query_back, pairs_back = attention_backward(
+    (
+        grad_inputs,
+        sum_outer,
+        sum_inner,
+        sum_mix,
+        sum_query,
+        sum_key,
+        sum_value,
+        sum_small,
+    ) = backward(
         deal_row,
         lengths,
+        deal_row // 8,
+        grad_mixed,
         query_groups,
-        grad_groups,
         out_heads,
         log_totals,
         pairs,
         pairs_turned,
-    )
-    grad_query, grad_pairs = grads_home(query_back, pairs_back)
-    grad_query_weight = jnp.einsum(
-        "td,te->de", inputs, grad_query, preferred_element_type=jnp.float32
-    )
-    grad_pair_weight = jnp.einsum(
-        "td,te->de", inputs, grad_pairs, preferred_element_type=jnp.float32
-    )
-    grad_query_bias = jnp.sum(grad_query.astype(jnp.float32), axis=0)
-    grad_pair_bias = jnp.sum(grad_pairs.astype(jnp.float32), axis=0)
-    grad_value_bias = grad_pair_bias.reshape(HEADS, 2, HEAD_DIM)[:, 1, :].reshape(width)
-    grad_inputs = (
-        grad_one
-        + jnp.einsum("te,de->td", grad_query, query_weight, preferred_element_type=jnp.float32)
-        + jnp.einsum("te,de->td", grad_pairs, pair_weights, preferred_element_type=jnp.float32)
-    )
-    rows = jnp.stack(
+        inputs,
+        query_weight,
+        pair_weights,
+        grad_one,
+        to_half(grad_outer),
+        to_half(grad_inner),
+        to_half(grad_mix),
         [
-            grad_query_bias,
-            grad_value_bias,
-            grad_mix_bias,
-            grad_gain_one,
-            grad_shift_one,
-            grad_outer_bias,
-            grad_gain_two,
-            grad_shift_two,
-        ]
-    )
-    shares = jnp.transpose(rows.reshape(8, 4, part), (1, 0, 2)).reshape(4, 2 * width)
-    shares = jnp.concatenate([shares, grad_inner_bias.reshape(4, width)], axis=1)
-    shares = jnp.pad(shares, ((0, 0), (0, 64 * 256 - 3 * width))).reshape(256, 256)
-    (
-        sum_query,
-        sum_pairs,
-        sum_mix,
-        sum_inner,
-        sum_outer,
-        sum_small,
-    ) = reduce_grads(
-        [
-            to_half(grad_query_weight),
-            to_half(grad_pair_weight),
-            to_half(grad_mix),
-            to_half(grad_inner),
-            to_half(grad_outer),
-            to_half(shares),
-        ]
-    )
-    sum_pairs = sum_pairs.astype(jnp.float32).reshape(part, HEADS, 2, HEAD_DIM)
-    flat = sum_small.astype(jnp.float32).reshape(-1)[: 3 * width]
-    small = flat[: 2 * width].reshape(8, part)
+            item.reshape(1, -1)
+            for item in (
+                grad_mix_bias,
+                grad_gain_one,
+                grad_shift_one,
+                grad_outer_bias,
+                grad_gain_two,
+                grad_shift_two,
+                grad_inner_bias,
+            )
+        ],
+    )
+    sum_small = sum_small.astype(jnp.float32)
+    small = jnp.where(odd, sum_small[:8, HEAD_DIM:], sum_small[:8, :part])
+    others = small[2:]
     return (
         layer_out.astype(jnp.bfloat16)[None],
         grad_inputs[None],
         sum_query.astype(jnp.float32),
-        sum_pairs[:, :, 0, :].reshape(part, width),
-        sum_pairs[:, :, 1, :].reshape(part, width),
+        sum_key.astype(jnp.float32),
+        sum_value.astype(jnp.float32),
         sum_mix.astype(jnp.float32),
         small[0],
         small[1],
-        small[2],
-        small[3],
-        small[4],
+        others[0],
+        others[1],
+        others[2],
         sum_inner.astype(jnp.float32),
-        flat[2 * width :],
+        sum_small[8:11].reshape(width),
         sum_outer.astype(jnp.float32),
-        small[5],
-        small[6],
-        small[7],
+        others[3],
+        others[4],
+        others[5],
     )
 
 

time: 351 us -> 313 us (0.89)
  Pallas kernels: 263 us -> 236 us
  local copies, waits for them, and re-layouts: 23.9 us -> 17.1 us
  matrix products: 41.9 us -> 35.3 us
    pallas_call x4 -> x1, Pallas kernels: 171 us -> 144 us  [backward(): pl.pallas_call(functools.partial(backward_kernel, chunks), out_shape=[ful...]
    unnamed x75 -> x65, local copies, waits for them, and re-layouts: 16.2 us -> 8.03 us
    dot_general x4 -> x0, matrix products: 7.74 us -> none  [the longest x1 3.35 us: body_fast(): jnp.einsum('te,de->td', grad_pairs, pair_weights, preferred_element_type=...]
where the time goes in v3:
time: 313 us
  Pallas kernels  236 us (75%)
  matrix products  35.3 us (11%)
  other arithmetic  23 us (7%)
  local copies, waits for them, and re-layouts  17.1 us (5%)
    pallas_call x1, Pallas kernels, backward(): pl.pallas_call(functools.partial(backward_kernel, chunks), out_shape=[ful...  144 us
    pallas_call x1, Pallas kernels, gather_project(): pl.pallas_call(gather_project_kernel, out_shape=[half(4, rows, 256), half...  64.2 us
    pallas_call x1, Pallas kernels, heads_home(): pl.pallas_call(heads_home_kernel, out_shape=half(256, 768), in_specs=vmem...  16.4 us
    dot_general x1, matrix products, body_fast(): jnp.dot(normal_half, inner_weight, preferred_element_type=jnp.float32)  11.6 us
    pallas_call x1, Pallas kernels, attention_forward(): pl.pallas_call(attention_kernel, out_shape=[half(4, 256, 256), full(3, 8,...  11.2 us
    unnamed x65, local copies, waits for them, and re-layouts  8.03 us
    dot_general x1, matrix products, body_fast(): jnp.einsum('td,fd->tf', grad_branch, outer_weight, preferred_element_type...  6.91 us
    another operation x9, other arithmetic  6.28 us

profile of v3, /device:TPU:0, one launch (start us, length us, event | category | flops | bytes accessed | tf_op | source)
XLA Modules:
  0.0 312.6 jit_solution(6745210575276838586)
XLA Ops:
  0.7 0.8 select_convert_fusion
  1.5 0.7 convert.54
  2.4 0.7 convert.61
  3.1 0.7 convert.55
  3.8 0.7 convert.56
  4.5 0.7 convert.57
  5.2 0.7 convert.58
  5.9 0.7 convert.59
  6.6 0.7 convert.60
  7.3 1.2 copy.38
  8.6 1.2 copy.39
  10.3 2.0 convert_element_type.106.refs_4_
  13.0 0.7 copy-done
  13.8 64.2 %gather_project.1 = (bf16[4,256,256]{2,1,0:T(8,128)(2,1)S(1)}, bf16[8,256,384]{2,1,0:T(8,128)(2,1)S(1)}, bf16[768,768]{1,0:T(8,128)(2,1)S(1)}, bf16[768,1536]{1,...) custom-call(bf16[256,768]{1,0:T(8,128)(2,1)S(1)} %bitcast.54, ...), custom_call_target="tpu_custom_call" | custom-call | flops 1000000000 | bytes 100000000 | tf_op jit(solution)/shard_map/gather_project/pallas_call | solution.py:732
  78.0 1.0 copy-done.2
  79.1 11.2 %attention_forward.1 = (bf16[4,256,256]{2,1,0:T(8,128)(2,1)S(1)}, f32[3,8,64,128]{3,2,1,0:T(8,128)S(1)}, f32[3,8,8,128]{3,2,1,0:T(8,128)S(1)}, bf16[3,2,1024,128...) custom-call(s32[16]{0:T(128)S(1)} %bitcast.56, s32[2]{0:T(128)S(1)} %bitcast.58, ...), custom_call_target="tpu_custom_call" | custom-call | flops 2000000000 | bytes 10000000 | tf_op jit(solution)/shard_map/attention_forward/pallas_call | solution.py:838
  90.3 1.1 copy-done.6
  91.4 1.2 copy-done.7
  92.6 16.4 %heads_home.1 = bf16[256,768]{1,0:T(8,128)(2,1)S(1)} custom-call(bf16[4,256,256]{2,1,0:T(8,128)(2,1)S(1)} %get-tuple-element.40.win), custom_call_target="tpu_custom_call" | custom-call | flops 1000000 | bytes 10000000 | tf_op jit(solution)/shard_map/heads_home/pallas_call | solution.py:876
  109.0 0.6 slice_reduce_fusion.1
  110.7 11.6 %multiply_convert_fusion = (bf16[256,3072]{1,0:T(8,128)(2,1)}, f32[256,3072]{1,0:T(8,128)}, f32[256,3072]{1,0:T(8,128)}) fusion(f32[3072]{0:T(1024)S(1)} %add.107, bf16[768,3072]{1,0:T(8,128)(2,1)} %get-tuple-element.43, f32[256,768]{1,0:T(8,128)S(1)} %get-tuple-element.88, f32[768]{0:T(1024)S(1)} %add.104, f32[768]{0:T(1024)S(1)} %mul.127, ...), kind=kOutput, calls=%fused_computation.7 | convolution fusion | flops 1260847104 | bytes 13389824 | tf_op jit(solution)/shard_map/dot_general | solution.py:1525
  122.3 0.7 add.111
  123.0 4.4 %fusion.32 = (f32[256]{0:T(256)S(1)}, f32[256,768]{1,0:T(8,128)S(1)}) fusion(f32[768]{0:T(1024)} %add.111, bf16[256,3072]{1,0:T(8,128)(2,1)} %get-tuple-element.76, bf16[3072,768]{1,0:T(8,128)(2,1)} %get-tuple-element.44, f32[768]{0:T(1024)S(1)} %add.104, f32[768]{0:T(1024)S(1)} %mul.127, f32[256]{0:T(256)} %copy-done.27, ...), kind=kOutput, calls=%fused_computation.81 | convolution fusion | flops 1209335552 | bytes 7876608 | tf_op jit(solution)/shard_map/dot_general | solution.py:1530
  128.2 0.8 mul.136
  129.0 1.7 fusion.16
  131.3 1.4 add.115
  132.6 2.0 convert_reduce_fusion.2
  134.6 6.9 %convert_reduce_fusion = (f32[3072]{0:T(1024)}, bf16[256,3072]{1,0:T(8,128)(2,1)S(1)}) fusion(f32[256,3072]{1,0:T(8,128)} %get-tuple-element.77, f32[256,3072]{1,0:T(8,128)} %get-tuple-element.89, bf16[3072,768]{1,0:T(8,128)(2,1)} %get-tuple-element.44, f32[256,768]{1,0:T(8,128)S(1)} %get-tuple-element.73), kind=kOutput, calls=%fused_computation.5 | convolution fusion | flops 1220736000 | bytes 13381632 | tf_op jit(solution)/shard_map/td,fd->tf/dot_general | solution.py:1541
  141.6 1.7 multiply_reduce_fusion
  143.6 1.5 convolution_convert_fusion.2.refs_15_
  145.1 3.8 %convolution_convert_fusion.refs_14_ = bf16[768,3072]{1,0:T(8,128)(2,1)} fusion(bf16[256,3072]{1,0:T(8,128)(2,1)S(1)} %get-tuple-element.94, f32[256,768]{1,0:T(8,128)S(1)} %get-tuple-element.88, f32[768]{0:T(1024)S(1)} %add.104, f32[768]{0:T(1024)S(1)} %mul.127, f32[256]{0:T(256)S(1)} %copy-done.28, f32[256]{0:T(256)S(1)} %copy-done.24), kind=kOutput, calls=%fused_computation | convolution fusion | flops 1211301888 | bytes 7086080 | tf_op jit(solution)/shard_map/td,tf->df/dot_general | solution.py:1546
  148.9 3.6 %convolution_convert_fusion.1.refs_13_ = bf16[3072,768]{1,0:T(8,128)(2,1)} fusion(bf16[256,3072]{1,0:T(8,128)(2,1)S(1)} %copy-done.11, f32[256,768]{1,0:T(8,128)S(1)} %get-tuple-element.73), kind=kOutput, calls=%fused_computation.1 | convolution fusion | flops 1210515456 | bytes 7077888 | tf_op jit(solution)/shard_map/tf,td->fd/dot_general | solution.py:1540
  152.5 1.3 convolution_convert_fusion.3.refs_3_
  153.8 0.6 reshape.115.refs_16_
  154.3 0.6 reshape.116.refs_17_
  155.5 0.6 reshape.118.refs_19_
  156.1 0.6 reshape.119.refs_20_
  156.8 0.6 reshape.120.refs_21_
  157.9 144.5 %backward.1 = (f32[256,768]{1,0:T(8,128)}, bf16[768,768]{1,0:T(8,128)(2,1)}, bf16[192,3072]{1,0:T(8,128)(2,1)}, bf16[192,768]{1,0:T(8,128)(2,1)}, bf16[192,768]{...) custom-call(s32[16]{0:T(128)} %bitcast.55, s32[2]{0:T(128)} %bitcast.57, ...), custom_call_target="tpu_custom_call" | custom-call | flops 10000000000 | bytes 100000000 | tf_op jit(solution)/shard_map/backward/pallas_call | solution.py:1426
  302.4 3.1 convert_element_type.129
  305.5 1.6 convert_element_type.130
  307.0 0.9 convert_element_type.124
  307.9 0.9 convert_element_type.125
  308.7 0.9 convert_element_type.126
  309.6 0.9 convert_element_type.127
  310.5 0.6 fusion.30
  311.2 0.6 reshape.122
  311.8 0.9 copy.45
  (107 shorter events, 5.6 us)
Async XLA Ops:
  10.3 2.4 copy-start.13
  10.3 2.5 copy-start.16
  10.3 2.6 copy-start.17
  12.7 1.1 copy-start
  12.8 66.2 %copy-start.4 = (s32[1,16]{1,0:T(1,128)S(1)}, s32[1,16]{1,0:T(1,128)}, u32[]{:S(2)}) copy-start(s32[1,16]{1,0:T(1,128)} %param.21) | copy-start | bytes 196
  12.8 66.2 %copy-start.5 = (s32[1,2]{1,0:T(1,128)S(1)}, s32[1,2]{1,0:T(1,128)}, u32[]{:S(2)}) copy-start(s32[1,2]{1,0:T(1,128)} %param.20) | copy-start | bytes 28
  78.0 1.0 copy-start.2
  79.0 11.2 %copy-start.1 = (bf16[768,1536]{1,0:T(8,128)(2,1)}, bf16[768,1536]{1,0:T(8,128)(2,1)S(1)}, u32[]{:S(2)}) copy-start(bf16[768,1536]{1,0:T(8,128)(2,1)S(1)} %get-tuple-element.50.refs_11_) | copy-start | bytes 7077892
  79.0 11.2 %copy-start.3 = (bf16[4,256,256]{2,1,0:T(8,128)(2,1)}, bf16[4,256,256]{2,1,0:T(8,128)(2,1)S(1)}, u32[]{:S(2)}) copy-start(bf16[4,256,256]{2,1,0:T(8,128)(2,1)S(1)} %get-tuple-element.38.qg.refs_4_) | copy-start | bytes 1572868
  90.2 1.2 copy-start.6
  91.4 1.2 copy-start.7
  92.6 16.4 %copy-start.8 = (f32[3,8,64,128]{3,2,1,0:T(8,128)}, f32[3,8,64,128]{3,2,1,0:T(8,128)S(1)}, u32[]{:S(2)}) copy-start(f32[3,8,64,128]{3,2,1,0:T(8,128)S(1)} %get-tuple-element.45.refs_5_) | copy-start | bytes 2359300
  92.6 16.4 %copy-start.9 = (f32[3,8,8,128]{3,2,1,0:T(8,128)}, f32[3,8,8,128]{3,2,1,0:T(8,128)S(1)}, u32[]{:S(2)}) copy-start(f32[3,8,8,128]{3,2,1,0:T(8,128)S(1)} %get-tuple-element.46.refs_6_) | copy-start | bytes 294916
  110.3 12.7 %copy-start.23 = (f32[256]{0:T(256)}, f32[256]{0:T(256)S(1)}, u32[]{:S(2)}) copy-start(f32[256]{0:T(256)S(1)} %broadcast_multiply_fusion.5) | copy-start | bytes 3076
  110.6 11.8 %copy-start.27 = (f32[256]{0:T(256)}, f32[256]{0:T(256)S(1)}, u32[]{:S(2)}) copy-start(f32[256]{0:T(256)S(1)} %add_rsqrt_fusion.1) | copy-start | bytes 3076
  123.0 6.0 %copy-start.12 = (bf16[1,256,768]{2,1,0:T(8,128)(2,1)S(1)}, bf16[1,256,768]{2,1,0:T(8,128)(2,1)}, u32[]{:S(2)}) copy-start(bf16[1,256,768]{2,1,0:T(8,128)(2,1)} %param.37) | copy-start | bytes 1179652
  127.4 0.8 copy-start.25
  132.6 8.9 %slice-start = ((s8[4718592]{0:T(1024)(128)(4,1)}), s8[4194304]{0:T(1024)(128)(4,1)S(1)}, s32[]{:S(2)}) async-start(s8[4718592]{0:T(1024)(128)(4,1)} %bitcast.71), calls=%async_computation | async-start | bytes 8388608
  134.6 6.9 %copy-start.24 = (f32[256]{0:T(256)S(1)}, f32[256]{0:T(256)}, u32[]{:S(2)}) copy-start(f32[256]{0:T(256)} %copy-done.23) | copy-start | bytes 3076
  134.6 6.9 %copy-start.28 = (f32[256]{0:T(256)S(1)}, f32[256]{0:T(256)}, u32[]{:S(2)}) copy-start(f32[256]{0:T(256)} %copy-done.27) | copy-start | bytes 3076
  134.6 6.9 %slice-start.1 = ((s8[4718592]{0:T(1024)(128)(4,1)}), s8[524288]{0:T(1024)(128)(4,1)S(1)}, s32[]{:S(2)}) async-start(s8[4718592]{0:T(1024)(128)(4,1)} %bitcast.71), calls=%async_computation.1 | async-start | bytes 1048576
  143.6 8.9 %copy-start.10 = (f32[256,768]{1,0:T(8,128)}, f32[256,768]{1,0:T(8,128)S(1)}, u32[]{:S(2)}) copy-start(f32[256,768]{1,0:T(8,128)S(1)} %get-tuple-element.75.refs_12_) | copy-start | bytes 2359300
  145.1 3.8 %copy-start.11 = (bf16[256,3072]{1,0:T(8,128)(2,1)S(1)}, bf16[256,3072]{1,0:T(8,128)(2,1)}, u32[]{:S(2)}) copy-start(bf16[256,3072]{1,0:T(8,128)(2,1)} %get-tuple-element.76) | copy-start | bytes 4718596
  148.9 7.2 %copy-start.26 = (f32[768]{0:T(1024)S(1)}, f32[768]{0:T(1024)}, u32[]{:S(2)}) copy-start(f32[768]{0:T(1024)} %get-tuple-element.61) | copy-start | bytes 9220
  302.3 3.1 copy-start.14
  302.3 4.7 %copy-start.21 = (bf16[192,768]{1,0:T(8,128)(2,1)S(1)}, bf16[192,768]{1,0:T(8,128)(2,1)}, u32[]{:S(2)}) copy-start(bf16[192,768]{1,0:T(8,128)(2,1)} %get-tuple-element.52) | copy-start | bytes 884740
  302.4 5.5 %copy-start.20 = (bf16[192,768]{1,0:T(8,128)(2,1)S(1)}, bf16[192,768]{1,0:T(8,128)(2,1)}, u32[]{:S(2)}) copy-start(bf16[192,768]{1,0:T(8,128)(2,1)} %get-tuple-element.53) | copy-start | bytes 884740
  305.4 3.3 %copy-start.19 = (bf16[192,768]{1,0:T(8,128)(2,1)S(1)}, bf16[192,768]{1,0:T(8,128)(2,1)}, u32[]{:S(2)}) copy-start(bf16[192,768]{1,0:T(8,128)(2,1)} %get-tuple-element.54) | copy-start | bytes 884740
  305.4 4.2 %copy-start.18 = (bf16[192,768]{1,0:T(8,128)(2,1)S(1)}, bf16[192,768]{1,0:T(8,128)(2,1)}, u32[]{:S(2)}) copy-start(bf16[192,768]{1,0:T(8,128)(2,1)} %get-tuple-element.55) | copy-start | bytes 884740
  305.4 5.0 %copy-start.22 = (bf16[64,256]{1,0:T(8,128)(2,1)S(1)}, bf16[64,256]{1,0:T(8,128)(2,1)}, u32[]{:S(2)}) copy-start(bf16[64,256]{1,0:T(8,128)(2,1)} %get-tuple-element.56) | copy-start | bytes 98308
  305.4 6.3 %copy-start.15 = (f32[256,768]{1,0:T(8,128)S(1)}, f32[256,768]{1,0:T(8,128)}, u32[]{:S(2)}) copy-start(f32[256,768]{1,0:T(8,128)} %get-tuple-element.51) | copy-start | bytes 2359300

commit v4 on v3

--- a/solution.py
+++ b/solution.py
@@ -496,219 +496,6 @@
     )
 
 
-GATHER_PIECES = ((True, 3), (True, 3), (False, 1), (True, 2), (False, 4))
-
-
-def gather_project_kernel(*refs):
-    (tok, wq_s, wkv_s, wo_s, win_s, wout_s, vec_s) = refs[:7]
-    (qg, kvg, wq_o, wkv_o, wo_o, win_o, wout_o, vec_o) = refs[7:15]
-    (wq_v, wkv_v, vec_v, send_kv, send_q) = refs[15:20]
-    (own_s, own_r, own_l, y_s, y_r, cy_s, cy_r, x_s, x_r, cx_s, cx_r) = refs[20:31]
-    (v_s, v_r, v_l, zk_s, zk_r, zq_s, zq_r, f_s, f_r, l_sem, out_sem) = refs[31:]
-    c, f, z, x, y, k = places()
-    sib = (c, y * 2 + (1 - k))
-    yp = (c, (1 - y) * 2 + k)
-    diag = (c, (1 - y) * 2 + (1 - k))
-    xp = (z * 2 + (1 - x), f)
-    zt = [(z + d) % 4 for d in (1, 2, 3)]
-    zp = [(item * 2 + x, f) for item in zt]
-    greet([sib, yp, diag, xp] + zp)
-    shards = (wq_s, wkv_s, wo_s, win_s, wout_s)
-    wholes = (wq_v, wkv_v, wo_o, win_o, wout_o)
-    fy = (1 - y) * 2 + k
-    first = [0]
-    for split, count in GATHER_PIECES:
-        first.append(first[-1] + count)
-
-    def piece_rows(u, j, xx):
-        rows = shards[u].shape[0]
-        split, count = GATHER_PIECES[u]
-        if split:
-            size = rows // 2 // count
-            return xx * (rows // 2) + j * size, size
-        size = rows // count
-        return j * size, size
-
-    def own(u):
-        rows = shards[u].shape[0]
-        there = wholes[u].at[at_row(f * rows, rows)]
-        return remote_copy(shards[u], there, own_s.at[u], own_r.at[u], sib)
-
-    def keep(u):
-        rows = shards[u].shape[0]
-        there = wholes[u].at[at_row(f * rows, rows)]
-        return pltpu.make_async_copy(shards[u], there, own_l.at[u])
-
-    def over_y(u, j):
-        rows = shards[u].shape[0]
-        start, size = piece_rows(u, j, x)
-        i = first[u] + j
-        return remote_copy(
-            shards[u].at[at_row(start, size)],
-            wholes[u].at[at_row(f * rows + start, size)],
-            y_s.at[i],
-            y_r.at[i],
-            yp,
-        )
-
-    def landed(u, j, xx):
-        rows = shards[u].shape[0]
-        start, size = piece_rows(u, j, xx)
-        return wholes[u].at[at_row(fy * rows + start, size)]
-
-    def relay_core(u, j):
-        i = first[u] + j
-        ref = landed(u, j, x)
-        return remote_copy(ref, ref, cy_s.at[i], cy_r.at[i], sib)
-
-    def relay_x(u, j):
-        i = first[u] + j
-        ref = landed(u, j, x)
-        return remote_copy(ref, ref, x_s.at[i], x_r.at[i], xp)
-
-    def relay_core_x(u, j):
-        i = first[u] + j
-        ref = landed(u, j, 1 - x)
-        return remote_copy(ref, ref, cx_s.at[i], cx_r.at[i], sib)
-
-    def on_y(u, j):
-        over_y(u, j).wait_recv()
-        relay_core(u, j).start()
-        if GATHER_PIECES[u][0]:
-            relay_x(u, j).start()
-
-    def on_x(u, j):
-        if GATHER_PIECES[u][0]:
-            relay_x(u, j).wait_recv()
-            relay_core_x(u, j).start()
-
-    def finish_recv(u):
-        own(u).wait_recv()
-        keep(u).wait()
-        for j in range(GATHER_PIECES[u][1]):
-            relay_core(u, j).wait_recv()
-            if GATHER_PIECES[u][0]:
-                relay_core_x(u, j).wait_recv()
-
-    def finish_send(u):
-        own(u).wait_send()
-        for j in range(GATHER_PIECES[u][1]):
-            over_y(u, j).wait_send()
-            relay_core(u, j).wait_send()
-            if GATHER_PIECES[u][0]:
-                relay_x(u, j).wait_send()
-                relay_core_x(u, j).wait_send()
-
-    def vec(i, device):
-        return remote_copy(vec_s, vec_v.at[f], v_s.at[i], v_r.at[i], device)
-
-    for j in range(3):
-        over_y(1, j).start()
-        over_y(0, j).start()
-    vec_peers = (sib, yp, diag)
-    for i in range(3):
-        vec(i, vec_peers[i]).start()
-    vec_keep = pltpu.make_async_copy(vec_s, vec_v.at[f], v_l)
-    vec_keep.start()
-    for u in (1, 0):
-        own(u).start()
-        keep(u).start()
-    for j in range(3):
-        on_y(1, j)
-        on_y(0, j)
-    for u in (3, 2, 4):
-        for j in range(GATHER_PIECES[u][1]):
-            over_y(u, j).start()
-        own(u).start()
-        keep(u).start()
-    for j in range(3):
-        on_x(1, j)
-        on_x(0, j)
-    for i in range(3):
-        vec(i, vec_peers[i]).wait_recv()
-    vec_keep.wait()
-    finish_recv(1)
-
-    def z_kv(d):
-        return remote_copy(
-            send_kv.at[zt[d]], kvg.at[c], zk_s.at[d], zk_r.at[d], zp[d]
-        )
-
-    def z_kv_in(d):
-        slot = ((z + 3 - d) % 4) * 2 + x
-        return remote_copy(kvg.at[slot], kvg.at[slot], zk_s.at[d], zk_r.at[d], zp[d])
-
-    def z_q(d):
-        return remote_copy(
-            send_q.at[zt[d]], qg.at[z], zq_s.at[d], zq_r.at[d], zp[d]
-        )
-
-    def own_x():
-        return remote_copy(send_kv.at[z], kvg.at[c], f_s.at[3], f_r.at[3], xp)
-
-    def fwd_x(d):
-        slot = ((z + 3 - d) % 4) * 2 + x
-        return remote_copy(kvg.at[slot], kvg.at[slot], f_s.at[d], f_r.at[d], xp)
-
-    inputs = tok[...]
-    for part in range(4):
-        lanes = pl.ds(384 * part, 384)
-        made = jnp.dot(inputs, wkv_v[:, lanes], preferred_element_type=jnp.float32)
-        made = made + vec_v[part, 1:2, :].astype(jnp.float32)
-        send_kv[part] = made.astype(jnp.bfloat16)
-    own_x().start()
-    for d in (1, 0, 2):
-        z_kv(d).start()
-    keep_kv = pltpu.make_async_copy(send_kv.at[z], kvg.at[c], l_sem.at[0])
-    keep_kv.start()
-    finish_recv(0)
-    bias = lane_windows([vec_v[part, 0:1, 0:256].astype(jnp.float32) for part in range(4)])
-    for part in range(4):
-        lanes = pl.ds(window_start(part), 256)
-        made = jnp.dot(inputs, wq_v[:, lanes], preferred_element_type=jnp.float32)
-        made = made + bias[:, window_start(part) : window_start(part) + 256]
-        send_q[part] = made.astype(jnp.bfloat16)
-    for d in (1, 0, 2):
-        z_q(d).start()
-    keep_q = pltpu.make_async_copy(send_q.at[z], qg.at[z], l_sem.at[1])
-    keep_q.start()
-    outs = (
-        pltpu.make_async_copy(wq_v, wq_o, out_sem.at[0]),
-        pltpu.make_async_copy(wkv_v, wkv_o, out_sem.at[1]),
-        pltpu.make_async_copy(vec_v, vec_o, out_sem.at[2]),
-    )
-    for item in outs:
-        item.start()
-    on_y(3, 0)
-    z_kv_in(0).wait_recv()
-    fwd_x(0).start()
-    z_kv_in(2).wait_recv()
-    fwd_x(2).start()
-    z_kv_in(1).wait_recv()
-    fwd_x(1).start()
-    on_y(3, 1)
-    on_y(2, 0)
-    on_x(3, 0)
-    on_x(3, 1)
-    for j in range(4):
-        on_y(4, j)
-    for d in range(3):
-        z_kv(d).wait_send()
-        z_q(d).wait()
-        fwd_x(d).wait()
-    own_x().wait()
-    keep_kv.wait()
-    keep_q.wait()
-    for u in (2, 3, 4):
-        finish_recv(u)
-    for u in range(5):
-        finish_send(u)
-    for i in range(3):
-        vec(i, vec_peers[i]).wait_send()
-    for item in outs:
-        item.wait()
-
-
 def any_specs(count):
     return [pl.BlockSpec(memory_space=pl.ANY)] * count
 
@@ -723,44 +510,6 @@
 
 def full(*shape):
     return jax.ShapeDtypeStruct(shape, jnp.float32)
-
-
-def gather_project(tok, wq, wkv, wo, win, wout, vec):
-    rows, width = tok.shape
-    d = pltpu.SemaphoreType.DMA
-    count = sum(item[1] for item in GATHER_PIECES)
-    return pl.pallas_call(
-        gather_project_kernel,
-        out_shape=[
-            half(4, rows, 256),
-            half(8, rows, 384),
-            half(width, width),
-            half(width, 2 * width),
-            half(width, width),
-            half(width, win.shape[1]),
-            half(4 * wout.shape[0], width),
-            half(4, 16, 384),
-        ],
-        in_specs=vmem_specs(1) + any_specs(6),
-        out_specs=any_specs(8),
-        scratch_shapes=[
-            pltpu.VMEM((width, width), jnp.bfloat16),
-            pltpu.VMEM((width, 2 * width), jnp.bfloat16),
-            pltpu.VMEM((4, 16, 384), jnp.bfloat16),
-            pltpu.VMEM((4, rows, 384), jnp.bfloat16),
-            pltpu.VMEM((4, rows, 256), jnp.bfloat16),
-            d((5,)),
-            d((5,)),
-            d((5,)),
-        ]
-        + [d((count,))] * 8
-        + [d((3,)), d((3,)), d, d((3,)), d((3,)), d((3,)), d((3,)), d((4,)), d((4,)), d((2,)), d((3,))],
-        compiler_params=pltpu.CompilerParams(
-            collective_id=2, has_side_effects=True, vmem_limit_bytes=40 * 2**20
-        ),
-        cost_estimate=pl.CostEstimate(flops=10**9, bytes_accessed=10**8, transcendentals=0),
-        name="gather_project",
-    )(tok, wq, wkv, wo, win, wout, vec)
 
 
 def pick(parity, value_side, by_window):
@@ -778,111 +527,6 @@
     return lax.dot_general(
         left, right, (((1,), (1,)), ((), ())), preferred_element_type=jnp.float32
     )
-
-
-def attention_kernel(deal, lengths, qg, kvg, owin, osave, lse, kvn, kvt, qt):
-    c = lax.axis_index("ctx")
-    z = c // 2
-    x = c % 2
-    scale = HEAD_DIM ** (-0.5)
-    span = 1024
-    for b in range(16):
-        seq = deal[b] // 8
-        natural = pl.multiple_of((deal[b] % 8) * BLOCK, BLOCK)
-        for h in range(3):
-            tile = kvg[b // 2, pl.ds((b % 2) * BLOCK, BLOCK), pl.ds(128 * h, 128)]
-            kvn[h, seq, pl.ds(natural, BLOCK), :] = tile
-            kvt[h, seq, :, pl.ds(natural, BLOCK)] = jnp.transpose(tile.astype(jnp.float32)).astype(
-                jnp.bfloat16
-            )
-    spread = (pick(z % 2, False, False) * scale).astype(jnp.bfloat16)
-    gather = pick(z % 2, True, False).astype(jnp.bfloat16)
-    for part in range(4):
-        qt[:, pl.ds(256 * part, 256)] = dot_nt(spread, qg[part]).astype(jnp.bfloat16)
-
-    @pl.loop(0, 8)
-    def _(b):
-        dealt = ((b // 2) * 2 + x) * 2 + b % 2
-        seq = deal[dealt] // 8
-        length = lengths[seq]
-        here = pl.ds(pl.multiple_of(b * BLOCK, BLOCK), BLOCK)
-        rows = lax.broadcasted_iota(jnp.int32, (span, BLOCK), 0)
-        made = []
-        for h in range(3):
-            scores = jnp.dot(
-                kvn[h, seq],
-                qt[pl.ds(128 * h, 128), here],
-                preferred_element_type=jnp.float32,
-            )
-            scores = jnp.where(rows < length, scores, NEG_FILL)
-            top = jnp.max(scores, axis=0, keepdims=True)
-            weights = jnp.exp(scores - top)
-            total = jnp.sum(weights, axis=0, keepdims=True)
-            mixed = jnp.dot(
-                kvt[h, seq],
-                weights.astype(jnp.bfloat16),
-                preferred_element_type=jnp.float32,
-            )
-            mixed = mixed / total
-            osave[h, b] = mixed[64:]
-            lse[h, b] = jnp.broadcast_to(top + jnp.log(total), (8, BLOCK))
-            made.append(jnp.transpose(mixed).astype(jnp.bfloat16))
-        joined = jnp.concatenate(made, axis=1)
-        owin[b // 2, pl.ds(pl.multiple_of((b % 2) * BLOCK, BLOCK), BLOCK), :] = jnp.dot(
-            joined, gather, preferred_element_type=jnp.float32
-        ).astype(jnp.bfloat16)
-
-
-def attention_forward(deal, lengths, qg, kvg):
-    smem = [pl.BlockSpec(memory_space=pltpu.SMEM)] * 2
-    return pl.pallas_call(
-        attention_kernel,
-        out_shape=[
-            half(4, 256, 256),
-            full(3, 8, 64, BLOCK),
-            full(3, 8, 8, BLOCK),
-            half(3, 2, 1024, 128),
-            half(3, 2, 128, 1024),
-        ],
-        in_specs=smem + vmem_specs(2),
-        out_specs=vmem_specs(5),
-        scratch_shapes=[pltpu.VMEM((384, 1024), jnp.bfloat16)],
-        compiler_params=pltpu.CompilerParams(vmem_limit_bytes=40 * 2**20),
-        cost_estimate=pl.CostEstimate(flops=2 * 10**9, bytes_accessed=10**7, transcendentals=3 * 10**6),
-        name="attention_forward",
-    )(deal, lengths, qg, kvg)
-
-
-def heads_home_kernel(win, out, got, send, recv, local):
-    c, f, z, x, y, k = places()
-    zt = [(z + d) % 4 for d in (1, 2, 3)]
-    zp = [(item * 2 + x, f) for item in zt]
-    greet(zp)
-    copies = [
-        remote_copy(win.at[zt[d]], got.at[z], send.at[d], recv.at[d], zp[d]) for d in range(3)
-    ]
-    for d in (1, 0, 2):
-        copies[d].start()
-    keep = pltpu.make_async_copy(win.at[z], got.at[z], local)
-    keep.start()
-    keep.wait()
-    for item in copies:
-        item.wait()
-    out[...] = lane_windows([got[part] for part in range(4)])
-
-
-def heads_home(win):
-    d = pltpu.SemaphoreType.DMA
-    return pl.pallas_call(
-        heads_home_kernel,
-        out_shape=half(256, 768),
-        in_specs=vmem_specs(1),
-        out_specs=pl.BlockSpec(memory_space=pltpu.VMEM),
-        scratch_shapes=[pltpu.VMEM((4, 256, 256), jnp.bfloat16), d((3,)), d((3,)), d],
-        compiler_params=pltpu.CompilerParams(collective_id=3, has_side_effects=True, vmem_limit_bytes=16 * 2**20),
-        cost_estimate=pl.CostEstimate(flops=10**6, bytes_accessed=10**7, transcendentals=0),
-        name="heads_home",
-    )(win)
 
 
 class Reducer:
@@ -1126,17 +770,17 @@
 def backward_kernel(chunks, *refs):
     deal, lengths, seqs = refs[:3]
     refs = refs[1:]
-    (gm, qg_h, os_h, lse_h, kvn_h, kvt_h, tok_h, wq_h, wkv_h, gone_h, gout, gin, gmix) = refs[2:15]
-    small_h = refs[15:22]
-    gtok = refs[22]
-    outs = refs[23:30]
-    (qg, osave, lse, kvn, kvt, tok, wq, wkv, gone) = refs[30:39]
-    small = refs[39:46]
-    gvec = refs[46]
-    (dog, qt, dot_t, qd, acc, dqw, give, theirs, mine, got_q, got_kv, gq, gk, gv, tok_out) = refs[47:62]
-    (load_sem, o_s, o_r, o_l, q_s, q_r, q_l, x_s, x_r, k_s, k_r, k_l, t_l) = refs[62:75]
+    (gm, qg_h, os_h, lse_h, kvn_h, kvt_h, tok_h, wq_h, wk_h, wv_h, gone_h, gout, gin, gmix) = refs[2:16]
+    small_h = refs[16:23]
+    gtok = refs[23]
+    outs = refs[24:31]
+    (qg, osave, lse, kvn, kvt, tok, wq, wk, wv, gone) = refs[31:41]
+    small = refs[41:48]
+    gvec = refs[48]
+    (dog, qt, dot_t, qd, acc, dqw, give, theirs, mine, got_q, got_kv, gq, gk, gv, tok_out) = refs[49:64]
+    (load_sem, o_s, o_r, o_l, q_s, q_r, q_l, x_s, x_r, k_s, k_r, k_l, t_l) = refs[64:77]
     ins = (gout, gin, gmix, gq, gk, gv, gvec)
-    red = Reducer(chunks, ins, outs, refs[75:])
+    red = Reducer(chunks, ins, outs, refs[77:])
     c, f, z, x, y, k = places()
     zt = [(z + d) % 4 for d in (1, 2, 3)]
     zp = [(item * 2 + x, f) for item in zt]
@@ -1152,7 +796,8 @@
                 (lse_h, lse),
                 (tok_h, tok),
                 (wq_h, wq),
-                (wkv_h, wkv),
+                (wk_h, wk),
+                (wv_h, wv),
                 (gone_h, gone),
             )
             + tuple(zip(small_h, small))
@@ -1332,9 +977,6 @@
         kv_copy(i).wait()
     split = split_pairs()
     keys, values = [], []
-    for part in range(4):
-        block = got_kv[part]
-        total = total + dot_nt(block, wkv[:, pl.ds(384 * part, 384)])
     joined = jnp.concatenate([got_kv[part] for part in range(4)], axis=1)
     for i in range(6):
         apart = jnp.dot(
@@ -1363,7 +1005,7 @@
         gvec[pl.ds(64 * part, 16), :] = top.astype(jnp.bfloat16)
         gvec[pl.ds(64 * part + 16, 48), :] = jnp.zeros((48, 256), jnp.bfloat16)
     red.start(12)
-    tok_out[...] = total
+    tok_out[...] = total + dot_nt(dk, wk[...]) + dot_nt(dv, wv[...])
     keep_tok = pltpu.make_async_copy(tok_out, gtok, t_l)
     keep_tok.start()
     for t in range(8, red.n + 8):
@@ -1374,7 +1016,7 @@
         over_x(i).wait_send()
 
 
-def backward(deal, lengths, seqs, gm, qg, osave, lse, kvn, kvt, tok, wq, wkv, gone, gout, gin, gmix, small):
+def backward(deal, lengths, seqs, gm, qg, osave, lse, kvn, kvt, tok, wq, wk, wv, gone, gout, gin, gmix, small):
     chunks = reduce_plan(
         [gout.shape, gin.shape, gmix.shape, (768, 768), (768, 768), (768, 768), (256, 256)]
     )
@@ -1388,7 +1030,8 @@
         v((3, 2, 128, 1024), bf),
         v((256, 768), bf),
         v((768, 768), bf),
-        v((768, 1536), bf),
+        v((768, 768), bf),
+        v((768, 768), bf),
         v((256, 768), f32),
     ]
     scratch += [v(item.shape, f32) for item in small]
@@ -1409,7 +1052,7 @@
         v((768, 768), bf),
         v((768, 768), bf),
         v((256, 768), f32),
-        d((16,)),
+        d((17,)),
         d((3,)),
         d((3,)),
         d,
@@ -1435,7 +1078,7 @@
             half(192, 768),
             half(64, 256),
         ],
-        in_specs=[pl.BlockSpec(memory_space=pltpu.SMEM)] * 3 + any_specs(20),
+        in_specs=[pl.BlockSpec(memory_space=pltpu.SMEM)] * 3 + any_specs(21),
         out_specs=any_specs(8),
         scratch_shapes=scratch + reduce_scratch(chunks),
         compiler_params=pltpu.CompilerParams(
@@ -1443,7 +1086,443 @@
         ),
         cost_estimate=pl.CostEstimate(flops=10**10, bytes_accessed=10**8, transcendentals=3 * 10**6),
         name="backward",
-    )(deal, lengths, seqs, gm, qg, osave, lse, kvn, kvt, tok, wq, wkv, gone, gout, gin, gmix, *small)
+    )(deal, lengths, seqs, gm, qg, osave, lse, kvn, kvt, tok, wq, wk, wv, gone, gout, gin, gmix, *small)
+
+
+GATHER_PIECES = ((True, 3), (True, 3), (True, 3), (True, 2), (False, 1), (False, 4))
+
+
+def forward_kernel(*refs):
+    deal, lengths = refs[:2]
+    tok_h = refs[2]
+    shard_h = refs[3:9]
+    small_h = refs[9:18]
+    (attn_o, qg_o, kvn_o, kvt_o, os_o, lse_o, wq_o, wk_o, wv_o, wo_o, win_o, wout_o, vec_o, bin_o) = refs[18:32]
+    tok = refs[32]
+    stage = refs[33:39]
+    small = refs[39:48]
+    (wk_v, wv_v, wq_v, sh_in, sh_mix, sh_out, vec_v, vec_all, bin_all) = refs[48:57]
+    (send_kv, send_q, kvg, qg, kvn, kvt, qt, owin, got, osave, lse, attn) = refs[57:69]
+    (load_sem, own_s, own_r, own_l, y_s, y_r, cy_s, cy_r, x_s, x_r, cx_s, cx_r) = refs[69:81]
+    (v_s, v_r, zk_s, zk_r, zq_s, zq_r, f_s, f_r, l_sem, o_s, o_r, out_sem) = refs[81:]
+    c, f, z, x, y, k = places()
+    sib = (c, y * 2 + (1 - k))
+    yp = (c, (1 - y) * 2 + k)
+    diag = (c, (1 - y) * 2 + (1 - k))
+    xp = (z * 2 + (1 - x), f)
+    zt = [(z + d) % 4 for d in (1, 2, 3)]
+    zp = [(item * 2 + x, f) for item in zt]
+    loads = [
+        pltpu.make_async_copy(src, dst, load_sem.at[i])
+        for i, (src, dst) in enumerate(
+            tuple(zip(shard_h[:3], stage[:3]))
+            + ((tok_h, tok),)
+            + tuple(zip(small_h, small))
+            + tuple(zip(shard_h[3:], stage[3:]))
+        )
+    ]
+    for item in loads:
+        item.start()
+    greet([sib, yp, diag, xp] + zp)
+    wholes = (wk_v, wv_v, wq_v, win_o, wo_o, wout_o)
+    fy = (1 - y) * 2 + k
+    first = [0]
+    for split, count in GATHER_PIECES:
+        first.append(first[-1] + count)
+    heights = [item.shape[0] for item in stage]
+    shards = [wholes[u].at[at_row(f * heights[u], heights[u])] for u in range(3)]
+    shards += [sh_in, sh_mix, sh_out]
+
+    def piece_rows(u, j, xx):
+        rows = heights[u]
+        split, count = GATHER_PIECES[u]
+        if split:
+            size = rows // 2 // count
+            return xx * (rows // 2) + j * size, size
+        size = rows // count
+        return j * size, size
+
+    def home(u):
+        return wholes[u].at[at_row(f * heights[u], heights[u])]
+
+    def own(u):
+        return remote_copy(shards[u], home(u), own_s.at[u], own_r.at[u], sib)
+
+    def keep(u):
+        return pltpu.make_async_copy(shards[u], home(u), own_l.at[u])
+
+    def over_y(u, j):
+        start, size = piece_rows(u, j, x)
+        i = first[u] + j
+        if u < 3:
+            src = wholes[u].at[at_row(f * heights[u] + start, size)]
+        else:
+            src = shards[u].at[at_row(start, size)]
+        dst = wholes[u].at[at_row(f * heights[u] + start, size)]
+        return remote_copy(src, dst, y_s.at[i], y_r.at[i], yp)
+
+    def landed(u, j, xx):
+        start, size = piece_rows(u, j, xx)
+        return wholes[u].at[at_row(fy * heights[u] + start, size)]
+
+    def relay_core(u, j):
+        i = first[u] + j
+        ref = landed(u, j, x)
+        return remote_copy(ref, ref, cy_s.at[i], cy_r.at[i], sib)
+
+    def relay_x(u, j):
+        i = first[u] + j
+        ref = landed(u, j, x)
+        return remote_copy(ref, ref, x_s.at[i], x_r.at[i], xp)
+
+    def relay_core_x(u, j):
+        i = first[u] + j
+        ref = landed(u, j, 1 - x)
+        return remote_copy(ref, ref, cx_s.at[i], cx_r.at[i], sib)
+
+    def pieces(u):
+        return range(GATHER_PIECES[u][1])
+
+    def on_y(u, j):
+        over_y(u, j).wait_recv()
+        if GATHER_PIECES[u][0]:
+            relay_x(u, j).start()
+        relay_core(u, j).start()
+
+    def on_x(u, j):
+        if GATHER_PIECES[u][0]:
+            relay_x(u, j).wait_recv()
+            relay_core_x(u, j).start()
+
+    def finish_recv(u):
+        own(u).wait_recv()
+        if u >= 3:
+            keep(u).wait()
+        for j in pieces(u):
+            relay_core(u, j).wait_recv()
+            if GATHER_PIECES[u][0]:
+                relay_core_x(u, j).wait_recv()
+
+    def finish_send(u):
+        own(u).wait_send()
+        for j in pieces(u):
+            over_y(u, j).wait_send()
+            relay_core(u, j).wait_send()
+            if GATHER_PIECES[u][0]:
+                relay_x(u, j).wait_send()
+                relay_core_x(u, j).wait_send()
+
+    def cast(u):
+        rows = heights[u]
+
+        @pl.loop(0, rows // 32)
+        def _(i):
+            here = pl.ds(pl.multiple_of(i * 32, 32), 32)
+            value = stage[u][here, :].astype(jnp.bfloat16)
+            if u < 3:
+                wholes[u][at_row(f * rows + i * 32, 32), :] = value
+            else:
+                shards[u][here, :] = value
+
+    for u in range(3):
+        loads[u].wait()
+        cast(u)
+        for j in pieces(u):
+            over_y(u, j).start()
+        own(u).start()
+    for item in loads[4:13]:
+        item.wait()
+    line = lax.broadcasted_iota(jnp.int32, (16, 192), 0)
+    rows = jnp.zeros((16, 192), jnp.float32)
+    for i in range(8):
+        rows = jnp.where(line == i, small[i][...], rows)
+    widen = jnp.where(
+        lax.broadcasted_iota(jnp.int32, (192, 256), 0)
+        == lax.broadcasted_iota(jnp.int32, (192, 256), 1),
+        1.0,
+        0.0,
+    ).astype(jnp.bfloat16)
+    rows = jnp.dot(rows.astype(jnp.bfloat16), widen, preferred_element_type=jnp.float32)
+    line = lax.broadcasted_iota(jnp.int32, (16, 256), 0)
+    for i in range(3):
+        rows = jnp.where(line == 8 + i, small[8][:, 256 * i : 256 * (i + 1)], rows)
+    vec_v[f] = rows.astype(jnp.bfloat16)
+
+    def vec(i, device):
+        return remote_copy(vec_v.at[f], vec_v.at[f], v_s.at[i], v_r.at[i], device)
+
+    vec_peers = (sib, yp, diag)
+    vec_from = (y * 2 + (1 - k), fy, (1 - y) * 2 + (1 - k))
+
+    def vec_in(i):
+        slot = vec_v.at[vec_from[i]]
+        return remote_copy(slot, slot, v_s.at[i], v_r.at[i], vec_peers[i])
+
+    for i in range(3):
+        vec(i, vec_peers[i]).start()
+    for n, u in enumerate((3, 4, 5)):
+        loads[13 + n].wait()
+        cast(u)
+        own(u).start()
+        keep(u).start()
+    for i in range(3):
+        vec_in(i).wait_recv()
+    from_lane = lax.broadcasted_iota(jnp.int32, (256, 768), 0)
+    to_lane = lax.broadcasted_iota(jnp.int32, (256, 768), 1)
+    spread = jnp.zeros((16, 768), jnp.float32)
+    for p in range(4):
+        place = jnp.where((from_lane < 192) & (to_lane == from_lane + 192 * p), 1.0, 0.0)
+        spread = spread + jnp.dot(
+            vec_v[p], place.astype(jnp.bfloat16), preferred_element_type=jnp.float32
+        )
+        for i in range(3):
+            base = 768 * p + 256 * i
+            bin_all[:, base : base + 256] = vec_v[p].astype(jnp.float32)[8 + i : 9 + i, :]
+    vec_all[...] = spread
+    for u in range(3):
+        for j in pieces(u):
+            on_y(u, j)
+    for u in (3, 4, 5):
+        for j in pieces(u):
+            over_y(u, j).start()
+    loads[3].wait()
+    inputs = tok[...]
+
+    def z_kv(d):
+        return remote_copy(
+            send_kv.at[zt[d]], kvg.at[pl.ds(2 * c, 2)], zk_s.at[d], zk_r.at[d], zp[d]
+        )
+
+    def arrived(d):
+        return kvg.at[pl.ds((((z + 3 - d) % 4) * 2 + x) * 2, 2)]
+
+    def z_kv_in(d):
+        return remote_copy(arrived(d), arrived(d), zk_s.at[d], zk_r.at[d], zp[d])
+
+    def own_x():
+        return remote_copy(send_kv.at[z], kvg.at[pl.ds(2 * c, 2)], f_s.at[3], f_r.at[3], xp)
+
+    def fwd_x(d):
+        return remote_copy(arrived(d), arrived(d), f_s.at[d], f_r.at[d], xp)
+
+    def z_q(d):
+        return remote_copy(send_q.at[zt[d]], qg.at[z], zq_s.at[d], zq_r.at[d], zp[d])
+
+    for u in (0, 1):
+        for j in pieces(u):
+            on_x(u, j)
+        finish_recv(u)
+    keys = jnp.dot(inputs, wk_v[...], preferred_element_type=jnp.float32).astype(jnp.bfloat16)
+    values = jnp.dot(inputs, wv_v[...], preferred_element_type=jnp.float32) + vec_all[1:2, :]
+    values = values.astype(jnp.bfloat16)
+    join = split_pairs()
+    for i in range(6):
+        lanes = slice(128 * i, 128 * (i + 1))
+        pair = jnp.concatenate([keys[:, lanes], values[:, lanes]], axis=1)
+        pair = dot_nt(pair, join).astype(jnp.bfloat16)
+        for t in (2 * i, 2 * i + 1):
+            tile = pair[:, 128 * (t % 2) : 128 * (t % 2) + 128]
+            send_kv[t // 3, :, :, pl.ds(128 * (t % 3), 128)] = tile.reshape(2, BLOCK, 128)
+    own_x().start()
+    for d in (1, 0, 2):
+        z_kv(d).start()
+    keep_kv = pltpu.make_async_copy(send_kv.at[z], kvg.at[pl.ds(2 * c, 2)], l_sem.at[0])
+    keep_kv.start()
+    for j in pieces(2):
+        on_x(2, j)
+    finish_recv(2)
+    query = jnp.dot(inputs, wq_v[...], preferred_element_type=jnp.float32) + vec_all[0:1, :]
+    query = query.astype(jnp.bfloat16)
+    for part in range(4):
+        send_q[part] = query[:, window_start(part) : window_start(part) + 256]
+    for d in (1, 0, 2):
+        z_q(d).start()
+    keep_q = pltpu.make_async_copy(send_q.at[z], qg.at[z], l_sem.at[1])
+    keep_q.start()
+    outs = [
+        pltpu.make_async_copy(src, dst, out_sem.at[i])
+        for i, (src, dst) in enumerate(
+            (
+                (wq_v, wq_o),
+                (wk_v, wk_o),
+                (wv_v, wv_o),
+                (vec_all, vec_o),
+                (bin_all, bin_o),
+                (qg, qg_o),
+                (kvn, kvn_o),
+                (kvt, kvt_o),
+                (osave, os_o),
+                (lse, lse_o),
+                (attn, attn_o),
+            )
+        )
+    ]
+    for item in outs[:5]:
+        item.start()
+    natural = []
+    for n in range(16):
+        slot = jnp.int32(0)
+        for b in range(1, 16):
+            slot = jnp.where(deal[b] == n, b, slot)
+        natural.append(slot)
+    z_kv_in(0).wait_recv()
+    fwd_x(0).start()
+    z_kv_in(2).wait_recv()
+    fwd_x(2).start()
+    on_y(3, 0)
+    z_kv_in(1).wait_recv()
+    fwd_x(1).start()
+    on_y(3, 1)
+    keep_q.wait()
+    for d in range(3):
+        z_q(d).wait_recv()
+    outs[5].start()
+    scale = HEAD_DIM ** (-0.5)
+    lift = (pick(z % 2, False, False) * scale).astype(jnp.bfloat16)
+    gather = pick(z % 2, True, False).astype(jnp.bfloat16)
+    for part in range(4):
+        qt[:, pl.ds(256 * part, 256)] = dot_nt(lift, qg[part]).astype(jnp.bfloat16)
+    keep_kv.wait()
+    for d in range(3):
+        fwd_x(d).wait_recv()
+    own_x().wait_recv()
+    on_y(4, 0)
+    for j in pieces(3):
+        on_x(3, j)
+    for n in range(16):
+        for h in range(3):
+            tile = kvg[natural[n], :, pl.ds(128 * h, 128)]
+            here = pl.ds((n % 8) * BLOCK, BLOCK)
+            kvn[h, n // 8, here, :] = tile
+            kvt[h, n // 8, :, here] = jnp.transpose(tile.astype(jnp.float32)).astype(jnp.bfloat16)
+    outs[6].start()
+    outs[7].start()
+    span = 1024
+
+    def o_copy(d):
+        return remote_copy(owin.at[zt[d]], got.at[z], o_s.at[d], o_r.at[d], zp[d])
+
+    def attend(part, i):
+        b = part * 2 + i
+        seq = jnp.where(deal[(part * 2 + x) * 2 + i] >= 8, 1, 0)
+        length = lengths[seq]
+        here = pl.ds(pl.multiple_of(b * BLOCK, BLOCK), BLOCK)
+        key_rows = lax.broadcasted_iota(jnp.int32, (span, BLOCK), 0)
+        made = []
+        for h in range(3):
+            scores = jnp.dot(
+                kvn[h, seq], qt[pl.ds(128 * h, 128), here], preferred_element_type=jnp.float32
+            )
+            scores = jnp.where(key_rows < length, scores, NEG_FILL)
+            top = jnp.max(scores, axis=0, keepdims=True)
+            weights = jnp.exp(scores - top)
+            total = jnp.sum(weights, axis=0, keepdims=True)
+            mixed = jnp.dot(
+                kvt[h, seq], weights.astype(jnp.bfloat16), preferred_element_type=jnp.float32
+            )
+            mixed = mixed / total
+            osave[h, b] = mixed[64:]
+            lse[h, b] = jnp.broadcast_to(top + jnp.log(total), (8, BLOCK))
+            made.append(jnp.transpose(mixed).astype(jnp.bfloat16))
+        owin[part, pl.ds(pl.multiple_of(i * BLOCK, BLOCK), BLOCK), :] = jnp.dot(
+            jnp.concatenate(made, axis=1), gather, preferred_element_type=jnp.float32
+        ).astype(jnp.bfloat16)
+
+    for d in (1, 0, 2, 3):
+        part = zt[d] if d < 3 else z
+        pl.loop(0, 2)(functools.partial(attend, part))
+        if d < 3:
+            o_copy(d).start()
+        on_y(5, {1: 0, 0: 1, 2: 2, 3: 3}[d])
+    keep_o = pltpu.make_async_copy(owin.at[z], got.at[z], l_sem.at[2])
+    keep_o.start()
+    outs[8].start()
+    outs[9].start()
+    keep_o.wait()
+    for d in range(3):
+        o_copy(d).wait_recv()
+    attn[...] = lane_windows([got[part] for part in range(4)])
+    outs[10].start()
+    own_x().wait_send()
+    for d in range(3):
+        z_kv(d).wait_send()
+        z_q(d).wait_send()
+        fwd_x(d).wait_send()
+        o_copy(d).wait_send()
+        vec(d, vec_peers[d]).wait_send()
+    for u in (3, 4, 5):
+        finish_recv(u)
+    for u in range(6):
+        finish_send(u)
+    for item in outs:
+        item.wait()
+
+
+def forward(deal, lengths, tok, shards, small):
+    rows, width = tok.shape
+    bf, f32, d, v = jnp.bfloat16, jnp.float32, pltpu.SemaphoreType.DMA, pltpu.VMEM
+    count = sum(item[1] for item in GATHER_PIECES)
+    wide = shards[3].shape[1]
+    deep = shards[5].shape[0]
+    scratch = [v((rows, width), bf)]
+    scratch += [v(item.shape, f32) for item in shards]
+    scratch += [v(item.shape, f32) for item in small]
+    scratch += [
+        v((width, width), bf),
+        v((width, width), bf),
+        v((width, width), bf),
+        v((width // 4, wide), bf),
+        v((width // 4, width), bf),
+        v((deep, width), bf),
+        v((4, 16, 256), bf),
+        v((16, width), f32),
+        v((1, wide), f32),
+        v((4, 2, BLOCK, 384), bf),
+        v((4, rows, 256), bf),
+        v((16, BLOCK, 384), bf),
+        v((4, rows, 256), bf),
+        v((3, 2, 1024, 128), bf),
+        v((3, 2, 128, 1024), bf),
+        v((384, 1024), bf),
+        v((4, rows, 256), bf),
+        v((4, rows, 256), bf),
+        v((3, 8, 64, BLOCK), f32),
+        v((3, 8, 8, BLOCK), f32),
+        v((rows, width), bf),
+        d((16,)),
+        d((6,)),
+        d((6,)),
+        d((6,)),
+    ]
+    scratch += [d((count,))] * 8
+    scratch += [d((3,))] * 6 + [d((4,)), d((4,)), d((3,)), d((3,)), d((3,)), d((11,))]
+    return pl.pallas_call(
+        forward_kernel,
+        out_shape=[
+            half(rows, width),
+            half(4, rows, 256),
+            half(3, 2, 1024, 128),
+            half(3, 2, 128, 1024),
+            full(3, 8, 64, BLOCK),
+            full(3, 8, 8, BLOCK),
+            half(width, width),
+            half(width, width),
+            half(width, width),
+            half(width, width),
+            half(width, wide),
+            half(4 * deep, width),
+            full(16, width),
+            full(1, wide),
+        ],
+        in_specs=[pl.BlockSpec(memory_space=pltpu.SMEM)] * 2 + any_specs(16),
+        out_specs=any_specs(14),
+        scratch_shapes=scratch,
+        compiler_params=pltpu.CompilerParams(
+            collective_id=2, has_side_effects=True, vmem_limit_bytes=56 * 2**20
+        ),
+        cost_estimate=pl.CostEstimate(flops=10**10, bytes_accessed=10**8, transcendentals=0),
+        name="forward",
+    )(deal, lengths, tok, *shards, *small)
 
 
 def body_fast(
@@ -1471,50 +1550,47 @@
     width = inputs.shape[1]
     part = width // 4
     odd = lax.axis_index("fsdp") % 2 == 1
-    pair_shape = (part, HEADS, HEAD_DIM)
-    pair_weight = jnp.stack(
-        [to_half(w_key).reshape(pair_shape), to_half(w_value).reshape(pair_shape)], axis=2
-    ).reshape(part, 2 * width)
-    query_row = jnp.where(
-        odd, jnp.pad(b_query, (HEAD_DIM, 384 - 256)), jnp.pad(b_query, (0, 384 - 192))
-    )
-    value_heads = b_value.reshape(3, HEAD_DIM)
-    pair_row = jnp.stack([jnp.zeros_like(value_heads), value_heads], axis=1).reshape(384)
-    small = [query_row, pair_row]
-    for item in (b_attn_out, norm1_gain, norm1_bias, b_out, norm2_gain, norm2_bias):
-        small.append(jnp.pad(item, (0, 384 - part)))
-    packed = jnp.concatenate(
-        [jnp.stack(small), b_in.reshape(2, 384), jnp.zeros((6, 384), jnp.float32)], axis=0
-    )
+    deal_row = deal[0]
+    lengths = seq_lengths[0]
     (
+        attn_in,
         query_groups,
-        pair_groups,
+        pairs,
+        pairs_turned,
+        out_heads,
+        log_totals,
         query_weight,
-        pair_weights,
+        key_weight,
+        value_weight,
         mix_weight,
         inner_weight,
         outer_weight,
         vectors,
-    ) = gather_project(
+        inner_bias,
+    ) = forward(
+        deal_row,
+        lengths,
         inputs,
-        to_half(w_query),
-        pair_weight,
-        to_half(w_attn_out),
-        to_half(w_in),
-        to_half(w_out),
-        to_half(packed),
-    )
-    vectors = vectors.astype(jnp.float32)
+        [w_key, w_value, w_query, w_in, w_attn_out, w_out],
+        [
+            item.reshape(1, -1)
+            for item in (
+                b_query,
+                b_value,
+                b_attn_out,
+                norm1_gain,
+                norm1_bias,
+                b_out,
+                norm2_gain,
+                norm2_bias,
+                b_in,
+            )
+        ],
+    )
     mix_bias, gain_one, shift_one, outer_bias, gain_two, shift_two = (
-        vectors[:, 2 + i, :part].reshape(width) for i in range(6)
-    )
-    inner_bias = vectors[:, 8:10, :].reshape(4 * width)
-    deal_row = deal[0]
-    lengths = seq_lengths[0]
-    out_windows, out_heads, log_totals, pairs, pairs_turned = attention_forward(
-        deal_row, lengths, query_groups, pair_groups
-    )
-    attn_in = heads_home(out_windows)
+        vectors[2 + i] for i in range(6)
+    )
+    inner_bias = inner_bias[0]
     residual_one = (
         inputs.astype(jnp.float32)
         + jnp.dot(attn_in, mix_weight, preferred_element_type=jnp.float32)
@@ -1577,7 +1653,8 @@
         pairs_turned,
         inputs,
         query_weight,
-        pair_weights,
+        key_weight,
+        value_weight,
         grad_one,
         to_half(grad_outer),
         to_half(grad_inner),

time: 313 us -> 281 us (0.90)
  other arithmetic: 23 us -> 11.1 us
  local copies, waits for them, and re-layouts: 17.1 us -> 7.94 us
  matrix products: 35.3 us -> 28.2 us
  Pallas kernels: 236 us -> 231 us
    unnamed x65 -> x37, local copies, waits for them, and re-layouts: 8.03 us -> 0.96 us
    another operation x10 -> x0, other arithmetic: 6.44 us -> none
    dot_general x1, matrix products: 6.91 us -> 2.78 us  [body_fast(): jnp.einsum('td,fd->tf', grad_branch, outer_weight, preferred_element_type...]
    pallas_call x1, Pallas kernels: 144 us -> 141 us  [backward(): pl.pallas_call(functools.partial(backward_kernel, chunks), out_shape=[ful...]
    pallas_call x3 -> x1, Pallas kernels: 91.8 us -> 90.6 us  [forward(): pl.pallas_call(forward_kernel, out_shape=[half(rows, width), half(4, rows...]
where the time goes in v4:
time: 281 us; the launch traced here: 279 us
  Pallas kernels  231 us (82%)
  matrix products  28.2 us (10%)
  other arithmetic  11.1 us (4%)
  local copies, waits for them, and re-layouts  7.94 us (3%)
    pallas_call x1, Pallas kernels, backward(): pl.pallas_call(functools.partial(backward_kernel, chunks), out_shape=[ful...  141 us
    pallas_call x1, Pallas kernels, forward(): pl.pallas_call(forward_kernel, out_shape=[half(rows, width), half(4, rows...  90.6 us
    dot_general x1, matrix products, body_fast(): jnp.dot(normal_half, inner_weight, preferred_element_type=jnp.float32)  9.93 us

profile of v4, /device:TPU:0, one launch (start us, length us, event | category | flops | bytes accessed | tf_op | source)
XLA Modules:
  0.0 279.2 jit_solution(3499927410835170464)
XLA Ops:
  0.7 1.3 reshape.134.refs_17_
  1.9 90.6 %forward.1 = (bf16[256,768]{1,0:T(8,128)(2,1)}, bf16[4,256,256]{2,1,0:T(8,128)(2,1)}, bf16[3,2,1024,128]{3,2,1,0:T(8,128)(2,1)}, bf16[3,2,128,1024]{3,2,1,0:T(8,...) custom-call(s32[16]{0:T(128)} %bitcast.78, ...), custom_call_target="tpu_custom_call" | custom-call | flops 10000000000 | bytes 100000000 | tf_op jit(solution)/shard_map/forward/pallas_call | solution.py:1499
  92.5 0.0 copy-start.13
  92.5 1.0 slice_reduce_fusion.1
  93.5 0.0 copy-done.6
  93.6 0.0 slice-start.2
  93.6 2.1 fusion.31
  95.7 0.2 multiply_reduce_fusion.3
  95.9 0.0 copy-done.13
  95.9 0.0 slice-start.3
  95.9 9.9 %multiply_convert_fusion = (bf16[256,3072]{1,0:T(8,128)(2,1)S(1)}, f32[256,3072]{1,0:T(8,128)S(1)}, f32[256,3072]{1,0:T(8,128)S(1)}) fusion(f32[3072]{0:T(1024)S(1)} %bitcast.83, bf16[768,3072]{1,0:T(8,128)(2,1)} %get-tuple-element.42, f32[256,768]{1,0:T(8,128)S(1)} %get-tuple-element.90, f32[768]{0:T(1024)S(1)} %get-tuple-element.71, ...), kind=kOutput, calls=%fused_computation.7 | convolution fusion | flops 1260847104 | bytes 13389824 | tf_op jit(solution)/shard_map/dot_general | solution.py:1601
  105.9 0.0 copy-start.2
  105.9 1.6 fusion.32
  107.5 0.2 multiply_reduce_fusion.2
  107.7 0.4 fusion.16
  108.2 0.0 slice-start
  108.2 1.1 convert_reduce_fusion.2
  109.3 2.8 convert_reduce_fusion
  112.1 1.7 multiply_reduce_fusion
  113.8 0.3 convert_reduce_fusion.3
  114.1 0.0 copy-start
  114.2 1.5 convolution_convert_fusion.2.refs_16_
  115.7 3.8 %convolution_convert_fusion.refs_15_ = bf16[768,3072]{1,0:T(8,128)(2,1)} fusion(bf16[256,3072]{1,0:T(8,128)(2,1)S(1)} %get-tuple-element.96, f32[256,768]{1,0:T(8,128)S(1)} %get-tuple-element.90, f32[768]{0:T(1024)S(1)} %get-tuple-element.71, f32[768]{0:T(1024)S(1)} %get-tuple-element.72, f32[256]{0:T(256)S(1)} %add_rsqrt_fusion.1, ...), kind=kOutput, calls=%fused_computation | convolution fusion | flops 1211301888 | bytes 7086080 | tf_op jit(solution)/shard_map/td,tf->df/dot_general | solution.py:1622
  119.5 3.6 %convolution_convert_fusion.1.refs_14_ = bf16[3072,768]{1,0:T(8,128)(2,1)} fusion(bf16[256,3072]{1,0:T(8,128)(2,1)S(1)} %get-tuple-element.78, f32[256,768]{1,0:T(8,128)S(1)} %get-tuple-element.75), kind=kOutput, calls=%fused_computation.1 | convolution fusion | flops 1210515456 | bytes 7077888 | tf_op jit(solution)/shard_map/tf,td->fd/dot_general | solution.py:1616
  123.0 1.3 convolution_convert_fusion.3.refs_3_
  124.3 0.6 reshape.135.refs_17_
  124.9 0.6 reshape.136.refs_18_
  125.5 0.6 reshape.137.refs_19_
  126.0 0.6 reshape.138.refs_20_
  126.6 0.6 reshape.139.refs_21_
  127.2 0.1 convert_reduce_fusion.1
  127.3 0.6 reshape.140.refs_22_
  127.9 0.0 copy-done.12
  127.9 0.5 and_select_fusion.refs_2_
  128.4 140.5 %backward.1 = (f32[256,768]{1,0:T(8,128)}, bf16[768,768]{1,0:T(8,128)(2,1)}, bf16[192,3072]{1,0:T(8,128)(2,1)}, bf16[192,768]{1,0:T(8,128)(2,1)}, bf16[192,768]{...) custom-call(s32[16]{0:T(128)} %bitcast.79, s32[2]{0:T(128)} %bitcast.81, ...), custom_call_target="tpu_custom_call" | custom-call | flops 10000000000 | bytes 100000000 | tf_op jit(solution)/shard_map/backward/pallas_call | solution.py:1069
  269.0 3.1 %convert_element_type.90 = f32[192,3072]{1,0:T(8,128)} convert(bf16[192,3072]{1,0:T(8,128)(2,1)} %get-tuple-element.59) | non-fusion elementwise | flops 589824 | bytes 3538944 | tf_op jit(solution)/shard_map/convert_element_type | solution.py:1690
  272.0 0.0 copy-start.5
  272.0 1.6 convert_element_type.91
  273.6 0.9 convert_element_type.85
  274.5 0.9 convert_element_type.86
  275.3 0.9 convert_element_type.87
  276.2 0.9 convert_element_type.88
  277.0 0.0 copy-done.11
  277.1 0.1 slice_select_fusion
  277.1 0.6 fusion.30
  277.8 0.6 reshape.142
  278.4 0.0 copy-done.5
  278.4 0.9 copy.37
  (35 shorter events, 0.1 us)
Async XLA Ops:
  1.9 91.6 %copy-start.6 = (bf16[1,256,768]{2,1,0:T(8,128)(2,1)S(1)}, bf16[1,256,768]{2,1,0:T(8,128)(2,1)}, u32[]{:S(2)}) copy-start(bf16[1,256,768]{2,1,0:T(8,128)(2,1)} %param.19) | copy-start | bytes 1179652
  92.5 3.4 %copy-start.13 = (f32[1,3072]{1,0:T(1,128)S(1)}, f32[1,3072]{1,0:T(1,128)}, u32[]{:S(2)}) copy-start(f32[1,3072]{1,0:T(1,128)} %get-tuple-element.43) | copy-start | bytes 36868
  93.6 12.3 %slice-start.2 = ((s8[4718592]{0:T(1024)(128)(4,1)}), s8[4194304]{0:T(1024)(128)(4,1)S(1)}, s32[]{:S(2)}) async-start(s8[4718592]{0:T(1024)(128)(4,1)} %bitcast.86), calls=%async_computation.2 | async-start | bytes 8388608
  95.9 10.0 %slice-start.3 = ((s8[4718592]{0:T(1024)(128)(4,1)}), s8[524288]{0:T(1024)(128)(4,1)S(1)}, s32[]{:S(2)}) async-start(s8[4718592]{0:T(1024)(128)(4,1)} %bitcast.86), calls=%async_computation.3 | async-start | bytes 1048576
  105.9 1.8 copy-start.2
  108.2 3.9 %slice-start = ((s8[4718592]{0:T(1024)(128)(4,1)}), s8[4194304]{0:T(1024)(128)(4,1)S(1)}, s32[]{:S(2)}) async-start(s8[4718592]{0:T(1024)(128)(4,1)} %bitcast.84), calls=%async_computation | async-start | bytes 8388608
  109.3 2.8 slice-start.1
  112.1 2.1 copy-start.3
  114.1 8.9 %copy-start = (f32[256,768]{1,0:T(8,128)}, f32[256,768]{1,0:T(8,128)S(1)}, u32[]{:S(2)}) copy-start(f32[256,768]{1,0:T(8,128)S(1)} %get-tuple-element.77.refs_13_) | copy-start | bytes 2359300
  119.5 3.6 %copy-start.1 = (bf16[768,768]{1,0:T(8,128)(2,1)S(1)}, bf16[768,768]{1,0:T(8,128)(2,1)}, u32[]{:S(2)}) copy-start(bf16[768,768]{1,0:T(8,128)(2,1)} %get-tuple-element.40) | copy-start | bytes 3538948
  119.5 8.4 %copy-start.12 = (s32[1,16]{1,0:T(1,128)S(1)}, s32[1,16]{1,0:T(1,128)}, u32[]{:S(2)}) copy-start(s32[1,16]{1,0:T(1,128)} %param.21) | copy-start | bytes 196
  268.9 3.1 %copy-start.4 = (bf16[768,768]{1,0:T(8,128)(2,1)S(1)}, bf16[768,768]{1,0:T(8,128)(2,1)}, u32[]{:S(2)}) copy-start(bf16[768,768]{1,0:T(8,128)(2,1)} %get-tuple-element.60) | copy-start | bytes 3538948
  268.9 4.7 %copy-start.10 = (bf16[192,768]{1,0:T(8,128)(2,1)S(1)}, bf16[192,768]{1,0:T(8,128)(2,1)}, u32[]{:S(2)}) copy-start(bf16[192,768]{1,0:T(8,128)(2,1)} %get-tuple-element.54) | copy-start | bytes 884740
  268.9 5.5 %copy-start.9 = (bf16[192,768]{1,0:T(8,128)(2,1)S(1)}, bf16[192,768]{1,0:T(8,128)(2,1)}, u32[]{:S(2)}) copy-start(bf16[192,768]{1,0:T(8,128)(2,1)} %get-tuple-element.55) | copy-start | bytes 884740
  272.0 3.3 %copy-start.8 = (bf16[192,768]{1,0:T(8,128)(2,1)S(1)}, bf16[192,768]{1,0:T(8,128)(2,1)}, u32[]{:S(2)}) copy-start(bf16[192,768]{1,0:T(8,128)(2,1)} %get-tuple-element.56) | copy-start | bytes 884740
  272.0 4.2 %copy-start.7 = (bf16[192,768]{1,0:T(8,128)(2,1)S(1)}, bf16[192,768]{1,0:T(8,128)(2,1)}, u32[]{:S(2)}) copy-start(bf16[192,768]{1,0:T(8,128)(2,1)} %get-tuple-element.57) | copy-start | bytes 884740
  272.0 5.0 %copy-start.11 = (bf16[64,256]{1,0:T(8,128)(2,1)S(1)}, bf16[64,256]{1,0:T(8,128)(2,1)}, u32[]{:S(2)}) copy-start(bf16[64,256]{1,0:T(8,128)(2,1)} %get-tuple-element.58) | copy-start | bytes 98308
  272.0 6.3 %copy-start.5 = (f32[256,768]{1,0:T(8,128)S(1)}, f32[256,768]{1,0:T(8,128)}, u32[]{:S(2)}) copy-start(f32[256,768]{1,0:T(8,128)} %get-tuple-element.53) | copy-start | bytes 2359300
